TPU v7x, 32 devices: a whole 2x2x4 slice. The times are simulated.
32 devices in a mesh: dp: 8 (over y, x, core), seq: 4 (over z).
Axes of the slice: x: 2, y: 2, z: 4, core: 2. Of those that a mesh axis runs over, the one named last changes fastest.
Arguments:
- tokens: bfloat16 [16, 1024, 768], P('dp', 'seq'), may hold values from -6 to 6
- encoded: bfloat16 [16, 256, 768], P('dp', 'seq'), may hold values from -6 to 6
- cotangent: bfloat16 [16, 1024, 768], P('dp', 'seq'), may hold values from -6 to 6
- attn_in: bfloat16 [768, 2304], P('dp'), may hold values from -0.21875 to 0.21875
- attn_out: bfloat16 [768, 768], P('dp'), may hold values from -3.5 to 3.5
- cross_in: bfloat16 [768, 2304], P('dp'), may hold values from -0.21875 to 0.21875
- cross_out: bfloat16 [768, 768], P('dp'), may hold values from -3.5 to 3.5
- ffn_in: bfloat16 [768, 3072], P('dp'), may hold values from -0.21875 to 0.21875
- ffn_out: bfloat16 [3072, 768], P('dp'), may hold values from -0.109375 to 0.109375
- gains: bfloat16 [3, 768], P(None, 'dp'), may hold values from 0.5 to 1.5
- biases: bfloat16 [10, 768], P(None, 'dp'), may hold values from -1.5 to 1.5
- bias_ff: bfloat16 [3072], P('dp'), may hold values from -1.5 to 1.5
- block_ids: int32 [16, 1024], P('dp'), may hold values from 0 to 7, never falling along the last dimension, each value on 1 to 256 neighbouring positions
- enc_lengths: int32 [16], P('dp'), may hold values from 1 to 256, 3072 in all
Outputs:
- output: bfloat16 [16, 1024, 768], P('dp', 'seq')
- input_token_gradient: float32 [16, 1024, 768], P('dp', 'seq')
- encoded_grad: float32 [16, 256, 768], P('dp', 'seq')
- attn_in_grad: float32 [768, 2304], P('dp')
- attn_out_grad: float32 [768, 768], P('dp')
- cross_in_grad: float32 [768, 2304], P('dp')
- cross_out_grad: float32 [768, 768], P('dp')
- ffn_in_grad: float32 [768, 3072], P('dp')
- ffn_out_grad: float32 [3072, 768], P('dp')
- gains_grad: float32 [3, 768], P(None, 'dp')
- biases_grad: float32 [10, 768], P(None, 'dp')
- bias_ff_grad: float32 [3072], P('dp')
Inputs may be any that keep to these rules, and one draw needn't show every extreme that they name: `block_ids`: along each sequence the ids never fall, every id from 0 to 7 occurs, and each id covers 1 to 256 tokens. `enc_lengths`: the lengths sum to 3072 and the largest is 256.
All inputs are finite; a program needn't handle non-finite values. No bound on the sum of `enc_lengths` on one device may be relied on, other than what follows from the above.
Results may differ from a plain program's by a relative error of at most 0.025.
Values may be sent and summed in bfloat16 or wider, within the bound.
No kernel may reach another device: no remote copies, remote signals or barrier semaphores. Data moves between devices by JAX's collectives and lax.ppermute only.
A program may use at most 256 MiB of HBM per device.

v0:
```python
import jax
import jax.numpy as jnp
from jax import lax
from jax.sharding import PartitionSpec as P

HD = 64
MICRO = 2


EPSILON = 1e-05
MASKED = -1e30


def as_sent(array):

    def short(part):
        return part.astype(jnp.bfloat16) if part.dtype == jnp.float32 else part

    return jax.tree.map(short, array)


def product(left, right):
    return jnp.dot(left, right, preferred_element_type=jnp.float32)


def left_transposed(left, right):
    return lax.dot_general(
        left, right, (((0,), (0,)), ((), ())), preferred_element_type=jnp.float32
    )


def right_transposed(left, right):
    return lax.dot_general(
        left, right, (((1,), (1,)), ((), ())), preferred_element_type=jnp.float32
    )


def column_total(values):
    return jnp.sum(values.astype(jnp.float32), axis=0)


def layer_norm(summed, gain, offset):
    centre = summed - jnp.mean(summed, axis=-1, keepdims=True)
    spread = jnp.mean(centre * centre, axis=-1, keepdims=True)
    return centre * lax.rsqrt(spread + EPSILON) * gain + offset


def norm_backward(summed, gain, offset, upstream):
    _, pull_back = jax.vjp(layer_norm, summed, gain, offset)
    return pull_back(upstream)


def gelu_exact(values):
    return jax.nn.gelu(values, approximate=False)


def attend_forward(queries, keys_all, values_all, allowed):
    factor = float(HD) ** (-0.5)
    context_parts = []
    total_parts = []
    for head_index in range(queries.shape[2]):
        raw_scores = jnp.einsum(
            "jlt,jst->jls",
            queries[:, :, head_index],
            keys_all[:, :, head_index],
            preferred_element_type=jnp.float32,
        )
        scores = jnp.where(allowed, raw_scores * factor, MASKED)
        highest = jnp.max(scores, axis=-1, keepdims=True)
        exponent = jnp.exp(scores - highest)
        denominator = jnp.sum(exponent, axis=-1, keepdims=True)
        weights_low = (exponent / denominator).astype(jnp.bfloat16)
        context_parts.append(
            jnp.einsum(
                "ljo,low->ljw",
                weights_low,
                values_all[:, :, head_index],
                preferred_element_type=jnp.float32,
            )
        )
        total_parts.append(highest + jnp.log(denominator))
    return (jnp.stack(context_parts, axis=2), jnp.stack(total_parts, axis=2))


def attend_backward(queries, keys_all, values_all, allowed, log_totals, upstream):
    factor = float(HD) ** (-0.5)
    query_grads = []
    key_grads = []
    value_grads = []
    for head_index in range(queries.shape[2]):
        single_query_head = queries[:, :, head_index]
        single_key_head = keys_all[:, :, head_index]
        upstream_head = upstream[:, :, head_index]
        raw_scores = jnp.einsum(
            "jlt,jst->jls", single_query_head, single_key_head, preferred_element_type=jnp.float32
        )
        scores = jnp.where(allowed, raw_scores * factor, MASKED)
        softmax_weights = jnp.exp(scores - log_totals[:, :, head_index])
        weight_grads = jnp.einsum(
            "jlt,jst->jls",
            upstream_head,
            values_all[:, :, head_index],
            preferred_element_type=jnp.float32,
        )
        value_grads.append(
            jnp.einsum(
                "xgn,xgp->xnp",
                softmax_weights.astype(jnp.bfloat16),
                upstream_head,
                preferred_element_type=jnp.float32,
            )
        )
        row_inner = jnp.sum(softmax_weights * weight_grads, axis=-1, keepdims=True)
        score_gradients = (softmax_weights * (weight_grads - row_inner) * factor).astype(
            jnp.bfloat16
        )
        query_grads.append(
            jnp.einsum(
                "ljo,low->ljw", score_gradients, single_key_head, preferred_element_type=jnp.float32
            )
        )
        key_grads.append(
            jnp.einsum(
                "xgn,xgp->xnp",
                score_gradients,
                single_query_head,
                preferred_element_type=jnp.float32,
            )
        )
    return (
        jnp.stack(query_grads, axis=2),
        jnp.stack(key_grads, axis=2),
        jnp.stack(value_grads, axis=2),
    )


def gather_weights(shards):
    return (
        lax.all_gather(shards[0], "dp", axis=0, tiled=True),
        lax.all_gather(shards[1], "dp", axis=0, tiled=True),
        lax.all_gather(shards[2], "dp", axis=0, tiled=True),
        lax.all_gather(shards[3], "dp", axis=0, tiled=True),
        lax.all_gather(shards[4], "dp", axis=0, tiled=True),
        lax.all_gather(shards[5], "dp", axis=0, tiled=True),
        lax.all_gather(shards[6], "dp", axis=1, tiled=True),
        lax.all_gather(shards[7], "dp", axis=1, tiled=True),
        lax.all_gather(shards[8], "dp", axis=0, tiled=True),
    )


def reduce_grads(gradients):
    shares = (
        lax.psum_scatter(gradients[0], "dp", scatter_dimension=0, tiled=True),
        lax.psum_scatter(gradients[1], "dp", scatter_dimension=0, tiled=True),
        lax.psum_scatter(gradients[2], "dp", scatter_dimension=0, tiled=True),
        lax.psum_scatter(gradients[3], "dp", scatter_dimension=0, tiled=True),
        lax.psum_scatter(gradients[4], "dp", scatter_dimension=0, tiled=True),
        lax.psum_scatter(gradients[5], "dp", scatter_dimension=0, tiled=True),
        lax.psum_scatter(gradients[6], "dp", scatter_dimension=1, tiled=True),
        lax.psum_scatter(gradients[7], "dp", scatter_dimension=1, tiled=True),
        lax.psum_scatter(gradients[8], "dp", scatter_dimension=0, tiled=True),
    )
    return jax.tree.map(lambda part: part.astype(jnp.float32), lax.psum(as_sent(shares), "seq"))


def micro_step(weights_full, tokens, encoded, cotangent, block_row, enc_valid):
    attn_in, attn_out, cross_in, cross_out, ffn_in, ffn_out, gains, biases, bias_ff = weights_full
    groups = lax.axis_size("seq")
    batch_size, local_len, model_width = tokens.shape
    enc_local = encoded.shape[1]
    token_rows = batch_size * local_len
    enc_rows = batch_size * enc_local
    part_width = model_width // groups
    head_count = part_width // HD
    length = local_len * groups
    enc_length = enc_local * groups
    gain_all = gains.astype(jnp.float32)
    bias_all = biases.astype(jnp.float32)
    bias_hidden = bias_ff.astype(jnp.float32)
    blank = jnp.zeros((model_width,), jnp.float32)
    cross_q_weight = cross_in[:, :model_width]
    cross_kv_weight = cross_in[:, model_width:]
    token_flat = tokens.reshape(token_rows, model_width)
    self_bias = jnp.concatenate([bias_all[0], blank, bias_all[1]])
    packed = (
        (product(token_flat, attn_in) + self_bias)
        .astype(jnp.bfloat16)
        .reshape(batch_size, local_len, 3, groups, part_width)
    )
    enc_flat = encoded.reshape(enc_rows, model_width)
    enc_bias = jnp.concatenate([blank, bias_all[4]])
    enc_packed = (
        (product(enc_flat, cross_kv_weight) + enc_bias)
        .astype(jnp.bfloat16)
        .reshape(batch_size, enc_local, 2, groups, part_width)
    )
    head_packed, enc_heads = (
        lax.all_to_all(packed, "seq", split_axis=3, concat_axis=1, tiled=True),
        lax.all_to_all(enc_packed, "seq", split_axis=3, concat_axis=1, tiled=True),
    )
    queries = head_packed[:, :, 0, 0].reshape(batch_size, length, head_count, HD)
    keys_all = head_packed[:, :, 1, 0].reshape(batch_size, length, head_count, HD)
    values_all = head_packed[:, :, 2, 0].reshape(batch_size, length, head_count, HD)
    cross_keys = enc_heads[:, :, 0, 0].reshape(batch_size, enc_length, head_count, HD)
    cross_values = enc_heads[:, :, 1, 0].reshape(batch_size, enc_length, head_count, HD)
    self_allowed = block_row[:, None, :] <= block_row[:, :, None]
    context, self_totals = attend_forward(queries, keys_all, values_all, self_allowed)
    context_send = context.astype(jnp.bfloat16).reshape(batch_size, length, 1, part_width)
    context_flat = lax.all_to_all(
        context_send, "seq", split_axis=1, concat_axis=2, tiled=True
    ).reshape(token_rows, model_width)
    first_sum = token_flat.astype(jnp.float32) + product(context_flat, attn_out) + bias_all[2]
    first = layer_norm(first_sum, gain_all[0], bias_all[7])
    first_low = first.astype(jnp.bfloat16)
    cross_send = (
        (product(first_low, cross_q_weight) + bias_all[3])
        .astype(jnp.bfloat16)
        .reshape(batch_size, local_len, groups, part_width)
    )
    cross_queries = lax.all_to_all(
        cross_send, "seq", split_axis=2, concat_axis=1, tiled=True
    ).reshape(batch_size, length, head_count, HD)
    cross_allowed = (
        jnp.arange(enc_length, dtype=jnp.int32)[None, None, :] < enc_valid[:, None, None]
    )
    cross_context, cross_totals = attend_forward(
        cross_queries, cross_keys, cross_values, cross_allowed
    )
    cross_ctx_send = cross_context.astype(jnp.bfloat16).reshape(batch_size, length, 1, part_width)
    cross_flat = lax.all_to_all(
        cross_ctx_send, "seq", split_axis=1, concat_axis=2, tiled=True
    ).reshape(token_rows, model_width)
    second_sum = first + product(cross_flat, cross_out) + bias_all[5]
    second = layer_norm(second_sum, gain_all[1], bias_all[8])
    second_low = second.astype(jnp.bfloat16)
    activation = product(second_low, ffn_in) + bias_hidden
    hidden, gelu_pull = jax.vjp(gelu_exact, activation)
    hidden_low = hidden.astype(jnp.bfloat16)
    third_sum = second + product(hidden_low, ffn_out) + bias_all[6]
    final = layer_norm(third_sum, gain_all[2], bias_all[9])
    upstream = cotangent.reshape(token_rows, model_width).astype(jnp.float32)
    d_third_sum, d_gain_three, d_offset_three = norm_backward(
        third_sum, gain_all[2], bias_all[9], upstream
    )
    d_ffn = d_third_sum.astype(jnp.bfloat16)
    grad_ffn_out = left_transposed(hidden_low, d_ffn)
    d_hidden = right_transposed(d_ffn, ffn_out)
    d_activation = gelu_pull(d_hidden)[0].astype(jnp.bfloat16)
    grad_ffn_in = left_transposed(second_low, d_activation)
    d_second = d_third_sum + right_transposed(d_activation, ffn_in)
    d_second_sum, d_gain_two, d_offset_two = norm_backward(
        second_sum, gain_all[1], bias_all[8], d_second
    )
    d_cross = d_second_sum.astype(jnp.bfloat16)
    cross_output_gradient = left_transposed(cross_flat, d_cross)
    d_cross_ctx = (
        right_transposed(d_cross, cross_out)
        .astype(jnp.bfloat16)
        .reshape(batch_size, local_len, groups, part_width)
    )
    d_cross_heads = lax.all_to_all(
        d_cross_ctx, "seq", split_axis=2, concat_axis=1, tiled=True
    ).reshape(batch_size, length, head_count, HD)
    d_cross_q, d_cross_k, d_cross_v = attend_backward(
        cross_queries, cross_keys, cross_values, cross_allowed, cross_totals, d_cross_heads
    )
    d_cross_q_send = d_cross_q.astype(jnp.bfloat16).reshape(batch_size, length, 1, part_width)
    d_cross_q_flat = lax.all_to_all(
        d_cross_q_send, "seq", split_axis=1, concat_axis=2, tiled=True
    ).reshape(token_rows, model_width)
    d_enc_heads = (
        jnp.stack([d_cross_k, d_cross_v], axis=2)
        .astype(jnp.bfloat16)
        .reshape(batch_size, enc_length, 2, 1, part_width)
    )
    grad_cross_q = left_transposed(first_low, d_cross_q_flat)
    d_first = d_second_sum + right_transposed(d_cross_q_flat, cross_q_weight)
    d_first_sum, d_gain_one, d_offset_one = norm_backward(
        first_sum, gain_all[0], bias_all[7], d_first
    )
    d_attn = d_first_sum.astype(jnp.bfloat16)
    grad_attn_out = left_transposed(context_flat, d_attn)
    d_context = (
        right_transposed(d_attn, attn_out)
        .astype(jnp.bfloat16)
        .reshape(batch_size, local_len, groups, part_width)
    )
    d_context_heads = lax.all_to_all(
        d_context, "seq", split_axis=2, concat_axis=1, tiled=True
    ).reshape(batch_size, length, head_count, HD)
    d_query, d_key, value_gradient = attend_backward(
        queries, keys_all, values_all, self_allowed, self_totals, d_context_heads
    )
    d_packed = (
        jnp.stack([d_query, d_key, value_gradient], axis=2)
        .astype(jnp.bfloat16)
        .reshape(batch_size, length, 3, 1, part_width)
    )
    d_token_heads, d_enc_back = (
        lax.all_to_all(d_packed, "seq", split_axis=1, concat_axis=3, tiled=True),
        lax.all_to_all(d_enc_heads, "seq", split_axis=1, concat_axis=3, tiled=True),
    )
    d_inputs = d_token_heads.reshape(token_rows, 3 * model_width)
    d_enc_inputs = d_enc_back.reshape(enc_rows, 2 * model_width)
    grad_attn_in = left_transposed(token_flat, d_inputs)
    d_tokens = d_first_sum + right_transposed(d_inputs, attn_in)
    grad_cross_kv = left_transposed(enc_flat, d_enc_inputs)
    d_encoded = right_transposed(d_enc_inputs, cross_kv_weight)
    grad_cross_in = jnp.concatenate([grad_cross_q, grad_cross_kv], axis=1)
    grad_gains = jnp.stack([d_gain_one, d_gain_two, d_gain_three])
    grad_biases = jnp.stack(
        [
            column_total(d_inputs[:, :model_width]),
            column_total(d_inputs[:, 2 * model_width :]),
            column_total(d_attn),
            column_total(d_cross_q_flat),
            column_total(d_enc_inputs[:, model_width:]),
            column_total(d_cross),
            column_total(d_ffn),
            d_offset_one,
            d_offset_two,
            d_offset_three,
        ]
    )
    grad_bias_ff = column_total(d_activation)
    gradients = (
        grad_attn_in,
        grad_attn_out,
        grad_cross_in,
        cross_output_gradient,
        grad_ffn_in,
        grad_ffn_out,
        grad_gains,
        grad_biases,
        grad_bias_ff,
    )
    result = final.astype(jnp.bfloat16).reshape(batch_size, local_len, model_width)
    return (
        result,
        d_tokens.reshape(batch_size, local_len, model_width),
        d_encoded.reshape(batch_size, enc_local, model_width),
        gradients,
    )


def local(
    tokens,
    encoded,
    cotangent,
    attn_in,
    attn_out,
    cross_in,
    cross_out,
    ffn_in,
    ffn_out,
    gains,
    biases,
    bias_ff,
    block_ids,
    enc_lengths,
):
    shards = (attn_in, attn_out, cross_in, cross_out, ffn_in, ffn_out, gains, biases, bias_ff)
    microbatch_length = tokens.shape[0] // MICRO
    result_parts = []
    token_pieces = []
    encoded_parts = []
    shares = None
    totals = None
    for micro_index in range(MICRO):
        start_row = micro_index * microbatch_length
        stop_row = start_row + microbatch_length
        weights_full = gather_weights(shards)
        result, d_tokens, d_encoded, gradients = micro_step(
            weights_full,
            tokens[start_row:stop_row],
            encoded[start_row:stop_row],
            cotangent[start_row:stop_row],
            block_ids[start_row:stop_row],
            enc_lengths[start_row:stop_row],
        )
        result_parts.append(result)
        token_pieces.append(d_tokens)
        encoded_parts.append(d_encoded)
        totals = (
            gradients
            if totals is None
            else tuple((earlier + later for earlier, later in zip(totals, gradients)))
        )
    shares = reduce_grads(totals)
    return (
        jnp.concatenate(result_parts, axis=0),
        jnp.concatenate(token_pieces, axis=0),
        jnp.concatenate(encoded_parts, axis=0),
    ) + tuple(shares)


def solution(mesh):
    in_specs = (
        P("dp", "seq", None),
        P("dp", "seq", None),
        P("dp", "seq", None),
        P("dp", None),
        P("dp", None),
        P("dp", None),
        P("dp", None),
        P("dp", None),
        P("dp", None),
        P(None, "dp"),
        P(None, "dp"),
        P("dp"),
        P("dp", None),
        P("dp"),
    )
    out_specs = (
        P("dp", "seq", None),
        P("dp", "seq", None),
        P("dp", "seq", None),
        P("dp", None),
        P("dp", None),
        P("dp", None),
        P("dp", None),
        P("dp", None),
        P("dp", None),
        P(None, "dp"),
        P(None, "dp"),
        P("dp"),
    )
    return jax.shard_map(local, mesh=mesh, in_specs=in_specs, out_specs=out_specs, check_vma=False)
```

profile of v0, /device:TPU:0, one launch (start us, length us, event | category | flops | bytes accessed | tf_op | source)
XLA Modules:
  0.0 1132.9 jit_solution(11100311602562081562)
XLA Ops:
  10.6 10.6 all-gather.1
  21.2 9.1 all-gather
  31.1 15.4 %all-gather.14.cloned.1.call-done = bf16[768,2304]{1,0:T(8,128)(2,1)} async-done(((bf16[96,2304]{1,0:T(8,128)(2,1)}), bf16[768,2304]{1,0:T(8,128)(2,1)}) %all-gather.14.cloned.1.call-update) | async-done | bytes 3538960 | tf_op jit(solution)/shard_map/all_gather | solution.py:141
  57.8 5.9 all-to-all-done.8
  67.2 15.1 %all-gather.10.cloned.1.call-done = bf16[768,2304]{1,0:T(8,128)(2,1)} async-done(((bf16[96,2304]{1,0:T(8,128)(2,1)}), bf16[768,2304]{1,0:T(8,128)(2,1)}) %all-gather.10.cloned.1.call-update) | async-done | bytes 3538960 | tf_op jit(solution)/shard_map/all_gather | solution.py:139
  99.6 21.1 %all-to-all-done = bf16[1,256,3,4,192]{1,4,2,0,3:T(8,128)(2,1)S(1)} async-done(((bf16[1,256,3,4,192]{1,4,2,0,3:T(8,128)(2,1)}), bf16[1,256,3,4,192]{1,4,2,0,3:T(8,128)(2,1)S(1)}, u32[]{:S(2)}, u32[]{:S(2)}) %all-to-all-start) | async-done | bytes 1179680 | tf_op jit(solution)/shard_map/all_to_all | solution.py:198
  125.4 9.5 all-gather.2
  145.6 6.7 all-to-all-done.5
  241.7 5.5 all-to-all-start.4
  254.0 5.6 reduce.107
  265.9 5.3 all-to-all-start.9
  296.1 11.8 %multiply_convert_fusion.6 = (bf16[256,3072]{1,0:T(8,128)(2,1)}, f32[256,3072]{1,0:T(8,128)}, f32[256,3072]{1,0:T(8,128)}) fusion(f32[3072]{0:T(1024)S(1)} %bitcast.863, bf16[768,3072]{1,0:T(8,128)(2,1)} %all-gather.18.cloned.1.call-done, f32[256,768]{1,0:T(8,128)} %copy-done.27, f32[256]{0:T(256)S(1)} %fusion.243, f32[256]{0:T(256)S(1)} %broadcast_multiply_fusion.1, ...), kind=kOutput, calls=%fused_computation.68 | convolution fusion | flops 1260847104 | bytes 13389824 | tf_op jit(solution)/shard_map/dot_general | solution.py:23
  312.8 9.8 multiply_convert_fusion.7
  393.5 5.6 reduce.109
  401.5 5.2 all-to-all-start.11
  425.3 5.7 reduce.108
  510.9 7.6 maximum_add_fusion
  518.5 8.0 copy.330
  526.6 5.3 all-to-all-start.16
  594.4 6.0 pad_maximum_fusion
  600.4 5.2 all-to-all-start.13
  632.3 11.3 all-to-all-done.13
  653.1 36.3 %all-to-all-done.17 = bf16[1,1024,3,1,192]{4,2,3,0,1:T(4,128)(2,1)S(1)} async-done(((bf16[1,1024,3,1,192]{4,2,3,0,1:T(4,128)(2,1)}), bf16[1,1024,3,1,192]{4,2,3,0,1:T(4,128)(2,1)S(1)}, u32[]{:S(2)}, u32[]{:S(2)}) %all-to-all-start.17) | async-done | bytes 1179680 | tf_op jit(solution)/shard_map/all_to_all | solution.py:300
  700.0 8.0 copy.328
  712.0 6.5 convolution_add_fusion.1
  749.9 22.0 %reduce-scatter.25.cloned.1.call-done = f32[96,2304]{1,0:T(8,128)} async-done(((f32[768,2304]{1,0:T(8,128)}), f32[96,2304]{1,0:T(8,128)}) %reduce-scatter.25.cloned.1.call-update) | async-done | bytes 884752
  774.1 78.1 %reduce-scatter.21.cloned.1.call-done = f32[96,3072]{1,0:T(8,128)} async-done(((f32[768,3072]{1,0:T(8,128)}), f32[96,3072]{1,0:T(8,128)}) %reduce-scatter.21.cloned.1.call-update) | async-done | bytes 1179664 | tf_op jit(solution)/shard_map/reduce_scatter | solution.py:157
  854.4 78.0 %reduce-scatter.23.cloned.1.call-done = f32[384,768]{1,0:T(8,128)} async-done(((f32[3072,768]{1,0:T(8,128)}), f32[384,768]{1,0:T(8,128)}) %reduce-scatter.23.cloned.1.call-update) | async-done | bytes 1179664 | tf_op jit(solution)/shard_map/reduce_scatter | solution.py:158
  936.6 22.9 %all-reduce.1 = bf16[3072]{0:T(1024)(128)(2,1)} all-reduce(f32[3072]{0:T(1024)S(1)} %add.496), channel_id=10, replica_groups=mesh['dp'=8,'seq'=4] {'dp'}, use_global_device_ids=true, to_apply=%region_104.105.clone | all-reduce | flops 3072 | bytes 18432
  976.9 30.0 %reduce-scatter.31.cloned.1.call-done = f32[96,10]{1,0:T(8,128)} async-done(((f32[768,10]{1,0:T(8,128)}), f32[96,10]{1,0:T(8,128)}) %reduce-scatter.31.cloned.1.call-update) | async-done | bytes 3856
  1007.7 12.1 %all-reduce.2 = (bf16[3,96]{1,0:T(4,128)(2,1)S(1)}, bf16[10,96]{1,0:T(8,128)(2,1)S(1)}, bf16[384]{0:T(512)(128)(2,1)S(1)}) all-reduce(bf16[3,96]{1,0:T(4,128)(2,1)S(1)} %copy.333, bf16[10,96]{1,0:T(8,128)(2,1)S(1)} %copy.335, bf16[384]{0:T(512)(128)(2,1)S(1)} %dynamic-slice.3), channel_id=1, replica_groups=mesh['dp'=8,'seq'=4] {'seq'}, use_global_device_ids=true, to_apply=%region_79.80 | all-reduce | flops 1632 | bytes 6528 | tf_op jit(solution)/shard_map/psum | solution.py:163
  1021.5 94.5 %all-reduce.6.cloned.1.call-done = (bf16[96,2304]{0,1:T(8,128)(2,1)}, bf16[96,2304]{0,1:T(8,128)(2,1)}, bf16[96,768]{1,0:T(8,128)(2,1)}, bf16[96,768]{1,0:T(8,12...) async-done(((bf16[96,2304]{0,1:T(8,128)(2,1)}, bf16[96,2304]{0,1:T(8,128)(2,1)}, bf16[96,768]{1,0:T(8,128)(2,1)}, bf16[96,768]{1,0:T(8,128)(2,1)}, ...) | async-done | bytes 2359312 | tf_op jit(solution)/shard_map/psum | solution.py:163
  (901 shorter events, 534.7 us)
Async XLA Ops:
  7.2 39.4 %all-gather.14.cloned.1.call-start = ((), (), s32[]{:S(2)}) async-start(), calls=%async_computation.30 | async-start | bytes 3981312 | tf_op jit(solution)/shard_map/all_gather | solution.py:141
  7.9 74.4 %all-gather.10.cloned.1.call-start = ((), (), s32[]{:S(2)}) async-start(), calls=%async_computation.28 | async-start | bytes 3981312 | tf_op jit(solution)/shard_map/all_gather | solution.py:139
  8.7 197.1 %all-gather.12.cloned.1.call-start = ((), (), s32[]{:S(2)}) async-start(), calls=%async_computation.29 | async-start | bytes 1327104 | tf_op jit(solution)/shard_map/all_gather | solution.py:140
  9.4 281.6 %all-gather.16.cloned.1.call-start = ((), (), s32[]{:S(2)}) async-start(), calls=%async_computation.31 | async-start | bytes 1327104 | tf_op jit(solution)/shard_map/all_gather | solution.py:142
  10.0 286.1 %all-gather.18.cloned.1.call-start = ((), (), s32[]{:S(2)}) async-start(), calls=%async_computation.32 | async-start | bytes 5308416 | tf_op jit(solution)/shard_map/all_gather | solution.py:143
  49.8 13.9 %all-to-all-start.8 = ((bf16[1,64,2,4,192]{4,1,2,0,3:T(8,128)(2,1)}), bf16[1,64,2,4,192]{4,1,2,0,3:T(8,128)(2,1)S(1)}, u32[]{:S(2)}, u32[]{:S(2)}) async-start(bf16[1,64,2,4,192]{4,1,2,0,3:T(8,128)(2,1)} %copy.279), calls=%async_computation.8 | async-start | bytes 524288 | tf_op jit(solution)/shard_map/all_to_all | solution.py:199
  63.8 23.4 %all-to-all-start.3 = ((bf16[1,64,2,4,192]{4,1,2,0,3:T(8,128)(2,1)}), bf16[1,64,2,4,192]{4,1,2,0,3:T(8,128)(2,1)S(1)}, u32[]{:S(2)}, u32[]{:S(2)}) async-start(bf16[1,64,2,4,192]{4,1,2,0,3:T(8,128)(2,1)} %copy.263), calls=%async_computation.3 | async-start | bytes 524288 | tf_op jit(solution)/shard_map/all_to_all | solution.py:199
  87.2 33.5 %all-to-all-start = ((bf16[1,256,3,4,192]{1,4,2,0,3:T(8,128)(2,1)}), bf16[1,256,3,4,192]{1,4,2,0,3:T(8,128)(2,1)S(1)}, u32[]{:S(2)}, u32[]{:S(2)}) async-start(bf16[1,256,3,4,192]{1,4,2,0,3:T(8,128)(2,1)} %copy.254), calls=%async_computation | async-start | bytes 2359296 | tf_op jit(solution)/shard_map/all_to_all | solution.py:198
  91.8 216.1 %all-gather.20.cloned.1.call-start = ((), (), s32[]{:S(2)}) async-start(), calls=%async_computation.33 | async-start | bytes 5308416 | tf_op jit(solution)/shard_map/all_gather | solution.py:144
  120.7 31.6 %all-to-all-start.5 = ((bf16[1,256,3,4,192]{1,4,2,0,3:T(8,128)(2,1)}), bf16[1,256,3,4,192]{1,4,2,0,3:T(8,128)(2,1)S(1)}, u32[]{:S(2)}, u32[]{:S(2)}) async-start(bf16[1,256,3,4,192]{1,4,2,0,3:T(8,128)(2,1)} %copy.271), calls=%async_computation.5 | async-start | bytes 2359296 | tf_op jit(solution)/shard_map/all_to_all | solution.py:198
  177.0 22.0 %all-to-all-start.1 = ((bf16[4,2,24576]{2,1,0:T(2,128)(2,1)}), bf16[4,2,24576]{2,1,0:T(2,128)(2,1)S(1)}, u32[]{:S(2)}, u32[]{:S(2)}) async-start(bf16[4,2,24576]{2,1,0:T(2,128)(2,1)} %reshape.1926), calls=%async_computation.1 | async-start | bytes 786432 | tf_op jit(solution)/shard_map/all_to_all | solution.py:209
  199.0 15.8 %all-to-all-start.6 = ((bf16[4,2,24576]{2,1,0:T(2,128)(2,1)}), bf16[4,2,24576]{2,1,0:T(2,128)(2,1)S(1)}, u32[]{:S(2)}, u32[]{:S(2)}) async-start(bf16[4,2,24576]{2,1,0:T(2,128)(2,1)} %reshape.1930), calls=%async_computation.6 | async-start | bytes 786432 | tf_op jit(solution)/shard_map/all_to_all | solution.py:209
  241.7 24.2 %all-to-all-start.4 = ((bf16[4,2,24576]{2,1,0:T(2,128)(2,1)}), bf16[4,2,24576]{2,1,0:T(2,128)(2,1)}, u32[]{:S(2)}, u32[]{:S(2)}) async-start(bf16[4,2,24576]{2,1,0:T(2,128)(2,1)} %reshape.1928), calls=%async_computation.4 | async-start | bytes 786432 | tf_op jit(solution)/shard_map/all_to_all | solution.py:230
  265.9 14.2 %all-to-all-start.9 = ((bf16[4,2,24576]{2,1,0:T(2,128)(2,1)}), bf16[4,2,24576]{2,1,0:T(2,128)(2,1)}, u32[]{:S(2)}, u32[]{:S(2)}) async-start(bf16[4,2,24576]{2,1,0:T(2,128)(2,1)} %reshape.1932), calls=%async_computation.9 | async-start | bytes 786432 | tf_op jit(solution)/shard_map/all_to_all | solution.py:230
  350.9 13.9 %all-to-all-start.10 = ((bf16[1,256,4,192]{1,3,0,2:T(8,128)(2,1)}), bf16[1,256,4,192]{1,3,0,2:T(8,128)(2,1)}, u32[]{:S(2)}, u32[]{:S(2)}) async-start(bf16[1,256,4,192]{1,3,0,2:T(8,128)(2,1)} %bitcast.803), calls=%async_computation.10 | async-start | bytes 786432 | tf_op jit(solution)/shard_map/all_to_all | solution.py:261
  355.8 388.5 %reduce-scatter.19.cloned.1.call-start = ((), (), s32[]{:S(2)}) async-start(), calls=%async_computation.35 | async-start | bytes 2654208 | tf_op jit(solution)/shard_map/reduce_scatter | solution.py:156
  364.8 20.0 %all-to-all-start.14 = ((bf16[1,256,4,192]{1,3,0,2:T(8,128)(2,1)}), bf16[1,256,4,192]{1,3,0,2:T(8,128)(2,1)}, u32[]{:S(2)}, u32[]{:S(2)}) async-start(bf16[1,256,4,192]{1,3,0,2:T(8,128)(2,1)} %bitcast.146), calls=%async_computation.14 | async-start | bytes 786432 | tf_op jit(solution)/shard_map/all_to_all | solution.py:261
  401.5 33.9 %all-to-all-start.11 = ((bf16[4,2,24576]{2,1,0:T(2,128)(2,1)}), bf16[4,2,24576]{2,1,0:T(2,128)(2,1)}, u32[]{:S(2)}, u32[]{:S(2)}) async-start(bf16[4,2,24576]{2,1,0:T(2,128)(2,1)} %reshape.1934), calls=%async_computation.11 | async-start | bytes 786432 | tf_op jit(solution)/shard_map/all_to_all | solution.py:268
  435.4 16.1 %all-to-all-start.15 = ((bf16[4,2,24576]{2,1,0:T(2,128)(2,1)}), bf16[4,2,24576]{2,1,0:T(2,128)(2,1)}, u32[]{:S(2)}, u32[]{:S(2)}) async-start(bf16[4,2,24576]{2,1,0:T(2,128)(2,1)} %reshape.1936), calls=%async_computation.15 | async-start | bytes 786432 | tf_op jit(solution)/shard_map/all_to_all | solution.py:268
  451.4 29.1 %all-to-all-start.18 = ((bf16[1,256,2,1,192]{4,2,3,0,1:T(2,128)(2,1)}), bf16[1,256,2,1,192]{4,2,3,0,1:T(2,128)(2,1)}, u32[]{:S(2)}, u32[]{:S(2)}) async-start(bf16[1,256,2,1,192]{4,2,3,0,1:T(2,128)(2,1)} %pad_maximum_fusion.17), calls=%async_computation.18 | async-start | bytes 524288 | tf_op jit(solution)/shard_map/all_to_all | solution.py:301
  456.5 289.5 %reduce-scatter.17.cloned.1.call-start = ((), (), s32[]{:S(2)}) async-start(), calls=%async_computation.34 | async-start | bytes 2654208 | tf_op jit(solution)/shard_map/reduce_scatter | solution.py:154
  500.3 26.3 %all-to-all-start.12 = ((bf16[1,256,4,192]{1,3,0,2:T(8,128)(2,1)}), bf16[1,256,4,192]{1,3,0,2:T(8,128)(2,1)}, u32[]{:S(2)}, u32[]{:S(2)}) async-start(bf16[1,256,4,192]{1,3,0,2:T(8,128)(2,1)} %bitcast.122), calls=%async_computation.12 | async-start | bytes 786432 | tf_op jit(solution)/shard_map/all_to_all | solution.py:288
  504.4 243.2 %reduce-scatter.27.cloned.1.call-start = ((), (), s32[]{:S(2)}) async-start(), calls=%async_computation.39 | async-start | bytes 7962624
  526.6 20.5 %all-to-all-start.16 = ((bf16[1,256,4,192]{1,3,0,2:T(8,128)(2,1)}), bf16[1,256,4,192]{1,3,0,2:T(8,128)(2,1)S(1)}, u32[]{:S(2)}, u32[]{:S(2)}) async-start(bf16[1,256,4,192]{1,3,0,2:T(8,128)(2,1)} %bitcast.159), calls=%async_computation.16 | async-start | bytes 786432 | tf_op jit(solution)/shard_map/all_to_all | solution.py:288
  600.4 43.2 %all-to-all-start.13 = ((bf16[1,1024,3,1,192]{4,2,3,0,1:T(4,128)(2,1)}), bf16[1,1024,3,1,192]{4,2,3,0,1:T(4,128)(2,1)}, u32[]{:S(2)}, u32[]{:S(2)}) async-start(bf16[1,1024,3,1,192]{4,2,3,0,1:T(4,128)(2,1)} %pad_maximum_fusion), calls=%async_computation.13 | async-start | bytes 4194304 | tf_op jit(solution)/shard_map/all_to_all | solution.py:300
  643.6 45.9 %all-to-all-start.17 = ((bf16[1,1024,3,1,192]{4,2,3,0,1:T(4,128)(2,1)}), bf16[1,1024,3,1,192]{4,2,3,0,1:T(4,128)(2,1)S(1)}, u32[]{:S(2)}, u32[]{:S(2)}) async-start(bf16[1,1024,3,1,192]{4,2,3,0,1:T(4,128)(2,1)} %pad_maximum_fusion.1), calls=%async_computation.17 | async-start | bytes 4194304 | tf_op jit(solution)/shard_map/all_to_all | solution.py:300
  647.2 124.7 %reduce-scatter.25.cloned.1.call-start = ((), (), s32[]{:S(2)}) async-start(), calls=%async_computation.38 | async-start | bytes 7962624
  708.0 144.2 %reduce-scatter.21.cloned.1.call-start = ((), (), s32[]{:S(2)}) async-start(), calls=%async_computation.36 | async-start | bytes 10616832 | tf_op jit(solution)/shard_map/reduce_scatter | solution.py:157
  718.6 213.8 %reduce-scatter.23.cloned.1.call-start = ((), (), s32[]{:S(2)}) async-start(), calls=%async_computation.37 | async-start | bytes 10616832 | tf_op jit(solution)/shard_map/reduce_scatter | solution.py:158
  728.0 242.1 %reduce-scatter.29.cloned.1.call-start = ((), (), s32[]{:S(2)}) async-start(), calls=%async_computation.40 | async-start | bytes 442368
  742.2 264.6 %reduce-scatter.31.cloned.1.call-start = ((), (), s32[]{:S(2)}) async-start(), calls=%async_computation.41 | async-start | bytes 442368
  744.0 372.1 %all-reduce.6.cloned.1.call-start = ((), (), s32[]{:S(2)}) async-start(), calls=%async_computation.42 | async-start | bytes 5308416 | tf_op jit(solution)/shard_map/psum | solution.py:163
  (228 other events, 2925.1 us)
Sparse Core Ops, SparseCore 0:
  9.9 36.6 all-gather.13
  48.4 33.8 all-gather.9
  84.2 23.9 all-gather.11
  109.9 23.9 all-gather.15
  135.6 38.7 all-gather.17
  176.1 38.7 all-gather.19
  360.0 42.6 reduce-scatter.18
  476.0 42.6 reduce-scatter.16
  526.7 65.7 reduce-scatter.26
  708.1 63.6 reduce-scatter.24
  775.4 76.8 reduce-scatter.20
  855.6 76.8 reduce-scatter.22
  936.0 33.9 reduce-scatter.28
  973.0 33.8 reduce-scatter.30
  1010.7 105.3 all-reduce.5
where the time goes:
time: 1140 us; the launch traced here: 1130 us
  waiting for transfers between devices  438 us (38%)
  matrix products  207 us (18%)
  local copies, waits for them, and re-layouts  181 us (16%)
  other arithmetic  133 us (12%)
  starting transfers between devices  91.5 us (8%)
  blocking collectives  64.1 us (6%)
  between operations  18.4 us (2%)
    psum x1, waiting for transfers between devices, reduce_grads(): lax.psum(as_sent(shares), 'seq')  94.5 us
    unnamed x476, local copies, waits for them, and re-layouts  82.4 us
    reduce_scatter x1, waiting for transfers between devices, reduce_grads(): lax.psum_scatter(gradients[4], 'dp', scatter_dimension=0, tiled=True)  78.1 us
    reduce_scatter x1, waiting for transfers between devices, reduce_grads(): lax.psum_scatter(gradients[5], 'dp', scatter_dimension=0, tiled=True)  78 us
    unnamed x19, waiting for transfers between devices  60.4 us
    dot_general x14, matrix products, product(): return jnp.dot(left, right, preferred_element_type=jnp.float32)  48.8 us
    all_to_all x2, waiting for transfers between devices, micro_step(): lax.all_to_all(d_packed, 'seq', split_axis=1, concat_axis=3, tiled=True)  47.6 us
    dot_general x14, matrix products, left_transposed(): lax.dot_general(left, right, (((0,), (0,)), ((), ())), preferred_element_...  41 us
  transfers between devices with their start and end apart: 35, of which 18 were waited for; matrix products, arithmetic and copies ran while one was open for 39% of the time, Pallas kernels for 0%

commit v1 on v0

v1 whole, which is shorter than its diff:
```python
import jax
import jax.numpy as jnp
from jax import lax
from jax.experimental import pallas as pl
from jax.experimental.pallas import tpu as pltpu
from jax.sharding import PartitionSpec as P

HD = 64
PAIR = 2 * HD
EPSILON = 1e-05
MASKED = -1e30
LOW = jnp.bfloat16
WIDE = jnp.float32


def product(left, right):
    return jnp.dot(left, right, preferred_element_type=WIDE)


def left_transposed(left, right):
    return lax.dot_general(left, right, (((0,), (0,)), ((), ())), preferred_element_type=WIDE)


def right_transposed(left, right):
    return lax.dot_general(left, right, (((1,), (1,)), ((), ())), preferred_element_type=WIDE)


def column_total(values):
    return jnp.sum(values.astype(WIDE), axis=0)


def layer_norm(summed, gain, offset):
    centre = summed - jnp.mean(summed, axis=-1, keepdims=True)
    spread = jnp.mean(centre * centre, axis=-1, keepdims=True)
    return centre * lax.rsqrt(spread + EPSILON) * gain + offset


def norm_backward(summed, gain, upstream):
    centre = summed - jnp.mean(summed, axis=-1, keepdims=True)
    spread = jnp.mean(centre * centre, axis=-1, keepdims=True)
    inverse = lax.rsqrt(spread + EPSILON)
    unit = centre * inverse
    scaled = upstream * gain
    mean_scaled = jnp.mean(scaled, axis=-1, keepdims=True)
    mean_both = jnp.mean(scaled * unit, axis=-1, keepdims=True)
    d_summed = (scaled - mean_scaled - unit * mean_both) * inverse
    return d_summed, jnp.sum(upstream * unit, axis=0), jnp.sum(upstream, axis=0)


def stacked_heads(values):
    lane = lax.broadcasted_iota(jnp.int32, values.shape, 1)
    none = jnp.zeros_like(values)
    return jnp.concatenate(
        [jnp.where(lane < HD, values, none), jnp.where(lane >= HD, values, none)], axis=0
    )


def merged_heads(stacked):
    half = stacked.shape[0] // 2
    lane = lax.broadcasted_iota(jnp.int32, (half, PAIR), 1)
    return jnp.where(lane < HD, stacked[:half], stacked[half:])


def forward_kernel(q_ref, kv_ref, qid_ref, kid_ref, o_ref, total_ref):
    queries = stacked_heads(q_ref[0]) * jnp.asarray(HD**-0.5, LOW)
    scores = right_transposed(queries, kv_ref[0, :, :PAIR])
    qid = qid_ref[0]
    allowed = kid_ref[0] <= jnp.concatenate([qid, qid], axis=0)
    scores = jnp.where(allowed, scores, MASKED)
    highest = jnp.max(scores, axis=-1, keepdims=True)
    exponent = jnp.exp(scores - highest)
    denominator = jnp.sum(exponent, axis=-1, keepdims=True)
    context = product(exponent.astype(LOW), kv_ref[0, :, PAIR:]) / denominator
    o_ref[0] = merged_heads(context).astype(LOW)
    totals = highest + jnp.log(denominator)
    total_ref[0, 0] = jnp.transpose(jnp.broadcast_to(totals, (totals.shape[0], 128)))[:8]


def backward_kernel(q_ref, kv_ref, qid_ref, kid_ref, o_ref, do_ref, total_ref, dq_ref, dkv_ref):
    queries = stacked_heads(q_ref[0]) * jnp.asarray(HD**-0.5, LOW)
    upstream = stacked_heads(do_ref[0])
    both = do_ref[0].astype(WIDE) * o_ref[0].astype(WIDE)
    row = lax.broadcasted_iota(jnp.int32, (8, PAIR), 0)
    lane = lax.broadcasted_iota(jnp.int32, (8, PAIR), 1)
    pick = jnp.where(lane // HD == row, 1.0, 0.0).astype(WIDE)
    inner = lax.dot_general(
        pick,
        both,
        (((1,), (1,)), ((), ())),
        precision=lax.Precision.HIGHEST,
        preferred_element_type=WIDE,
    )
    inner = jnp.concatenate([inner[0:1], inner[1:2]], axis=1)
    keys = kv_ref[0, :, :PAIR]
    qid = qid_ref[0]
    allowed = kid_ref[0] <= jnp.concatenate([qid, qid], axis=1)
    scores = jnp.where(allowed, right_transposed(keys, queries), MASKED)
    weights = jnp.exp(scores - total_ref[0, 0, 0:1])
    dkv_ref[0, :, PAIR:] = product(weights.astype(LOW), upstream).astype(LOW)
    weight_grads = right_transposed(kv_ref[0, :, PAIR:], upstream)
    score_grads = (weights * (weight_grads - inner)).astype(LOW)
    dkv_ref[0, :, :PAIR] = product(score_grads, queries).astype(LOW)
    dq = left_transposed(score_grads, keys) * (HD**-0.5)
    dq_ref[0] = merged_heads(dq).astype(LOW)


def attend_forward(queries, keys_values, ids):
    batch, rows, width = queries.shape
    keys = keys_values.shape[1]
    pairs = width // PAIR
    one = pl.BlockSpec((1, rows, PAIR), lambda b, p: (b, 0, p))
    work = batch * pairs * rows * keys
    return pl.pallas_call(
        forward_kernel,
        grid=(batch, pairs),
        in_specs=[
            one,
            pl.BlockSpec((1, keys, 2 * PAIR), lambda b, p: (b, 0, p)),
            pl.BlockSpec((1, rows, 1), lambda b, p: (b, 0, 0)),
            pl.BlockSpec((1, 1, keys), lambda b, p: (b, 0, 0)),
        ],
        out_specs=[one, pl.BlockSpec((1, 1, 8, 2 * rows), lambda b, p: (b, p, 0, 0))],
        out_shape=[
            jax.ShapeDtypeStruct((batch, rows, width), LOW),
            jax.ShapeDtypeStruct((batch, pairs, 8, 2 * rows), WIDE),
        ],
        cost_estimate=pl.CostEstimate(
            flops=4000 * work, transcendentals=2 * work, bytes_accessed=8 * batch * keys * width
        ),
        name="attend_forward",
    )(queries, keys_values, ids[3], ids[0])


def attend_backward(queries, keys_values, ids, context, upstream, totals, start, count):
    _, rows, width = queries.shape
    keys = keys_values.shape[1]
    pairs = width // PAIR
    one = pl.BlockSpec((1, rows, PAIR), lambda b, p: (start + b, 0, p))
    work = count * pairs * rows * keys
    return pl.pallas_call(
        backward_kernel,
        grid=(count, pairs),
        in_specs=[
            one,
            pl.BlockSpec((1, keys, 2 * PAIR), lambda b, p: (start + b, 0, p)),
            pl.BlockSpec((1, 1, rows), lambda b, p: (start + b, 0, 0)),
            pl.BlockSpec((1, keys, 1), lambda b, p: (start + b, 0, 0)),
            one,
            one,
            pl.BlockSpec((1, 1, 8, 2 * rows), lambda b, p: (start + b, p, 0, 0)),
        ],
        out_specs=[
            pl.BlockSpec((1, rows, PAIR), lambda b, p: (b, 0, p)),
            pl.BlockSpec((1, keys, 2 * PAIR), lambda b, p: (b, 0, p)),
        ],
        out_shape=[
            jax.ShapeDtypeStruct((count, rows, width), LOW),
            jax.ShapeDtypeStruct((count, keys, 2 * width), LOW),
        ],
        cost_estimate=pl.CostEstimate(
            flops=4000 * work, transcendentals=2 * work, bytes_accessed=8 * count * keys * width
        ),
        name="attend_backward",
    )(queries, keys_values, ids[2], ids[1], context, upstream, totals)


CHUNK = 512


def normalised(summed):
    centre = summed - jnp.mean(summed, axis=-1, keepdims=True)
    inverse = lax.rsqrt(jnp.mean(centre * centre, axis=-1, keepdims=True) + EPSILON)
    return centre * inverse, inverse


def normalised_backward(unit, inverse, scaled):
    mean_scaled = jnp.mean(scaled, axis=-1, keepdims=True)
    mean_both = jnp.mean(scaled * unit, axis=-1, keepdims=True)
    return (scaled - mean_scaled - unit * mean_both) * inverse


def gelu_pair(values):
    size = jnp.abs(values) * (0.5**0.5)
    bell = jnp.exp(-0.5 * values * values)
    t = 1.0 / (1.0 + 0.3275911 * size)
    series = t * (
        0.127414796
        + t * (-0.142248368 + t * (0.7107068705 + t * (-0.7265760135 + t * 0.5307027145)))
    )
    tail = series * bell
    below = jnp.where(values >= 0, 1.0 - tail, tail)
    return values * below, below + values * bell * 0.3989422804014327


def total_row(values):
    return jnp.sum(values, axis=0, keepdims=True)


def ffn_kernel(
    first_ref,
    cross_ref,
    cot_ref,
    vector_ref,
    hidden_bias_ref,
    early_ref,
    in_ref,
    out_ref,
    final_ref,
    d_sum_ref,
    d_ctx_ref,
    g_cross_ref,
    sums_ref,
    hidden_sums_ref,
    g_in_ref,
    g_out_ref,
    w_cross,
    w_in,
    w_out,
    hidden,
    slope,
    total,
    low,
    d_low,
    g_in,
    g_out,
    load_sem,
    in_sem,
    out_sem,
):
    rows, width = first_ref.shape
    count = w_in.shape[1] // CHUNK
    cross_at = early_ref.shape[1] - width
    loads = [
        pltpu.make_async_copy(early_ref.at[:, cross_at:], w_cross, load_sem.at[0]),
        pltpu.make_async_copy(in_ref, w_in, load_sem.at[1]),
        pltpu.make_async_copy(out_ref, w_out, load_sem.at[2]),
    ]
    for load in loads:
        load.start()
    loads[0].wait()
    second_sum = first_ref[...] + product(cross_ref[...], w_cross[...]) + vector_ref[0:1]
    unit, inverse = normalised(second_sum)
    second = unit * vector_ref[1:2] + vector_ref[2:3]
    low[...] = second.astype(LOW)
    total[...] = second + vector_ref[3:4]
    d_sum_ref[...] = unit
    loads[1].wait()
    loads[2].wait()

    def forward(step, carry):
        at = pl.ds(pl.multiple_of(step * CHUNK, CHUNK), CHUNK)
        activation = product(low[...], w_in[:, at]) + hidden_bias_ref[:, at]
        value, slope_value = gelu_pair(activation)
        value = value.astype(LOW)
        hidden[:, at] = value
        slope[:, at] = slope_value
        total[...] += product(value, w_out[at, :])
        return carry

    lax.fori_loop(0, count, forward, 0)
    third, third_inverse = normalised(total[...])
    final_ref[...] = (third * vector_ref[4:5] + vector_ref[5:6]).astype(LOW)
    upstream = cot_ref[...].astype(WIDE)
    sums_ref[0:1] = total_row(upstream * third)
    sums_ref[1:2] = total_row(upstream)
    d_third = normalised_backward(third, third_inverse, upstream * vector_ref[4:5])
    d_low[...] = d_third.astype(LOW)
    sums_ref[2:3] = total_row(d_low[...].astype(WIDE))
    total[...] = d_third

    def copies(step):
        at = pl.ds(pl.multiple_of(step * CHUNK, CHUNK), CHUNK)
        return (
            pltpu.make_async_copy(g_in.at[:, at], g_in_ref.at[:, at], in_sem.at[step]),
            pltpu.make_async_copy(g_out.at[at, :], g_out_ref.at[at, :], out_sem.at[step]),
        )

    def backward(step, carry):
        at = pl.ds(pl.multiple_of(step * CHUNK, CHUNK), CHUNK)
        g_out[at, :] = left_transposed(hidden[:, at], d_low[...]).astype(LOW)
        d_hidden = right_transposed(d_low[...], w_out[at, :])
        d_activation = (d_hidden * slope[:, at]).astype(LOW)
        hidden_sums_ref[:, at] = total_row(d_activation.astype(WIDE))
        g_in[:, at] = left_transposed(low[...], d_activation).astype(LOW)
        total[...] += right_transposed(d_activation, w_in[:, at])
        for copy in copies(step):
            copy.start()
        return carry

    lax.fori_loop(0, count, backward, 0)
    d_second = total[...]
    unit = d_sum_ref[...]
    sums_ref[3:4] = total_row(d_second * unit)
    sums_ref[4:5] = total_row(d_second)
    d_second_sum = normalised_backward(unit, inverse, d_second * vector_ref[1:2])
    d_sum_ref[...] = d_second_sum
    d_cross = d_second_sum.astype(LOW)
    sums_ref[5:6] = total_row(d_cross.astype(WIDE))
    d_ctx = right_transposed(d_cross, w_cross[...]).astype(LOW)
    d_ctx_ref[...] = d_ctx
    sums_ref[6:7] = total_row(d_ctx.astype(WIDE))
    sums_ref[7:8] = jnp.zeros_like(sums_ref[7:8])
    g_cross_ref[...] = left_transposed(cross_ref[...], d_cross).astype(LOW)

    def drain(step, carry):
        for copy in copies(step):
            copy.wait()
        return carry

    lax.fori_loop(0, count, drain, 0)


def ffn_stage(first, cross, cotangent, vectors, hidden_bias, early, ffn_in, ffn_out):
    rows, width = first.shape
    hidden_width = ffn_in.shape[1]
    count = hidden_width // CHUNK
    inside = pl.BlockSpec(memory_space=pltpu.VMEM)
    outside = pl.BlockSpec(memory_space=pl.ANY)
    return pl.pallas_call(
        ffn_kernel,
        in_specs=[inside] * 5 + [outside] * 3,
        out_specs=[inside] * 6 + [outside] * 2,
        out_shape=[
            jax.ShapeDtypeStruct((rows, width), LOW),
            jax.ShapeDtypeStruct((rows, width), WIDE),
            jax.ShapeDtypeStruct((rows, width), LOW),
            jax.ShapeDtypeStruct((width, width), LOW),
            jax.ShapeDtypeStruct((8, width), WIDE),
            jax.ShapeDtypeStruct((1, hidden_width), WIDE),
            jax.ShapeDtypeStruct((width, hidden_width), LOW),
            jax.ShapeDtypeStruct((hidden_width, width), LOW),
        ],
        scratch_shapes=[
            pltpu.VMEM((width, width), LOW),
            pltpu.VMEM((width, hidden_width), LOW),
            pltpu.VMEM((hidden_width, width), LOW),
            pltpu.VMEM((rows, hidden_width), LOW),
            pltpu.VMEM((rows, hidden_width), WIDE),
            pltpu.VMEM((rows, width), WIDE),
            pltpu.VMEM((rows, width), LOW),
            pltpu.VMEM((rows, width), LOW),
            pltpu.VMEM((width, hidden_width), LOW),
            pltpu.VMEM((hidden_width, width), LOW),
            pltpu.SemaphoreType.DMA((3,)),
            pltpu.SemaphoreType.DMA((count,)),
            pltpu.SemaphoreType.DMA((count,)),
        ],
        compiler_params=pltpu.CompilerParams(vmem_limit_bytes=58 << 20),
        cost_estimate=pl.CostEstimate(
            flops=16 * rows * width * hidden_width,
            transcendentals=rows * hidden_width,
            bytes_accessed=12 * width * hidden_width,
        ),
        name="ffn_stage",
    )(first, cross, cotangent, vectors, hidden_bias, early, ffn_in, ffn_out)


def gathered_back(own, groups):
    place = lax.axis_index("seq")
    behind = lax.ppermute(own, "seq", [(source, source + 1) for source in range(groups - 1)])
    ahead = lax.ppermute(own, "seq", [(source, source - 1) for source in range(1, groups)])
    if groups == 4:
        last = lax.ppermute(own, "seq", [(0, 3)])
        going = jnp.where(place == 2, behind, own)
        slots = [own, behind, lax.ppermute(going, "seq", [(0, 2), (2, 3)])]
    else:
        slots = [own, behind]
        for step in range(2, groups):
            pairs = [(source, source + 1) for source in range(step - 1, groups - 1)]
            slots.append(lax.ppermute(slots[-1], "seq", pairs))
        last = slots.pop()
    return slots + [jnp.where(place == groups - 1, last, ahead)]


def scatter_back(slots, groups):
    parts = []
    for step in range(groups - 1, 0, -1):
        pairs = [(source, source - step) for source in range(step, groups)]
        parts.append(lax.ppermute(slots[step], "seq", pairs))
    pairs = [(source, source + 1) for source in range(groups - 1)]
    parts.append(lax.ppermute(slots[groups - 1], "seq", pairs))
    return parts


def tied(value, *others):
    return lax.optimization_barrier((value,) + others)[0]


def by_bit(bit, own, other, axis=0):
    own, other = jnp.expand_dims(own, axis), jnp.expand_dims(other, axis)
    return jnp.where(
        bit == 0,
        jnp.concatenate([own, other], axis=axis),
        jnp.concatenate([other, own], axis=axis),
    )


def crossed(value, axis_name, masks):
    count = lax.axis_size(axis_name)
    pairs = [(source, source ^ masks[source % len(masks)]) for source in range(count)]
    return lax.ppermute(value, axis_name, pairs)


CORE = (1,)
FIRST = (2, 4)
SECOND = (4, 2)


def chip_masks(core):
    first = jnp.where(core == 0, 1, 2)
    return first, 3 - first


def gather_rows(shard):
    return lax.all_gather(shard, "dp", axis=0, tiled=True)


def picked(values, position, axis=0):
    return lax.dynamic_index_in_dim(values, position, axis, keepdims=False)


def plus(left, right):
    return (left.astype(WIDE) + right.astype(WIDE)).astype(LOW)


class Chain:
    def __init__(self, steps):
        self.steps = steps
        self.pending = next(steps)
        self.result = None

    def step(self):
        if self.result is None:
            try:
                self.pending = self.steps.send(self.pending)
            except StopIteration as stop:
                self.result = stop.value


def pumped(values, *chains):
    live = [chain for chain in chains if chain.result is None]
    values, arrived = lax.optimization_barrier((values, [chain.pending for chain in live]))
    for chain, brought in zip(live, arrived):
        chain.pending = brought
        chain.step()
    return values


def finished(*chains):
    while any(chain.result is None for chain in chains):
        for chain in chains:
            chain.step()
    return [chain.result for chain in chains]


def places_steps(sums):
    place = lax.axis_index("seq")
    low_bit, high_bit = place % 2, place // 2
    sums = sums.reshape((2, 2) + sums.shape[1:])
    sums = plus(picked(sums, low_bit, 1), (yield crossed(picked(sums, 1 - low_bit, 1), "seq", (1,))))
    sums = plus(picked(sums, high_bit), (yield crossed(picked(sums, 1 - high_bit), "seq", (2,))))
    sums = by_bit(high_bit, sums, (yield crossed(sums, "seq", (2,))))
    return by_bit(low_bit, sums, (yield crossed(sums, "seq", (1,))), 1)


def offloaded_steps(gradient):
    share = yield lax.psum_scatter(gradient, "dp", scatter_dimension=0, tiled=True)
    if lax.axis_size("dp") != 8 or lax.axis_size("seq") != 4:
        return (yield lax.psum(share, "seq")).astype(WIDE)
    rows, columns = share.shape
    sums = yield from places_steps(share.reshape(4, rows // 4, columns))
    return sums.reshape(rows, columns).astype(WIDE)


def exchange_steps(gradient):
    if lax.axis_size("dp") != 8 or lax.axis_size("seq") != 4:
        return (yield from offloaded_steps(gradient))
    index = lax.axis_index("dp")
    core, chip = index % 2, index // 2
    first, second = chip_masks(core)
    rows, columns = gradient.shape
    half = rows // 16
    view = gradient.reshape(4, 2, 2, half, columns)
    sums = plus(picked(view, core, 2), (yield crossed(picked(view, 1 - core, 2), "dp", CORE)))
    going = jnp.stack([picked(sums, chip ^ first), picked(sums, chip ^ 3)])
    kept = jnp.stack([picked(sums, chip), picked(sums, chip ^ second)])
    sums = plus(kept, (yield crossed(going, "dp", FIRST)))
    sums = plus(sums[0], (yield crossed(sums[1], "dp", SECOND)))
    sums = yield from places_steps(sums.reshape(4, half // 2, columns))
    sums = sums.reshape(2, half, columns)
    own = by_bit(core, picked(sums, core), (yield crossed(picked(sums, 1 - core), "dp", CORE)))
    return own.reshape(2 * half, columns).astype(WIDE)


def gather_small(values):
    if lax.axis_size("dp") != 8:
        return lax.all_gather(values, "dp", axis=0)
    index = lax.axis_index("dp")
    out = by_bit(index % 2, values, crossed(values, "dp", CORE))
    out = by_bit(index // 2 % 2, out, crossed(out, "dp", (2,)))
    out = by_bit(index // 4, out, crossed(out, "dp", (4,)))
    return out.reshape((8,) + values.shape)


def small_steps(values):
    if lax.axis_size("dp") != 8 or lax.axis_size("seq") != 4:
        return (yield lax.psum(values, ("dp", "seq")))
    for axis_name, mask in (("dp", 1), ("dp", 2), ("dp", 4), ("seq", 1), ("seq", 2)):
        values = values + (yield crossed(values, axis_name, (mask,)))
    return values


def gather_steps(values):
    if lax.axis_size("seq") != 4:
        return (yield lax.all_gather(values, "seq", axis=0))
    place = lax.axis_index("seq")
    out = by_bit(place % 2, values, (yield crossed(values, "seq", (1,))))
    out = by_bit(place // 2, out, (yield crossed(out, "seq", (2,))))
    return out.reshape((4,) + values.shape)


def chunk_steps(values):
    if lax.axis_size("seq") != 4:
        return (yield lax.psum_scatter(values, "seq", scatter_dimension=0, tiled=False)).astype(WIDE)
    place = lax.axis_index("seq")
    low_bit, high_bit = place % 2, place // 2
    values = values.reshape((2, 2) + values.shape[1:])
    going = picked(values, 1 - low_bit, 1)
    values = plus(picked(values, low_bit, 1), (yield crossed(going, "seq", (1,))))
    going = picked(values, 1 - high_bit)
    return picked(values, high_bit).astype(WIDE) + (yield crossed(going, "seq", (2,))).astype(WIDE)


def interleaved(keys_values):
    rows, columns = keys_values.shape
    view = keys_values.reshape(rows, 2, columns // (2 * PAIR), PAIR)
    return view.transpose(0, 2, 1, 3).reshape(rows, columns)


def deinterleaved(keys_values):
    rows, columns = keys_values.shape
    view = keys_values.reshape(rows, columns // (2 * PAIR), 2, PAIR)
    return view.transpose(0, 2, 1, 3).reshape(rows, columns)


def local(
    tokens,
    encoded,
    cotangent,
    attn_in,
    attn_out,
    cross_in,
    cross_out,
    ffn_in,
    ffn_out,
    gains,
    biases,
    bias_ff,
    block_ids,
    enc_lengths,
):
    groups = lax.axis_size("seq")
    shards = lax.axis_size("dp")
    place = lax.axis_index("seq")
    owner = lax.axis_index("dp")
    batch, local_len, width = tokens.shape
    enc_local = encoded.shape[1]
    rows = batch * local_len
    length = local_len * groups
    enc_length = enc_local * groups
    hidden_width = ffn_in.shape[1]

    attn_q, attn_kv = attn_in[:, :width], interleaved(attn_in[:, width:])
    cross_q, cross_kv = cross_in[:, :width], interleaved(cross_in[:, width:])
    early = gather_rows(
        jnp.concatenate([attn_q, attn_kv, attn_out, cross_q, cross_kv, cross_out], axis=1)
    )
    slots = gathered_back(tokens, groups)
    small = jnp.concatenate([gains, biases, bias_ff.reshape(-1, gains.shape[1])], axis=0)
    small = gather_small(small)
    small = small.astype(WIDE)
    gain_rows = gains.shape[0]
    bias_rows = biases.shape[0]
    vectors = small[:, : gain_rows + bias_rows].transpose(1, 0, 2).reshape(-1, width)
    gain_all = vectors[:gain_rows]
    bias_all = vectors[gain_rows:]
    bias_hidden = small[:, gain_rows + bias_rows :].reshape(hidden_width)
    blank = jnp.zeros((width,), WIDE)
    value_bias = interleaved(jnp.concatenate([blank, bias_all[1]])[None])
    cross_value_bias = interleaved(jnp.concatenate([blank, bias_all[4]])[None])

    chunks = block_ids.reshape(batch, groups, local_len)
    order = (place - jnp.arange(groups)) % groups
    kid = jnp.take(chunks, order, axis=1).reshape(batch, length)
    qid = kid[:, :local_len]
    enc_kid = jnp.broadcast_to(jnp.arange(enc_length, dtype=jnp.int32)[None], (batch, enc_length))
    enc_qid = jnp.broadcast_to(enc_lengths[:, None] - 1, (batch, local_len))
    ids = (kid[:, None, :], kid[:, :, None], qid[:, None, :], qid[:, :, None])
    enc_ids = (enc_kid[:, None, :], enc_kid[:, :, None], enc_qid[:, None, :], enc_qid[:, :, None])

    vectors = (gain_all, bias_all, bias_hidden, value_bias, cross_value_bias)
    early, slots, vectors, ids, enc_ids = lax.optimization_barrier(
        (early, slots, vectors, ids, enc_ids)
    )
    gain_all, bias_all, bias_hidden, value_bias, cross_value_bias = vectors
    attn_q, attn_kv = early[:, :width], early[:, width : 3 * width]
    attn_out, cross_q = early[:, 3 * width : 4 * width], early[:, 4 * width : 5 * width]
    cross_kv = early[:, 5 * width : 7 * width]
    ffn_in = gather_rows(ffn_in)
    ffn_out = gather_rows(ffn_out)
    enc_gather = Chain(gather_steps(tied(encoded, slots[-1])))

    token_all = jnp.concatenate(slots, axis=1).reshape(batch * length, width)
    token_flat = tokens.reshape(rows, width)
    queries = (product(token_flat, attn_q) + bias_all[0]).astype(LOW)
    queries = queries.reshape(batch, local_len, width)
    keys_values = (product(token_all, attn_kv) + value_bias).astype(LOW)
    keys_values = keys_values.reshape(batch, length, 2 * width)

    queries, keys_values = pumped((queries, keys_values), enc_gather)
    context, totals = attend_forward(queries, keys_values, ids)
    context = pumped(context, enc_gather)
    encoded = enc_gather.result
    enc_all = encoded.transpose(1, 0, 2, 3).reshape(batch * enc_length, width)
    enc_kv = (product(enc_all, cross_kv) + cross_value_bias).astype(LOW)
    enc_kv = enc_kv.reshape(batch, enc_length, 2 * width)
    context_flat = context.reshape(rows, width)
    first_sum = token_flat.astype(WIDE) + product(context_flat, attn_out) + bias_all[2]
    first = layer_norm(first_sum, gain_all[0], bias_all[7])
    first_low = first.astype(LOW)
    cross_queries = (product(first_low, cross_q) + bias_all[3]).astype(LOW)
    cross_queries = cross_queries.reshape(batch, local_len, width)
    cross_context, cross_totals = attend_forward(cross_queries, enc_kv, enc_ids)
    cross_flat = cross_context.reshape(rows, width)
    stage_vectors = jnp.stack(
        [bias_all[5], gain_all[1], bias_all[8], bias_all[6], gain_all[2], bias_all[9]]
    )
    final, d_second_sum, d_cross_ctx, grad_cross_out, sums, d_bias_hidden, grad_in, grad_out = (
        ffn_stage(
            first,
            cross_flat,
            cotangent.reshape(rows, width),
            stage_vectors,
            bias_hidden[None],
            early,
            ffn_in,
            ffn_out,
        )
    )
    out_chain = Chain(offloaded_steps(grad_out))
    in_chain = Chain(offloaded_steps(grad_in))
    d_cross_ctx = d_cross_ctx.reshape(cross_context.shape)
    d_cross_q, d_enc = attend_backward(
        cross_queries, enc_kv, enc_ids, cross_context, d_cross_ctx, cross_totals, 0, batch
    )
    d_cross_q = d_cross_q.reshape(rows, width)
    d_enc = d_enc.reshape(-1, 2 * width)
    grad_cross_q = left_transposed(first_low, d_cross_q)
    grad_cross_kv = left_transposed(enc_all, d_enc)
    d_encoded = right_transposed(d_enc, cross_kv).reshape(batch, groups, enc_local, width)
    enc_chain = Chain(chunk_steps(d_encoded.astype(LOW).transpose(1, 0, 2, 3)))
    d_first = d_second_sum + right_transposed(d_cross_q, cross_q)
    d_first_sum, d_gain_one, d_offset_one = norm_backward(first_sum, gain_all[0], d_first)
    d_attn = d_first_sum.astype(LOW)
    middle = [left_transposed(context_flat, d_attn), grad_cross_q, grad_cross_kv, grad_cross_out]
    middle = jnp.concatenate([part.astype(LOW) for part in middle], axis=1)
    mid_chain = Chain(exchange_steps(middle))
    d_context = right_transposed(d_attn, attn_out).astype(LOW).reshape(context.shape)

    d_context = pumped(d_context, out_chain)
    d_queries, d_keys_values, d_parts = [], [], []
    for start in range(batch):
        d_q, d_kv = attend_backward(
            queries, keys_values, ids, context, d_context, totals, start, 1
        )
        d_q, d_kv, d_context = pumped((d_q, d_kv, d_context), mid_chain, out_chain, enc_chain)
        d_part = right_transposed(d_kv[0], attn_kv).astype(LOW)
        d_part = d_part.reshape(groups, local_len, width)
        d_parts.append([d_part[0]] + scatter_back(list(d_part), groups))
        d_queries.append(d_q)
        d_keys_values.append(d_kv)
    d_query = jnp.concatenate(d_queries, axis=0).reshape(rows, width)
    d_kv = jnp.concatenate(d_keys_values, axis=0).reshape(batch * length, 2 * width)
    d_query, d_kv = pumped((d_query, d_kv), mid_chain, out_chain)
    grad_attn = jnp.concatenate(
        [
            left_transposed(token_flat, d_query).astype(LOW),
            left_transposed(token_all, d_kv).astype(LOW),
        ],
        axis=1,
    )
    grad_attn = pumped(grad_attn, mid_chain, in_chain, enc_chain)
    attn_chain = Chain(exchange_steps(grad_attn))
    vector_grads = jnp.stack(
        [
            d_gain_one,
            sums[3],
            sums[0],
            column_total(d_query),
            column_total(d_context.reshape(rows, width)),
            column_total(d_attn),
            column_total(d_cross_q),
            sums[6],
            sums[5],
            sums[2],
            d_offset_one,
            sums[4],
            sums[1],
        ]
    )
    vector_grads = jnp.concatenate([vector_grads, d_bias_hidden.reshape(-1, width)], axis=0)
    small_chain = Chain(small_steps(vector_grads))
    d_tokens = d_first_sum + right_transposed(d_query, attn_q)
    d_tokens = d_tokens.reshape(tokens.shape)
    grad_attn, middle, grad_ffn_out, grad_ffn_in, d_encoded, vector_grads = finished(
        attn_chain, mid_chain, out_chain, in_chain, enc_chain, small_chain
    )
    d_tokens = jnp.stack(
        [
            sum([part.astype(WIDE) for part in parts], d_tokens[number])
            for number, parts in enumerate(d_parts)
        ]
    )
    grad_attn_in = jnp.concatenate(
        [grad_attn[:, :width], deinterleaved(grad_attn[:, width:])], axis=1
    )
    grad_cross_in = jnp.concatenate(
        [middle[:, width : 2 * width], deinterleaved(middle[:, 2 * width : 4 * width])], axis=1
    )
    flat_hidden = vector_grads[gain_rows + bias_rows :].reshape(-1)
    part = width // shards
    mine = lax.dynamic_slice_in_dim(vector_grads, owner * part, part, axis=1)
    hidden_part = hidden_width // shards
    grad_bias_ff = lax.dynamic_slice_in_dim(flat_hidden, owner * hidden_part, hidden_part)
    return (
        final.reshape(batch, local_len, width),
        d_tokens,
        d_encoded,
        grad_attn_in,
        middle[:, :width],
        grad_cross_in,
        middle[:, 4 * width :],
        grad_ffn_in,
        grad_ffn_out,
        mine[:gain_rows],
        mine[gain_rows : gain_rows + bias_rows],
        grad_bias_ff,
    )


def solution(mesh):
    split = P("dp", "seq", None)
    rows = P("dp", None)
    columns = P(None, "dp")
    vector = P("dp")
    in_specs = (split,) * 3 + (rows,) * 6 + (columns, columns, vector, rows, vector)
    out_specs = (split,) * 3 + (rows,) * 6 + (columns, columns, vector)
    return jax.shard_map(local, mesh=mesh, in_specs=in_specs, out_specs=out_specs, check_vma=False)
```

time: 1140 us -> 507 us (0.44)
  waiting for transfers between devices: 438 us -> 134 us
  matrix products: 207 us -> 60.6 us
  local copies, waits for them, and re-layouts: 181 us -> 45.8 us
  Pallas kernels: 0 us -> 104 us
  other arithmetic: 133 us -> 40.4 us
  blocking collectives: 64.1 us -> 0 us
    reduce_scatter x4 -> x2, waiting for transfers between devices: 156 us -> 9.3 us  [offloaded_steps(): lax.psum_scatter(gradient, 'dp', scatter_dimension=0, tiled=True)]
    dot_general x86 -> x5, matrix products: 139 us -> 22.6 us  [product(): return jnp.dot(left, right, preferred_element_type=WIDE)]
    ppermute x0 -> x48, waiting for transfers between devices: none -> 112 us  [the longest x36 84 us: crossed(): return lax.ppermute(value, axis_name, pairs)]
    pallas_call x0 -> x6, Pallas kernels: none -> 104 us  [the longest x3 38.2 us: attend_backward(): pl.pallas_call(backward_kernel, grid=(count, pairs), in_specs=[one, pl.Bl...]
    ppermute x0 -> x48, starting transfers between devices: none -> 102 us  [the longest x36 45.7 us: crossed(): return lax.ppermute(value, axis_name, pairs)]
    all_to_all x20 -> x0, waiting for transfers between devices: 96.1 us -> none  [the longest x2 47.6 us: micro_step(): lax.all_to_all(d_packed, 'seq', split_axis=1, concat_axis=3, tiled=True)]
    psum x1 -> x0, waiting for transfers between devices: 94.5 us -> none  [reduce_grads(): lax.psum(as_sent(shares), 'seq')]
    all_to_all x20 -> x0, starting transfers between devices: 90.1 us -> none  [the longest x2 10.7 us: micro_step(): lax.all_to_all(cross_ctx_send, 'seq', split_axis=1, concat_axis=2, tiled=...]
  transfers between devices with their start and end apart: 35 -> 53, of which waited for: 18 -> 25; matrix products, arithmetic and copies ran while one was open for 39% -> 26% of each run, Pallas kernels for 0% -> 14%
where the time goes in v1:
time: 507 us; the launch traced here: 502 us
  waiting for transfers between devices  134 us (26%)
  Pallas kernels  104 us (21%)
  starting transfers between devices  102 us (20%)
  matrix products  60.6 us (12%)
  local copies, waits for them, and re-layouts  45.8 us (9%)
  other arithmetic  40.4 us (8%)
  between operations  15.7 us (3%)
    ppermute x36, waiting for transfers between devices, crossed(): return lax.ppermute(value, axis_name, pairs)  84 us
    ppermute x36, starting transfers between devices, crossed(): return lax.ppermute(value, axis_name, pairs)  45.7 us
    pallas_call x3, Pallas kernels, attend_backward(): pl.pallas_call(backward_kernel, grid=(count, pairs), in_specs=[one, pl.Bl...  38.2 us
    pallas_call x1, Pallas kernels, ffn_stage(): pl.pallas_call(ffn_kernel, in_specs=[inside] * 5 + [outside] * 3, out_spe...  34.2 us
    pallas_call x2, Pallas kernels, attend_forward(): pl.pallas_call(forward_kernel, grid=(batch, pairs), in_specs=[one, pl.Blo...  31.4 us
    ppermute x1, starting transfers between devices, gathered_back(): slots = [own, behind, lax.ppermute(going, 'seq', [(0, 2), (2, 3)])]  30.7 us
    dot_general x5, matrix products, product(): return jnp.dot(left, right, preferred_element_type=WIDE)  22.6 us
    dot_general x6, matrix products, right_transposed(): lax.dot_general(left, right, (((1,), (1,)), ((), ())), preferred_element_...  19.8 us
  transfers between devices with their start and end apart: 53, of which 25 were waited for; matrix products, arithmetic and copies ran while one was open for 26% of the time, Pallas kernels for 14%

profile of v1, /device:TPU:0, one launch (start us, length us, event | category | flops | bytes accessed | tf_op | source)
XLA Modules:
  0.0 501.6 jit_solution(18394221433808072862)
XLA Ops:
  13.2 5.0 collective-permute-start
  37.0 30.7 %collective-permute-start.1 = (bf16[2,256,768]{2,1,0:T(8,128)(2,1)}, bf16[2,256,768]{2,1,0:T(8,128)(2,1)}, u32[]{:S(2)}, u32[]{:S(2)}) collective-permute-start(bf16[2,256,768]{2,1,0:T(8,128)(2,1)} %broadcast_select_fusion.1), channel_id=1, source_target_pairs={{0,2},{2,3},{4,6},{6,7},{8,10},{10,11},{12,14},{14,15},{16,18},{18... | collective-permute-start | bytes 2359304 | tf_op jit(solution)/shard_map/ppermute | solution.py:365
  70.2 6.2 %collective-permute-done.1 = bf16[2,256,768]{2,1,0:T(8,128)(2,1)} collective-permute-done((bf16[2,256,768]{2,1,0:T(8,128)(2,1)}, bf16[2,256,768]{2,1,0:T(8,128)(2,1)}, u32[]{:S(2)}, u32[]{:S(2)}) %collective-permute-start.1) | collective-permute-done | bytes 786464 | tf_op jit(solution)/shard_map/ppermute | solution.py:365
  80.7 4.0 pad_maximum_fusion.3
  84.7 9.7 %add_convert_fusion = bf16[2048,1536]{1,0:T(8,128)(2,1)} fusion(bf16[2048,768]{1,0:T(8,128)(2,1)S(1)} %bitcast.243, f32[1536]{0:T(1024)S(1)} %reduce.3, bf16[768,6144]{1,0:T(8,128)(2,1)} %all-gather.4.cloned.1.call-done.early_ref), kind=kOutput, calls=%fused_computation.1 | convolution fusion | flops 4838129664 | bytes 11802624 | tf_op jit(solution)/shard_map/dot_general | solution.py:17
  100.8 20.8 %attend_forward.2 = (bf16[2,256,768]{2,1,0:T(8,128)(2,1)}, f32[2,6,8,512]{3,2,1,0:T(8,128)}) custom-call(bf16[2,256,768]{2,1,0:T(8,128)(2,1)} %bitcast.323, bf16[2,1024,1536]{2,1,0:T(8,128)(2,1)} %bitcast.315, s32[2,256,1]{2,1,0:T(8,128)} %copy.48.qid_ref, s32[2,1,1024]{2,1,0:T(1,128)} %broadcast_select_fusion.3.kid_ref), custom_call_target="tpu_custom_call" | custom-call | flops 12582912000 | bytes 12582912 | tf_op jit(solution)/shard_map/attend_forward/pallas_call | solution.py:113
  129.7 4.2 fusion.6
  133.9 10.6 %attend_forward.3 = (bf16[2,256,768]{2,1,0:T(8,128)(2,1)}, f32[2,6,8,512]{3,2,1,0:T(8,128)}) custom-call(bf16[2,256,768]{2,1,0:T(8,128)(2,1)} %bitcast.326, bf16[2,256,1536]{2,1,0:T(8,128)(2,1)} %bitcast.320, s32[2,256,1]{2,1,0:T(8,128)} %broadcast_in_dim_broadcast_in_dim.11.qid_ref, s32[2,1,256]{2,1,0:T(1,128)} %broadcast_in_dim_broadcast_in_dim.8.kid_ref), custom_call_target="tpu_custom_call" | custom-call | flops 3145728000 | bytes 3145728 | tf_op jit(solution)/shard_map/attend_forward/pallas_call | solution.py:113
  144.5 11.3 %all-gather.8.cloned.1.call-done.out_ref = bf16[3072,768]{1,0:T(8,128)(2,1)} async-done(((bf16[384,768]{1,0:T(8,128)(2,1)}), bf16[3072,768]{1,0:T(8,128)(2,1)}) %all-gather.8.cloned.1.call-update) | async-done | bytes 4718608 | tf_op jit(solution)/shard_map/all_gather | solution.py:415
  155.9 34.2 %ffn_stage.1 = (bf16[512,768]{1,0:T(8,128)(2,1)}, f32[512,768]{1,0:T(8,128)}, bf16[512,768]{1,0:T(8,128)(2,1)}, bf16[768,768]{1,0:T(8,128)(2,1)}, f32[8,768]{1,0...) custom-call(f32[512,768]{1,0:T(8,128)} %copy-done.7, ...), custom_call_target="tpu_custom_call" | custom-call | flops 19327352832 | bytes 28311552 | tf_op jit(solution)/shard_map/ffn_stage/pallas_call | solution.py:319
  190.1 12.8 %attend_backward.3 = (bf16[2,256,768]{2,1,0:T(8,128)(2,1)}, bf16[2,256,1536]{2,1,0:T(8,128)(2,1)}) custom-call(bf16[2,256,768]{2,1,0:T(8,128)(2,1)} %bitcast.327, bf16[2,256,1536]{2,1,0:T(8,128)(2,1)} %bitcast.321, s32[2,1,256]{2,1,0:T(1,128)} %broadcast_in_dim_broadcast_in_dim.10.qid_ref, s32[2,256,1]{2,1,0:T(8,128)} %broadcast_in_dim_broadcast_in_dim.9.kid_ref, ...), custom_call_target="tpu_custom_call" | custom-call | flops 3145728000 | bytes 3145728 | tf_op jit(solution)/shard_map/attend_backward/pallas_call | solution.py:140
  234.7 9.3 %reduce-scatter.3.cloned.1.call-done = bf16[384,768]{1,0:T(8,128)(2,1)} async-done(((bf16[3072,768]{1,0:T(8,128)(2,1)}), bf16[384,768]{1,0:T(8,128)(2,1)}) %reduce-scatter.3.cloned.1.call-update) | async-done | bytes 589840 | tf_op jit(solution)/shard_map/reduce_scatter | solution.py:467
  246.5 12.8 %attend_backward.4 = (bf16[1,256,768]{2,1,0:T(8,128)(2,1)}, bf16[1,1024,1536]{2,1,0:T(8,128)(2,1)}) custom-call(bf16[2,256,768]{2,1,0:T(8,128)(2,1)} %bitcast.324, bf16[2,1024,1536]{2,1,0:T(8,128)(2,1)} %bitcast.316, s32[2,1,256]{2,1,0:T(1,128)} %broadcast_in_dim.124.qid_ref, s32[2,1024,1]{2,1,0:T(8,128)} %broadcast_select_fusion.2.kid_ref, ...), custom_call_target="tpu_custom_call" | custom-call | flops 6291456000 | bytes 6291456 | tf_op jit(solution)/shard_map/attend_backward/pallas_call | solution.py:140
  266.8 4.3 fusion.14
  278.0 4.2 collective-permute-start.14
  282.9 12.6 %attend_backward.5 = (bf16[1,256,768]{2,1,0:T(8,128)(2,1)}, bf16[1,1024,1536]{2,1,0:T(8,128)(2,1)}) custom-call(bf16[2,256,768]{2,1,0:T(8,128)(2,1)} %bitcast.325, bf16[2,1024,1536]{2,1,0:T(8,128)(2,1)} %bitcast.317, s32[2,1,256]{2,1,0:T(1,128)} %broadcast_in_dim.124.qid_ref, s32[2,1024,1]{2,1,0:T(8,128)} %broadcast_select_fusion.2.kid_ref, ...), custom_call_target="tpu_custom_call" | custom-call | flops 6291456000 | bytes 6291456 | tf_op jit(solution)/shard_map/attend_backward/pallas_call | solution.py:140
  295.5 5.8 %collective-permute-done.13 = bf16[96,768]{1,0:T(8,128)(2,1)} collective-permute-done((bf16[96,768]{1,0:T(8,128)(2,1)}, bf16[96,768]{1,0:T(8,128)(2,1)}, u32[]{:S(2)}, u32[]{:S(2)}) %collective-permute-start.13) | collective-permute-done | bytes 147488 | tf_op jit(solution)/shard_map/ppermute | solution.py:401
  303.8 4.3 collective-permute-start.16
  311.4 4.3 fusion.19
  322.9 5.3 %collective-permute-done.16 = bf16[96,768]{1,0:T(8,128)(2,1)S(1)} collective-permute-done((bf16[96,768]{1,0:T(8,128)(2,1)S(1)}, bf16[96,768]{1,0:T(8,128)(2,1)S(1)}, u32[]{:S(2)}, u32[]{:S(2)}) %collective-permute-start.16) | collective-permute-done | bytes 147488 | tf_op jit(solution)/shard_map/ppermute | solution.py:401
  331.7 9.4 %convolution_convert_fusion = bf16[768,1536]{1,0:T(8,128)(2,1)} fusion(bf16[2048,768]{1,0:T(8,128)(2,1)} %bitcast.244, bf16[2048,1536]{1,0:T(8,128)(2,1)} %bitcast.237), kind=kOutput, calls=%fused_computation.9 | convolution fusion | flops 4833017856 | bytes 11796480 | tf_op jit(solution)/shard_map/dot_general | solution.py:21
  363.1 16.1 %collective-permute-done.22 = bf16[256,768]{1,0:T(8,128)(2,1)S(1)} collective-permute-done((bf16[256,768]{1,0:T(8,128)(2,1)S(1)}, bf16[256,768]{1,0:T(8,128)(2,1)S(1)}, u32[]{:S(2)}, u32[]{:S(2)}) %collective-permute-start.22) | collective-permute-done | bytes 393248 | tf_op jit(solution)/shard_map/ppermute | solution.py:379
  383.5 6.9 %collective-permute-start.46 = (f32[17,768]{1,0:T(8,128)S(1)}, f32[17,768]{1,0:T(8,128)S(1)}, u32[]{:S(2)}, u32[]{:S(2)}) collective-permute-start(f32[17,768]{1,0:T(8,128)S(1)} %add.382), channel_id=1, source_target_pairs={{0,1},{1,0},{2,3},{3,2},{4,5},{5,4},{6,7},{7,6},{8,9},{9,8},{10,11... | collective-permute-start | bytes 156680 | tf_op jit(solution)/shard_map/ppermute | solution.py:401
  396.3 4.5 collective-permute-done.47
  412.8 10.6 %collective-permute-done.34 = bf16[24,3840]{1,0:T(8,128)(2,1)S(1)} collective-permute-done((bf16[24,3840]{1,0:T(8,128)(2,1)S(1)}, bf16[24,3840]{1,0:T(8,128)(2,1)S(1)}, u32[]{:S(2)}, u32[]{:S(2)}) %collective-permute-start.34) | collective-permute-done | bytes 184352 | tf_op jit(solution)/shard_map/ppermute | solution.py:401
  426.7 8.7 %collective-permute-done.35 = bf16[24,3840]{1,0:T(8,128)(2,1)S(1)} collective-permute-done((bf16[24,3840]{1,0:T(8,128)(2,1)S(1)}, bf16[24,3840]{1,0:T(8,128)(2,1)S(1)}, u32[]{:S(2)}, u32[]{:S(2)}) %collective-permute-start.35) | collective-permute-done | bytes 184352 | tf_op jit(solution)/shard_map/ppermute | solution.py:401
  440.6 7.9 %collective-permute-done.40 = bf16[24,3072]{1,0:T(8,128)(2,1)S(1)} collective-permute-done((bf16[24,3072]{1,0:T(8,128)(2,1)S(1)}, bf16[24,3072]{1,0:T(8,128)(2,1)S(1)}, u32[]{:S(2)}, u32[]{:S(2)}) %collective-permute-start.40) | collective-permute-done | bytes 147488 | tf_op jit(solution)/shard_map/ppermute | solution.py:401
  457.1 4.4 collective-permute-done.28
  463.4 4.2 collective-permute-done.29
  471.6 5.8 %collective-permute-done.30 = bf16[24,2304]{1,0:T(8,128)(2,1)S(1)} collective-permute-done((bf16[24,2304]{1,0:T(8,128)(2,1)S(1)}, bf16[24,2304]{1,0:T(8,128)(2,1)S(1)}, u32[]{:S(2)}, u32[]{:S(2)}) %collective-permute-start.30) | collective-permute-done | bytes 110624 | tf_op jit(solution)/shard_map/ppermute | solution.py:401
  479.4 4.7 collective-permute-done.31
  484.4 5.7 %collective-permute-done.32 = bf16[2,24,2304]{2,1,0:T(8,128)(2,1)S(1)} collective-permute-done((bf16[2,24,2304]{2,1,0:T(8,128)(2,1)S(1)}, bf16[2,24,2304]{2,1,0:T(8,128)(2,1)S(1)}, u32[]{:S(2)}, u32[]{:S(2)}) %collective-permute-start.32) | collective-permute-done | bytes 221216 | tf_op jit(solution)/shard_map/ppermute | solution.py:401
  (407 shorter events, 184.6 us)
Async XLA Ops:
  7.2 69.2 %all-gather.4.cloned.1.call-start = ((), (), s32[]{:S(2)}) async-start(), calls=%async_computation.2 | async-start | bytes 10616832 | tf_op jit(solution)/shard_map/all_gather | solution.py:415
  12.4 132.2 %all-gather.6.cloned.1.call-start = ((), (), s32[]{:S(2)}) async-start(), calls=%async_computation.3 | async-start | bytes 5308416 | tf_op jit(solution)/shard_map/all_gather | solution.py:415
  13.1 142.8 %all-gather.8.cloned.1.call-start = ((), (), s32[]{:S(2)}) async-start(), calls=%async_computation.4 | async-start | bytes 5308416 | tf_op jit(solution)/shard_map/all_gather | solution.py:415
  13.2 22.9 %collective-permute-start = (bf16[2,256,768]{2,1,0:T(8,128)(2,1)S(1)}, bf16[2,256,768]{2,1,0:T(8,128)(2,1)S(1)}, u32[]{:S(2)}, u32[]{:S(2)}) collective-permute-start(bf16[2,256,768]{2,1,0:T(8,128)(2,1)S(1)} %copy-done.11), channel_id=1, source_target_pairs={{0,1},{1,2},{2,3},{4,5},{5,6},{6,7},{8,9},{9,10},{10,11},{12,13},{... | collective-permute-start | bytes 2359304 | tf_op jit(solution)/shard_map/ppermute | solution.py:360
  18.2 50.7 %collective-permute-start.2 = (bf16[2,256,768]{2,1,0:T(8,128)(2,1)S(1)}, bf16[2,256,768]{2,1,0:T(8,128)(2,1)S(1)}, u32[]{:S(2)}, u32[]{:S(2)}) collective-permute-start(bf16[2,256,768]{2,1,0:T(8,128)(2,1)S(1)} %copy-done.11), channel_id=1, source_target_pairs={{0,3},{4,7},{8,11},{12,15},{16,19},{20,23},{24,27},{28,31}} | collective-permute-start | bytes 2359304 | tf_op jit(solution)/shard_map/ppermute | solution.py:363
  21.5 47.4 %collective-permute-start.3 = (bf16[2,256,768]{2,1,0:T(8,128)(2,1)S(1)}, bf16[2,256,768]{2,1,0:T(8,128)(2,1)}, u32[]{:S(2)}, u32[]{:S(2)}) collective-permute-start(bf16[2,256,768]{2,1,0:T(8,128)(2,1)S(1)} %copy-done.11), channel_id=1, source_target_pairs={{1,0},{2,1},{3,2},{5,4},{6,5},{7,6},{9,8},{10,9},{11,10},{13,12},{... | collective-permute-start | bytes 2359304 | tf_op jit(solution)/shard_map/ppermute | solution.py:361
  23.0 221.0 %reduce-scatter.3.cloned.1.call-start = ((), (), s32[]{:S(2)}) async-start(), calls=%async_computation.5 | async-start | bytes 5308416 | tf_op jit(solution)/shard_map/reduce_scatter | solution.py:467
  30.7 37.0 %collective-permute-start.6 = (bf16[2,2,17,96]{3,2,1,0:T(8,128)(2,1)S(1)}, bf16[2,2,17,96]{3,2,1,0:T(8,128)(2,1)S(1)}, u32[]{:S(2)}, u32[]{:S(2)}) collective-permute-start(bf16[2,2,17,96]{3,2,1,0:T(8,128)(2,1)S(1)} %maximum_select_fusion.19), channel_id=1, source_target_pairs={{0,16},{4,20},{8,24},{12,28},{16,0},{20,4},{24,8},{28,12},{1,17},{... | collective-permute-start | bytes 39176 | tf_op jit(solution)/shard_map/ppermute | solution.py:401
  37.0 39.4 %collective-permute-start.1 = (bf16[2,256,768]{2,1,0:T(8,128)(2,1)}, bf16[2,256,768]{2,1,0:T(8,128)(2,1)}, u32[]{:S(2)}, u32[]{:S(2)}) collective-permute-start(bf16[2,256,768]{2,1,0:T(8,128)(2,1)} %broadcast_select_fusion.1), channel_id=1, source_target_pairs={{0,2},{2,3},{4,6},{6,7},{8,10},{10,11},{12,14},{14,15},{16,18},{18... | collective-permute-start | bytes 2359304 | tf_op jit(solution)/shard_map/ppermute | solution.py:365
  79.1 18.2 %collective-permute-start.7 = (bf16[2,64,768]{2,1,0:T(8,128)(2,1)S(1)}, bf16[2,64,768]{2,1,0:T(8,128)(2,1)S(1)}, u32[]{:S(2)}, u32[]{:S(2)}) collective-permute-start(bf16[2,64,768]{2,1,0:T(8,128)(2,1)S(1)} %copy-done.36), channel_id=1, source_target_pairs={{0,1},{1,0},{2,3},{3,2},{4,5},{5,4},{6,7},{7,6},{8,9},{9,8},{10,11... | collective-permute-start | bytes 589832 | tf_op jit(solution)/shard_map/ppermute | solution.py:401
  97.4 24.3 %collective-permute-start.8 = (bf16[2,2,64,768]{3,2,1,0:T(8,128)(2,1)S(1)}, bf16[2,2,64,768]{3,2,1,0:T(8,128)(2,1)S(1)}, u32[]{:S(2)}, u32[]{:S(2)}) collective-permute-start(bf16[2,2,64,768]{3,2,1,0:T(8,128)(2,1)S(1)} %maximum_select_fusion.7), channel_id=1, source_target_pairs={{0,2},{1,3},{2,0},{3,1},{4,6},{5,7},{6,4},{7,5},{8,10},{9,11},{10,... | collective-permute-start | bytes 1179656 | tf_op jit(solution)/shard_map/ppermute | solution.py:401
  190.1 219.9 %reduce-scatter.5.cloned.1.call-start = ((), (), s32[]{:S(2)}) async-start(), calls=%async_computation.6 | async-start | bytes 5308416 | tf_op jit(solution)/shard_map/reduce_scatter | solution.py:467
  224.1 35.2 %collective-permute-start.9 = (bf16[4,2,48,3840]{3,2,1,0:T(8,128)(2,1)}, bf16[4,2,48,3840]{3,2,1,0:T(8,128)(2,1)}, u32[]{:S(2)}, u32[]{:S(2)}) collective-permute-start(bf16[4,2,48,3840]{3,2,1,0:T(8,128)(2,1)} %dynamic-slice_bitcast_fusion), channel_id=1, source_target_pairs={{0,4},{4,0},{8,12},{12,8},{16,20},{20,16},{24,28},{28,24},{1,5},{5... | collective-permute-start | bytes 8847368 | tf_op jit(solution)/shard_map/ppermute | solution.py:401
  228.2 31.2 %collective-permute-start.11 = (bf16[2,2,64,768]{3,2,1,0:T(8,128)(2,1)S(1)}, bf16[2,2,64,768]{3,2,1,0:T(8,128)(2,1)S(1)}, u32[]{:S(2)}, u32[]{:S(2)}) collective-permute-start(bf16[2,2,64,768]{3,2,1,0:T(8,128)(2,1)S(1)} %bitcast.289), channel_id=1, source_target_pairs={{0,1},{1,0},{2,3},{3,2},{4,5},{5,4},{6,7},{7,6},{8,9},{9,8},{10,11... | collective-permute-start | bytes 1179656 | tf_op jit(solution)/shard_map/ppermute | solution.py:401
  245.0 14.4 %collective-permute-start.10 = (bf16[2,96,768]{2,1,0:T(8,128)(2,1)S(1)}, bf16[2,96,768]{2,1,0:T(8,128)(2,1)S(1)}, u32[]{:S(2)}, u32[]{:S(2)}) collective-permute-start(bf16[2,96,768]{2,1,0:T(8,128)(2,1)S(1)} %dynamic-slice_bitcast_fusion.5), channel_id=1, source_target_pairs={{0,1},{1,0},{2,3},{3,2},{4,5},{5,4},{6,7},{7,6},{8,9},{9,8},{10,11... | collective-permute-start | bytes 884744 | tf_op jit(solution)/shard_map/ppermute | solution.py:401
  265.3 37.4 %collective-permute-start.12 = (bf16[2,2,48,3840]{3,2,1,0:T(8,128)(2,1)}, bf16[2,2,48,3840]{3,2,1,0:T(8,128)(2,1)S(1)}, u32[]{:S(2)}, u32[]{:S(2)}) collective-permute-start(bf16[2,2,48,3840]{3,2,1,0:T(8,128)(2,1)} %pad_maximum_fusion.5), channel_id=1, source_target_pairs={{0,8},{4,20},{8,0},{12,28},{16,24},{20,4},{24,16},{28,12},{1,9},{5... | collective-permute-start | bytes 4423688 | tf_op jit(solution)/shard_map/ppermute | solution.py:401
  272.2 75.0 %collective-permute-start.17 = (bf16[256,768]{1,0:T(8,128)(2,1)}, bf16[256,768]{1,0:T(8,128)(2,1)}, u32[]{:S(2)}, u32[]{:S(2)}) collective-permute-start(bf16[256,768]{1,0:T(8,128)(2,1)} %get-tuple-element.161), channel_id=1, source_target_pairs={{3,0},{7,4},{11,8},{15,12},{19,16},{23,20},{27,24},{31,28}} | collective-permute-start | bytes 1179656 | tf_op jit(solution)/shard_map/ppermute | solution.py:379
  273.6 84.7 %collective-permute-start.20 = (bf16[256,768]{1,0:T(8,128)(2,1)}, bf16[256,768]{1,0:T(8,128)(2,1)}, u32[]{:S(2)}, u32[]{:S(2)}) collective-permute-start(bf16[256,768]{1,0:T(8,128)(2,1)} %get-tuple-element.161), channel_id=1, source_target_pairs={{0,1},{1,2},{2,3},{4,5},{5,6},{6,7},{8,9},{9,10},{10,11},{12,13},{... | collective-permute-start | bytes 1179656 | tf_op jit(solution)/shard_map/ppermute | solution.py:381
  278.0 24.7 %collective-permute-start.14 = (bf16[2,64,768]{2,1,0:T(8,128)(2,1)S(1)}, bf16[2,64,768]{2,1,0:T(8,128)(2,1)}, u32[]{:S(2)}, u32[]{:S(2)}) collective-permute-start(bf16[2,64,768]{2,1,0:T(8,128)(2,1)S(1)} %dynamic-slice_bitcast_fusion.8), channel_id=1, source_target_pairs={{0,2},{1,3},{2,0},{3,1},{4,6},{5,7},{6,4},{7,5},{8,10},{9,11},{10,... | collective-permute-start | bytes 589832 | tf_op jit(solution)/shard_map/ppermute | solution.py:401
  282.9 18.4 %collective-permute-start.13 = (bf16[96,768]{1,0:T(8,128)(2,1)}, bf16[96,768]{1,0:T(8,128)(2,1)}, u32[]{:S(2)}, u32[]{:S(2)}) collective-permute-start(bf16[96,768]{1,0:T(8,128)(2,1)} %dynamic-slice_bitcast_fusion.11), channel_id=1, source_target_pairs={{0,2},{1,3},{2,0},{3,1},{4,6},{5,7},{6,4},{7,5},{8,10},{9,11},{10,... | collective-permute-start | bytes 442376 | tf_op jit(solution)/shard_map/ppermute | solution.py:401
  301.3 47.2 %collective-permute-start.18 = (bf16[256,768]{1,0:T(8,128)(2,1)}, bf16[256,768]{1,0:T(8,128)(2,1)}, u32[]{:S(2)}, u32[]{:S(2)}) collective-permute-start(bf16[256,768]{1,0:T(8,128)(2,1)} %get-tuple-element.159), channel_id=1, source_target_pairs={{2,0},{3,1},{6,4},{7,5},{10,8},{11,9},{14,12},{15,13},{18,16},{19,... | collective-permute-start | bytes 1179656 | tf_op jit(solution)/shard_map/ppermute | solution.py:379
  303.8 24.4 %collective-permute-start.16 = (bf16[96,768]{1,0:T(8,128)(2,1)S(1)}, bf16[96,768]{1,0:T(8,128)(2,1)S(1)}, u32[]{:S(2)}, u32[]{:S(2)}) collective-permute-start(bf16[96,768]{1,0:T(8,128)(2,1)S(1)} %fusion.58), channel_id=1, source_target_pairs={{0,2},{1,3},{2,0},{3,1},{4,6},{5,7},{6,4},{7,5},{8,10},{9,11},{10,... | collective-permute-start | bytes 442376 | tf_op jit(solution)/shard_map/ppermute | solution.py:401
  310.1 19.4 %collective-permute-start.15 = (bf16[2,48,3840]{2,1,0:T(8,128)(2,1)S(1)}, bf16[2,48,3840]{2,1,0:T(8,128)(2,1)S(1)}, u32[]{:S(2)}, u32[]{:S(2)}) collective-permute-start(bf16[2,48,3840]{2,1,0:T(8,128)(2,1)S(1)} %slice_bitcast_fusion.1), channel_id=1, source_target_pairs={{0,16},{4,12},{8,24},{12,4},{16,0},{20,28},{24,8},{28,20},{1,17},{... | collective-permute-start | bytes 2211848 | tf_op jit(solution)/shard_map/ppermute | solution.py:401
  328.2 24.3 %collective-permute-start.19 = (bf16[256,768]{1,0:T(8,128)(2,1)}, bf16[256,768]{1,0:T(8,128)(2,1)}, u32[]{:S(2)}, u32[]{:S(2)}) collective-permute-start(bf16[256,768]{1,0:T(8,128)(2,1)} %get-tuple-element.160), channel_id=1, source_target_pairs={{1,0},{2,1},{3,2},{5,4},{6,5},{7,6},{9,8},{10,9},{11,10},{13,12},{... | collective-permute-start | bytes 1179656 | tf_op jit(solution)/shard_map/ppermute | solution.py:379
  347.2 15.8 %collective-permute-start.21 = (bf16[256,768]{1,0:T(8,128)(2,1)S(1)}, bf16[256,768]{1,0:T(8,128)(2,1)S(1)}, u32[]{:S(2)}, u32[]{:S(2)}) collective-permute-start(bf16[256,768]{1,0:T(8,128)(2,1)S(1)} %copy-done.41), channel_id=1, source_target_pairs={{3,0},{7,4},{11,8},{15,12},{19,16},{23,20},{27,24},{31,28}} | collective-permute-start | bytes 1179656 | tf_op jit(solution)/shard_map/ppermute | solution.py:379
  348.5 31.3 %collective-permute-start.24 = (bf16[256,768]{1,0:T(8,128)(2,1)S(1)}, bf16[256,768]{1,0:T(8,128)(2,1)S(1)}, u32[]{:S(2)}, u32[]{:S(2)}) collective-permute-start(bf16[256,768]{1,0:T(8,128)(2,1)S(1)} %copy-done.41), channel_id=1, source_target_pairs={{0,1},{1,2},{2,3},{4,5},{5,6},{6,7},{8,9},{9,10},{10,11},{12,13},{... | collective-permute-start | bytes 1179656 | tf_op jit(solution)/shard_map/ppermute | solution.py:381
  352.5 26.7 %collective-permute-start.22 = (bf16[256,768]{1,0:T(8,128)(2,1)S(1)}, bf16[256,768]{1,0:T(8,128)(2,1)S(1)}, u32[]{:S(2)}, u32[]{:S(2)}) collective-permute-start(bf16[256,768]{1,0:T(8,128)(2,1)S(1)} %copy-done.43), channel_id=1, source_target_pairs={{2,0},{3,1},{6,4},{7,5},{10,8},{11,9},{14,12},{15,13},{18,16},{19,... | collective-permute-start | bytes 1179656 | tf_op jit(solution)/shard_map/ppermute | solution.py:379
  353.8 26.0 %collective-permute-start.23 = (bf16[256,768]{1,0:T(8,128)(2,1)S(1)}, bf16[256,768]{1,0:T(8,128)(2,1)S(1)}, u32[]{:S(2)}, u32[]{:S(2)}) collective-permute-start(bf16[256,768]{1,0:T(8,128)(2,1)S(1)} %copy-done.42), channel_id=1, source_target_pairs={{1,0},{2,1},{3,2},{5,4},{6,5},{7,6},{9,8},{10,9},{11,10},{13,12},{... | collective-permute-start | bytes 1179656 | tf_op jit(solution)/shard_map/ppermute | solution.py:379
  358.3 49.1 %collective-permute-start.42 = (bf16[2,96,768]{2,1,0:T(8,128)(2,1)}, bf16[2,96,768]{2,1,0:T(8,128)(2,1)}, u32[]{:S(2)}, u32[]{:S(2)}) collective-permute-start(bf16[2,96,768]{2,1,0:T(8,128)(2,1)} %maximum_select_fusion.14), channel_id=1, source_target_pairs={{0,1},{1,0},{2,3},{3,2},{4,5},{5,4},{6,7},{7,6},{8,9},{9,8},{10,11... | collective-permute-start | bytes 884744 | tf_op jit(solution)/shard_map/ppermute | solution.py:401
  363.1 46.9 %collective-permute-start.25 = (bf16[2,24,3840]{2,1,0:T(8,128)(2,1)}, bf16[2,24,3840]{2,1,0:T(8,128)(2,1)}, u32[]{:S(2)}, u32[]{:S(2)}) collective-permute-start(bf16[2,24,3840]{2,1,0:T(8,128)(2,1)} %dynamic-slice_bitcast_fusion.3), channel_id=1, source_target_pairs={{0,1},{1,0},{2,3},{3,2},{4,5},{5,4},{6,7},{7,6},{8,9},{9,8},{10,11... | collective-permute-start | bytes 1105928 | tf_op jit(solution)/shard_map/ppermute | solution.py:401
  412.8 26.3 %collective-permute-start.26 = (bf16[4,2,48,2304]{3,2,1,0:T(8,128)(2,1)S(1)}, bf16[4,2,48,2304]{3,2,1,0:T(8,128)(2,1)S(1)}, u32[]{:S(2)}, u32[]{:S(2)}) collective-permute-start(bf16[4,2,48,2304]{3,2,1,0:T(8,128)(2,1)S(1)} %dynamic-slice_bitcast_fusion.1), channel_id=1, source_target_pairs={{0,4},{4,0},{8,12},{12,8},{16,20},{20,16},{24,28},{28,24},{1,5},{5... | collective-permute-start | bytes 5308424 | tf_op jit(solution)/shard_map/ppermute | solution.py:401
  435.5 14.5 %collective-permute-start.36 = (bf16[2,24,3840]{2,1,0:T(8,128)(2,1)S(1)}, bf16[2,24,3840]{2,1,0:T(8,128)(2,1)S(1)}, u32[]{:S(2)}, u32[]{:S(2)}) collective-permute-start(bf16[2,24,3840]{2,1,0:T(8,128)(2,1)S(1)} %maximum_select_fusion.10), channel_id=1, source_target_pairs={{0,1},{1,0},{2,3},{3,2},{4,5},{5,4},{6,7},{7,6},{8,9},{9,8},{10,11... | collective-permute-start | bytes 1105928 | tf_op jit(solution)/shard_map/ppermute | solution.py:401
  (83 other events, 521.4 us)
Sparse Core Ops, SparseCore 0:
  12.5 61.9 all-gather.3
  76.3 38.7 all-gather.5
  117.1 38.7 all-gather.7
  190.2 53.7 reduce-scatter.2
  247.3 60.2 reduce-scatter.4

commit v2 on v1

--- a/solution.py
+++ b/solution.py
@@ -372,14 +372,26 @@
     return slots + [jnp.where(place == groups - 1, last, ahead)]
 
 
-def scatter_back(slots, groups):
-    parts = []
-    for step in range(groups - 1, 0, -1):
-        pairs = [(source, source - step) for source in range(step, groups)]
-        parts.append(lax.ppermute(slots[step], "seq", pairs))
-    pairs = [(source, source + 1) for source in range(groups - 1)]
-    parts.append(lax.ppermute(slots[groups - 1], "seq", pairs))
-    return parts
+def scatter_steps(slots, groups):
+    forth = [(source, source + 1) for source in range(groups - 1)]
+    if groups == 4:
+        ahead = lax.ppermute(slots[2], "seq", [(3, 2)])
+        parts = [
+            lax.ppermute(slots[3], "seq", [(3, 0)]),
+            lax.ppermute(slots[2], "seq", [(2, 0)]),
+            lax.ppermute(slots[3], "seq", forth),
+        ]
+        ahead, parts = yield ahead, parts
+        back = [(source, source - 1) for source in range(1, groups)]
+        last, parts = yield lax.ppermute(plus(slots[1], ahead), "seq", back), parts
+        parts = parts + [last]
+    else:
+        parts = [lax.ppermute(slots[groups - 1], "seq", forth)]
+        for step in range(groups - 1, 0, -1):
+            pairs = [(source, source - step) for source in range(step, groups)]
+            parts.append(lax.ppermute(slots[step], "seq", pairs))
+        parts = yield parts
+    return sum([part.astype(WIDE) for part in parts], slots[0].astype(WIDE))
 
 
 def tied(value, *others):
@@ -455,21 +467,17 @@
 
 def places_steps(sums):
     place = lax.axis_index("seq")
-    low_bit, high_bit = place % 2, place // 2
-    sums = sums.reshape((2, 2) + sums.shape[1:])
-    sums = plus(picked(sums, low_bit, 1), (yield crossed(picked(sums, 1 - low_bit, 1), "seq", (1,))))
-    sums = plus(picked(sums, high_bit), (yield crossed(picked(sums, 1 - high_bit), "seq", (2,))))
-    sums = by_bit(high_bit, sums, (yield crossed(sums, "seq", (2,))))
-    return by_bit(low_bit, sums, (yield crossed(sums, "seq", (1,))), 1)
+    sums = plus(sums, (yield lax.ppermute(sums, "seq", [(0, 1), (3, 2)])))
+    sums = plus(sums, (yield lax.ppermute(sums, "seq", [(1, 2), (2, 1)])))
+    back = yield lax.ppermute(sums, "seq", [(1, 0), (2, 3)])
+    return jnp.where((place == 0) | (place == 3), back, sums)
 
 
 def offloaded_steps(gradient):
     share = yield lax.psum_scatter(gradient, "dp", scatter_dimension=0, tiled=True)
     if lax.axis_size("dp") != 8 or lax.axis_size("seq") != 4:
         return (yield lax.psum(share, "seq")).astype(WIDE)
-    rows, columns = share.shape
-    sums = yield from places_steps(share.reshape(4, rows // 4, columns))
-    return sums.reshape(rows, columns).astype(WIDE)
+    return (yield from places_steps(share)).astype(WIDE)
 
 
 def exchange_steps(gradient):
@@ -486,8 +494,7 @@
     kept = jnp.stack([picked(sums, chip), picked(sums, chip ^ second)])
     sums = plus(kept, (yield crossed(going, "dp", FIRST)))
     sums = plus(sums[0], (yield crossed(sums[1], "dp", SECOND)))
-    sums = yield from places_steps(sums.reshape(4, half // 2, columns))
-    sums = sums.reshape(2, half, columns)
+    sums = yield from places_steps(sums)
     own = by_bit(core, picked(sums, core), (yield crossed(picked(sums, 1 - core), "dp", CORE)))
     return own.reshape(2 * half, columns).astype(WIDE)
 
@@ -655,33 +662,39 @@
     )
     d_cross_q = d_cross_q.reshape(rows, width)
     d_enc = d_enc.reshape(-1, 2 * width)
-    grad_cross_q = left_transposed(first_low, d_cross_q)
-    grad_cross_kv = left_transposed(enc_all, d_enc)
-    d_encoded = right_transposed(d_enc, cross_kv).reshape(batch, groups, enc_local, width)
-    enc_chain = Chain(chunk_steps(d_encoded.astype(LOW).transpose(1, 0, 2, 3)))
     d_first = d_second_sum + right_transposed(d_cross_q, cross_q)
     d_first_sum, d_gain_one, d_offset_one = norm_backward(first_sum, gain_all[0], d_first)
     d_attn = d_first_sum.astype(LOW)
-    middle = [left_transposed(context_flat, d_attn), grad_cross_q, grad_cross_kv, grad_cross_out]
-    middle = jnp.concatenate([part.astype(LOW) for part in middle], axis=1)
-    mid_chain = Chain(exchange_steps(middle))
     d_context = right_transposed(d_attn, attn_out).astype(LOW).reshape(context.shape)
 
-    d_context = pumped(d_context, out_chain)
-    d_queries, d_keys_values, d_parts = [], [], []
-    for start in range(batch):
+    def attention_backward(number, d_context):
         d_q, d_kv = attend_backward(
-            queries, keys_values, ids, context, d_context, totals, start, 1
+            queries, keys_values, ids, context, d_context, totals, number, 1
         )
-        d_q, d_kv, d_context = pumped((d_q, d_kv, d_context), mid_chain, out_chain, enc_chain)
         d_part = right_transposed(d_kv[0], attn_kv).astype(LOW)
         d_part = d_part.reshape(groups, local_len, width)
-        d_parts.append([d_part[0]] + scatter_back(list(d_part), groups))
+        return d_q, d_kv, Chain(scatter_steps(list(d_part), groups))
+
+    d_queries, d_keys_values, token_chains = [], [], []
+    for number in range(batch):
+        d_q, d_kv, chain = attention_backward(number, d_context)
         d_queries.append(d_q)
         d_keys_values.append(d_kv)
+        token_chains.append(chain)
+        if number == 0:
+            left = (context_flat, first_low, enc_all, d_attn, d_cross_q, d_enc)
+            left, d_kv = lax.optimization_barrier((left, d_kv))
+            middle = [left_transposed(one, two) for one, two in zip(left[:3], left[3:])]
+            middle.append(grad_cross_out)
+            middle = jnp.concatenate([part.astype(LOW) for part in middle], axis=1)
+            mid_chain = Chain(exchange_steps(middle))
+            d_encoded = right_transposed(left[5], cross_kv)
+            d_encoded = d_encoded.reshape(batch, groups, enc_local, width).astype(LOW)
+            enc_chain = Chain(chunk_steps(d_encoded.transpose(1, 0, 2, 3)))
+            d_context, middle, d_encoded = lax.optimization_barrier((d_context, middle, d_encoded))
     d_query = jnp.concatenate(d_queries, axis=0).reshape(rows, width)
     d_kv = jnp.concatenate(d_keys_values, axis=0).reshape(batch * length, 2 * width)
-    d_query, d_kv = pumped((d_query, d_kv), mid_chain, out_chain)
+    d_query, d_kv = pumped((d_query, d_kv), mid_chain, enc_chain, token_chains[0])
     grad_attn = jnp.concatenate(
         [
             left_transposed(token_flat, d_query).astype(LOW),
@@ -689,8 +702,9 @@
         ],
         axis=1,
     )
-    grad_attn = pumped(grad_attn, mid_chain, in_chain, enc_chain)
     attn_chain = Chain(exchange_steps(grad_attn))
+    d_tokens = d_first_sum + right_transposed(d_query, attn_q)
+    d_tokens = d_tokens.reshape(tokens.shape)
     vector_grads = jnp.stack(
         [
             d_gain_one,
@@ -710,17 +724,11 @@
     )
     vector_grads = jnp.concatenate([vector_grads, d_bias_hidden.reshape(-1, width)], axis=0)
     small_chain = Chain(small_steps(vector_grads))
-    d_tokens = d_first_sum + right_transposed(d_query, attn_q)
-    d_tokens = d_tokens.reshape(tokens.shape)
-    grad_attn, middle, grad_ffn_out, grad_ffn_in, d_encoded, vector_grads = finished(
-        attn_chain, mid_chain, out_chain, in_chain, enc_chain, small_chain
-    )
-    d_tokens = jnp.stack(
-        [
-            sum([part.astype(WIDE) for part in parts], d_tokens[number])
-            for number, parts in enumerate(d_parts)
-        ]
-    )
+    chains = [attn_chain, small_chain, mid_chain, out_chain, enc_chain, in_chain]
+    grad_attn, vector_grads, middle, grad_ffn_out, d_encoded, grad_ffn_in, *d_parts = finished(
+        *chains, *token_chains
+    )
+    d_tokens = jnp.stack([d_tokens[number] + part for number, part in enumerate(d_parts)])
     grad_attn_in = jnp.concatenate(
         [grad_attn[:, :width], deinterleaved(grad_attn[:, width:])], axis=1
     )

time: 507 us -> 506 us (level)
  waiting for transfers between devices: 134 us -> 124 us
  other arithmetic: 40.4 us -> 49.1 us
  starting transfers between devices: 102 us -> 108 us
    ppermute x8 -> x22, starting transfers between devices: 15.6 us -> 53.4 us  [the longest x4 26.4 us: places_steps(): sums = plus(sums, (yield lax.ppermute(sums, 'seq', [(0, 1), (3, 2)])))]
    ppermute x36 -> x20, waiting for transfers between devices: 84 us -> 49.5 us  [crossed(): return lax.ppermute(value, axis_name, pairs)]
    ppermute x1, starting transfers between devices: 30.7 us -> 5.28 us  [gathered_back(): slots = [own, behind, lax.ppermute(going, 'seq', [(0, 2), (2, 3)])]]
    ppermute x8 -> x22, waiting for transfers between devices: 18.2 us -> 36.5 us  [the longest x4 28.4 us: places_steps(): back = (yield lax.ppermute(sums, 'seq', [(1, 0), (2, 3)]))]
    ppermute x1, waiting for transfers between devices: 3.77 us -> 16.9 us  [gathered_back(): lax.ppermute(own, 'seq', [(source, source + 1) for source in range(groups...]
    ppermute x36 -> x20, starting transfers between devices: 45.7 us -> 35.3 us  [crossed(): return lax.ppermute(value, axis_name, pairs)]
    reduce_scatter x2, waiting for transfers between devices: 9.3 us -> 0.04 us  [offloaded_steps(): lax.psum_scatter(gradient, 'dp', scatter_dimension=0, tiled=True)]
    convert_element_type x15 -> x17, other arithmetic: 9.22 us -> 17.6 us  [plus(): return (left.astype(WIDE) + right.astype(WIDE)).astype(LOW)]
  transfers between devices with their start and end apart: 53 -> 51, of which waited for: 25 -> 20; matrix products, arithmetic and copies ran while one was open for 26% -> 27% of each run, Pallas kernels for 14% -> 11%
where the time goes in v2:
time: 506 us; the launch traced here: 500 us
  waiting for transfers between devices  124 us (25%)
  starting transfers between devices  108 us (21%)
  Pallas kernels  103 us (20%)
  matrix products  57.5 us (11%)
  other arithmetic  49.1 us (10%)
  local copies, waits for them, and re-layouts  43.3 us (9%)
  between operations  15.8 us (3%)
    ppermute x20, waiting for transfers between devices, crossed(): return lax.ppermute(value, axis_name, pairs)  49.5 us
    pallas_call x3, Pallas kernels, attend_backward(): pl.pallas_call(backward_kernel, grid=(count, pairs), in_specs=[one, pl.Bl...  37.5 us
    ppermute x20, starting transfers between devices, crossed(): return lax.ppermute(value, axis_name, pairs)  35.3 us
    pallas_call x1, Pallas kernels, ffn_stage(): pl.pallas_call(ffn_kernel, in_specs=[inside] * 5 + [outside] * 3, out_spe...  33.8 us
    pallas_call x2, Pallas kernels, attend_forward(): pl.pallas_call(forward_kernel, grid=(batch, pairs), in_specs=[one, pl.Blo...  31.2 us
    ppermute x4, waiting for transfers between devices, places_steps(): back = (yield lax.ppermute(sums, 'seq', [(1, 0), (2, 3)]))  28.4 us
    ppermute x4, starting transfers between devices, places_steps(): sums = plus(sums, (yield lax.ppermute(sums, 'seq', [(0, 1), (3, 2)])))  26.4 us
    dot_general x6, matrix products, right_transposed(): lax.dot_general(left, right, (((1,), (1,)), ((), ())), preferred_element_...  22.4 us
  transfers between devices with their start and end apart: 51, of which 20 were waited for; matrix products, arithmetic and copies ran while one was open for 27% of the time, Pallas kernels for 11%

profile of v2, /device:TPU:0, one launch (start us, length us, event | category | flops | bytes accessed | tf_op | source)
XLA Modules:
  0.0 500.5 jit_solution(8745280516538129214)
XLA Ops:
  13.2 7.9 %collective-permute-start.2 = (bf16[2,256,768]{2,1,0:T(8,128)(2,1)S(1)}, bf16[2,256,768]{2,1,0:T(8,128)(2,1)}, u32[]{:S(2)}, u32[]{:S(2)}) collective-permute-start(bf16[2,256,768]{2,1,0:T(8,128)(2,1)S(1)} %copy-done.5), channel_id=1, source_target_pairs={{0,3},{4,7},{8,11},{12,15},{16,19},{20,23},{24,27},{28,31}} | collective-permute-start | bytes 2359304 | tf_op jit(solution)/shard_map/ppermute | solution.py:363
  22.3 4.6 collective-permute-start
  37.0 16.9 %collective-permute-done = bf16[2,256,768]{2,1,0:T(8,128)(2,1)S(1)} collective-permute-done((bf16[2,256,768]{2,1,0:T(8,128)(2,1)S(1)}, bf16[2,256,768]{2,1,0:T(8,128)(2,1)S(1)}, u32[]{:S(2)}, u32[]{:S(2)}) %collective-permute-start) | collective-permute-done | bytes 786464 | tf_op jit(solution)/shard_map/ppermute | solution.py:360
  54.8 5.3 %collective-permute-start.1 = (bf16[2,256,768]{2,1,0:T(8,128)(2,1)}, bf16[2,256,768]{2,1,0:T(8,128)(2,1)S(1)}, u32[]{:S(2)}, u32[]{:S(2)}) collective-permute-start(bf16[2,256,768]{2,1,0:T(8,128)(2,1)} %broadcast_select_fusion.1), channel_id=1, source_target_pairs={{0,2},{2,3},{4,6},{6,7},{8,10},{10,11},{12,14},{14,15},{16,18},{18... | collective-permute-start | bytes 2359304 | tf_op jit(solution)/shard_map/ppermute | solution.py:365
  64.4 13.1 %collective-permute-done.1 = bf16[2,256,768]{2,1,0:T(8,128)(2,1)S(1)} collective-permute-done((bf16[2,256,768]{2,1,0:T(8,128)(2,1)}, bf16[2,256,768]{2,1,0:T(8,128)(2,1)S(1)}, u32[]{:S(2)}, u32[]{:S(2)}) %collective-permute-start.1) | collective-permute-done | bytes 786464 | tf_op jit(solution)/shard_map/ppermute | solution.py:365
  87.3 9.7 %add_convert_fusion = bf16[2048,1536]{1,0:T(8,128)(2,1)} fusion(bf16[2048,768]{1,0:T(8,128)(2,1)S(1)} %bitcast.169, f32[1536]{0:T(1024)S(1)} %copy-done.53, bf16[768,6144]{1,0:T(8,128)(2,1)} %all-gather.4.cloned.1.call-done.early_ref), kind=kOutput, calls=%fused_computation.1 | convolution fusion | flops 4838129664 | bytes 11802624 | tf_op jit(solution)/shard_map/dot_general | solution.py:17
  100.0 4.2 collective-permute-start.8
  104.2 20.8 %attend_forward.2 = (bf16[2,256,768]{2,1,0:T(8,128)(2,1)}, f32[2,6,8,512]{3,2,1,0:T(8,128)}) custom-call(bf16[2,256,768]{2,1,0:T(8,128)(2,1)} %bitcast.218, bf16[2,1024,1536]{2,1,0:T(8,128)(2,1)} %bitcast.210, s32[2,256,1]{2,1,0:T(8,128)} %copy.42.qid_ref, s32[2,1,1024]{2,1,0:T(1,128)} %broadcast_select_fusion.5.kid_ref), custom_call_target="tpu_custom_call" | custom-call | flops 12582912000 | bytes 12582912 | tf_op jit(solution)/shard_map/attend_forward/pallas_call | solution.py:113
  133.7 4.2 fusion.6
  138.0 10.5 %attend_forward.3 = (bf16[2,256,768]{2,1,0:T(8,128)(2,1)}, f32[2,6,8,512]{3,2,1,0:T(8,128)}) custom-call(bf16[2,256,768]{2,1,0:T(8,128)(2,1)} %bitcast.223, bf16[2,256,1536]{2,1,0:T(8,128)(2,1)} %bitcast.215, s32[2,256,1]{2,1,0:T(8,128)} %broadcast_in_dim_broadcast_in_dim.11.qid_ref, s32[2,1,256]{2,1,0:T(1,128)} %broadcast_in_dim_broadcast_in_dim.8.kid_ref), custom_call_target="tpu_custom_call" | custom-call | flops 3145728000 | bytes 3145728 | tf_op jit(solution)/shard_map/attend_forward/pallas_call | solution.py:113
  148.4 7.4 %all-gather.8.cloned.1.call-done.out_ref = bf16[3072,768]{1,0:T(8,128)(2,1)} async-done(((bf16[384,768]{1,0:T(8,128)(2,1)}), bf16[3072,768]{1,0:T(8,128)(2,1)}) %all-gather.8.cloned.1.call-update) | async-done | bytes 4718608 | tf_op jit(solution)/shard_map/all_gather | solution.py:427
  155.9 33.8 %ffn_stage.1 = (bf16[512,768]{1,0:T(8,128)(2,1)}, f32[512,768]{1,0:T(8,128)}, bf16[512,768]{1,0:T(8,128)(2,1)}, bf16[768,768]{1,0:T(8,128)(2,1)}, f32[8,768]{1,0...) custom-call(f32[512,768]{1,0:T(8,128)} %get-tuple-element.139.first_ref, ...), custom_call_target="tpu_custom_call" | custom-call | flops 19327352832 | bytes 28311552 | tf_op jit(solution)/shard_map/ffn_stage/pallas_call | solution.py:319
  189.7 12.3 %attend_backward.3 = (bf16[2,256,768]{2,1,0:T(8,128)(2,1)}, bf16[2,256,1536]{2,1,0:T(8,128)(2,1)}) custom-call(bf16[2,256,768]{2,1,0:T(8,128)(2,1)} %bitcast.224, bf16[2,256,1536]{2,1,0:T(8,128)(2,1)} %bitcast.216, s32[2,1,256]{2,1,0:T(1,128)} %broadcast_in_dim_broadcast_in_dim.10.qid_ref, s32[2,256,1]{2,1,0:T(8,128)} %broadcast_in_dim_broadcast_in_dim.9.kid_ref, ...), custom_call_target="tpu_custom_call" | custom-call | flops 3145728000 | bytes 3145728 | tf_op jit(solution)/shard_map/attend_backward/pallas_call | solution.py:140
  211.1 12.6 %attend_backward.4 = (bf16[1,256,768]{2,1,0:T(8,128)(2,1)}, bf16[1,1024,1536]{2,1,0:T(8,128)(2,1)}) custom-call(bf16[2,256,768]{2,1,0:T(8,128)(2,1)} %bitcast.219, bf16[2,1024,1536]{2,1,0:T(8,128)(2,1)} %bitcast.211, s32[2,1,256]{2,1,0:T(1,128)} %broadcast_in_dim.84.qid_ref, s32[2,1024,1]{2,1,0:T(8,128)} %broadcast_select_fusion.3.kid_ref, ...), custom_call_target="tpu_custom_call" | custom-call | flops 6291456000 | bytes 6291456 | tf_op jit(solution)/shard_map/attend_backward/pallas_call | solution.py:140
  223.7 5.3 %fusion.13 = bf16[1024,768]{1,0:T(8,128)(2,1)S(1)} fusion(bf16[768,6144]{1,0:T(8,128)(2,1)} %all-gather.4.cloned.1.call-done.early_ref, bf16[1,1024,1536]{2,1,0:T(8,128)(2,1)} %get-tuple-element.103), kind=kOutput, calls=%fused_computation.28 | convolution fusion | flops 2416705536 | bytes 7077888 | tf_op jit(solution)/shard_map/dot_general | solution.py:25
  237.4 3.8 fusion.25
  247.8 12.6 %attend_backward.5 = (bf16[1,256,768]{2,1,0:T(8,128)(2,1)}, bf16[1,1024,1536]{2,1,0:T(8,128)(2,1)}) custom-call(bf16[2,256,768]{2,1,0:T(8,128)(2,1)} %bitcast.220, bf16[2,1024,1536]{2,1,0:T(8,128)(2,1)} %bitcast.212, s32[2,1,256]{2,1,0:T(1,128)} %broadcast_in_dim.84.qid_ref, s32[2,1024,1]{2,1,0:T(8,128)} %broadcast_select_fusion.3.kid_ref, ...), custom_call_target="tpu_custom_call" | custom-call | flops 6291456000 | bytes 6291456 | tf_op jit(solution)/shard_map/attend_backward/pallas_call | solution.py:140
  260.3 5.4 %fusion.18 = bf16[1024,768]{1,0:T(8,128)(2,1)S(1)} fusion(bf16[768,6144]{1,0:T(8,128)(2,1)} %all-gather.4.cloned.1.call-done.early_ref, bf16[1,1024,1536]{2,1,0:T(8,128)(2,1)} %get-tuple-element.113), kind=kOutput, calls=%fused_computation.29 | convolution fusion | flops 2416705536 | bytes 7077888 | tf_op jit(solution)/shard_map/dot_general | solution.py:25
  272.3 4.2 collective-permute-start.14
  287.2 6.2 %collective-permute-done.10 = bf16[2,2,64,768]{3,2,1,0:T(8,128)(2,1)} collective-permute-done((bf16[2,2,64,768]{3,2,1,0:T(8,128)(2,1)}, bf16[2,2,64,768]{3,2,1,0:T(8,128)(2,1)}, u32[]{:S(2)}, u32[]{:S(2)}) %collective-permute-start.10) | collective-permute-done | bytes 393248 | tf_op jit(solution)/shard_map/ppermute | solution.py:413
  296.2 4.2 fusion
  304.4 6.6 %convolution_convert_fusion = bf16[768,1536]{1,0:T(8,128)(2,1)} fusion(bf16[2048,768]{1,0:T(8,128)(2,1)S(1)} %bitcast.170, bf16[2048,1536]{1,0:T(8,128)(2,1)S(1)} %bitcast.165), kind=kOutput, calls=%fused_computation.9 | convolution fusion | flops 4833017856 | bytes 11796480 | tf_op jit(solution)/shard_map/dot_general | solution.py:21
  317.6 5.3 %collective-permute-start.21 = (bf16[2,64,768]{2,1,0:T(8,128)(2,1)S(1)}, bf16[2,64,768]{2,1,0:T(8,128)(2,1)S(1)}, u32[]{:S(2)}, u32[]{:S(2)}) collective-permute-start(bf16[2,64,768]{2,1,0:T(8,128)(2,1)S(1)} %dynamic-slice_bitcast_fusion.5), channel_id=1, source_target_pairs={{0,2},{1,3},{2,0},{3,1},{4,6},{5,7},{6,4},{7,5},{8,10},{9,11},{10,... | collective-permute-start | bytes 589832 | tf_op jit(solution)/shard_map/ppermute | solution.py:413
  322.9 13.8 %collective-permute-done.42 = f32[17,768]{1,0:T(8,128)S(1)} collective-permute-done((f32[17,768]{1,0:T(8,128)S(1)}, f32[17,768]{1,0:T(8,128)S(1)}, u32[]{:S(2)}, u32[]{:S(2)}) %collective-permute-start.42) | collective-permute-done | bytes 52256 | tf_op jit(solution)/shard_map/ppermute | solution.py:413
  348.7 7.1 %collective-permute-start.45 = (f32[17,768]{1,0:T(8,128)S(1)}, f32[17,768]{1,0:T(8,128)S(1)}, u32[]{:S(2)}, u32[]{:S(2)}) collective-permute-start(f32[17,768]{1,0:T(8,128)S(1)} %add.363), channel_id=1, source_target_pairs={{0,2},{1,3},{2,0},{3,1},{4,6},{5,7},{6,4},{7,5},{8,10},{9,11},{10,... | collective-permute-start | bytes 156680 | tf_op jit(solution)/shard_map/ppermute | solution.py:413
  356.6 6.5 %collective-permute-done.45 = f32[17,768]{1,0:T(8,128)S(1)} collective-permute-done((f32[17,768]{1,0:T(8,128)S(1)}, f32[17,768]{1,0:T(8,128)S(1)}, u32[]{:S(2)}, u32[]{:S(2)}) %collective-permute-start.45) | collective-permute-done | bytes 52256 | tf_op jit(solution)/shard_map/ppermute | solution.py:413
  371.6 15.1 %collective-permute-done.23 = bf16[2,2,48,2304]{3,2,1,0:T(8,128)(2,1)S(1)} collective-permute-done((bf16[2,2,48,2304]{3,2,1,0:T(8,128)(2,1)S(1)}, bf16[2,2,48,2304]{3,2,1,0:T(8,128)(2,1)S(1)}, u32[]{:S(2)}, u32[]{:S(2)}) %collective-permute-start.23) | collective-permute-done | bytes 884768 | tf_op jit(solution)/shard_map/ppermute | solution.py:413
  403.8 4.5 collective-permute-start.25
  419.0 17.4 %collective-permute-start.38 = (bf16[384,768]{1,0:T(8,128)(2,1)}, bf16[384,768]{1,0:T(8,128)(2,1)S(1)}, u32[]{:S(2)}, u32[]{:S(2)}) collective-permute-start(bf16[384,768]{1,0:T(8,128)(2,1)} %reduce-scatter.5.cloned.1.call-done), channel_id=1, source_target_pairs={{0,1},{3,2},{4,5},{7,6},{8,9},{11,10},{12,13},{15,14},{16,17},{19,... | collective-permute-start | bytes 1769480 | tf_op jit(solution)/shard_map/ppermute | solution.py:470
  439.3 4.7 collective-permute-done.27
  468.0 11.7 %collective-permute-done.40 = bf16[384,768]{1,0:T(8,128)(2,1)S(1)} collective-permute-done((bf16[384,768]{1,0:T(8,128)(2,1)S(1)}, bf16[384,768]{1,0:T(8,128)(2,1)S(1)}, u32[]{:S(2)}, u32[]{:S(2)}) %collective-permute-start.40) | collective-permute-done | bytes 589856 | tf_op jit(solution)/shard_map/ppermute | solution.py:472
  480.8 11.6 %collective-permute-done.37 = bf16[96,3072]{1,0:T(8,128)(2,1)S(1)} collective-permute-done((bf16[96,3072]{1,0:T(8,128)(2,1)S(1)}, bf16[96,3072]{1,0:T(8,128)(2,1)S(1)}, u32[]{:S(2)}, u32[]{:S(2)}) %collective-permute-start.37) | collective-permute-done | bytes 589856 | tf_op jit(solution)/shard_map/ppermute | solution.py:472
  (398 shorter events, 175.5 us)
Async XLA Ops:
  7.2 70.3 %all-gather.4.cloned.1.call-start = ((), (), s32[]{:S(2)}) async-start(), calls=%async_computation.2 | async-start | bytes 10616832 | tf_op jit(solution)/shard_map/all_gather | solution.py:427
  12.4 136.1 %all-gather.6.cloned.1.call-start = ((), (), s32[]{:S(2)}) async-start(), calls=%async_computation.3 | async-start | bytes 5308416 | tf_op jit(solution)/shard_map/all_gather | solution.py:427
  13.1 142.8 %all-gather.8.cloned.1.call-start = ((), (), s32[]{:S(2)}) async-start(), calls=%async_computation.4 | async-start | bytes 5308416 | tf_op jit(solution)/shard_map/all_gather | solution.py:427
  13.2 50.0 %collective-permute-start.2 = (bf16[2,256,768]{2,1,0:T(8,128)(2,1)S(1)}, bf16[2,256,768]{2,1,0:T(8,128)(2,1)}, u32[]{:S(2)}, u32[]{:S(2)}) collective-permute-start(bf16[2,256,768]{2,1,0:T(8,128)(2,1)S(1)} %copy-done.5), channel_id=1, source_target_pairs={{0,3},{4,7},{8,11},{12,15},{16,19},{20,23},{24,27},{28,31}} | collective-permute-start | bytes 2359304 | tf_op jit(solution)/shard_map/ppermute | solution.py:363
  21.1 42.1 %collective-permute-start.3 = (bf16[2,256,768]{2,1,0:T(8,128)(2,1)S(1)}, bf16[2,256,768]{2,1,0:T(8,128)(2,1)}, u32[]{:S(2)}, u32[]{:S(2)}) collective-permute-start(bf16[2,256,768]{2,1,0:T(8,128)(2,1)S(1)} %copy-done.5), channel_id=1, source_target_pairs={{1,0},{2,1},{3,2},{5,4},{6,5},{7,6},{9,8},{10,9},{11,10},{13,12},{... | collective-permute-start | bytes 2359304 | tf_op jit(solution)/shard_map/ppermute | solution.py:361
  22.3 31.5 %collective-permute-start = (bf16[2,256,768]{2,1,0:T(8,128)(2,1)S(1)}, bf16[2,256,768]{2,1,0:T(8,128)(2,1)S(1)}, u32[]{:S(2)}, u32[]{:S(2)}) collective-permute-start(bf16[2,256,768]{2,1,0:T(8,128)(2,1)S(1)} %copy-done.5), channel_id=1, source_target_pairs={{0,1},{1,2},{2,3},{4,5},{5,6},{6,7},{8,9},{9,10},{10,11},{12,13},{... | collective-permute-start | bytes 2359304 | tf_op jit(solution)/shard_map/ppermute | solution.py:360
  27.2 391.8 %reduce-scatter.5.cloned.1.call-start = ((), (), s32[]{:S(2)}) async-start(), calls=%async_computation.6 | async-start | bytes 5308416 | tf_op jit(solution)/shard_map/reduce_scatter | solution.py:477
  35.4 24.7 %collective-permute-start.6 = (bf16[2,2,17,96]{3,2,1,0:T(8,128)(2,1)S(1)}, bf16[2,2,17,96]{3,2,1,0:T(8,128)(2,1)S(1)}, u32[]{:S(2)}, u32[]{:S(2)}) collective-permute-start(bf16[2,2,17,96]{3,2,1,0:T(8,128)(2,1)S(1)} %maximum_select_fusion.7), channel_id=1, source_target_pairs={{0,16},{4,20},{8,24},{12,28},{16,0},{20,4},{24,8},{28,12},{1,17},{... | collective-permute-start | bytes 39176 | tf_op jit(solution)/shard_map/ppermute | solution.py:413
  54.8 22.6 %collective-permute-start.1 = (bf16[2,256,768]{2,1,0:T(8,128)(2,1)}, bf16[2,256,768]{2,1,0:T(8,128)(2,1)S(1)}, u32[]{:S(2)}, u32[]{:S(2)}) collective-permute-start(bf16[2,256,768]{2,1,0:T(8,128)(2,1)} %broadcast_select_fusion.1), channel_id=1, source_target_pairs={{0,2},{2,3},{4,6},{6,7},{8,10},{10,11},{12,14},{14,15},{16,18},{18... | collective-permute-start | bytes 2359304 | tf_op jit(solution)/shard_map/ppermute | solution.py:365
  80.2 19.7 %collective-permute-start.7 = (bf16[2,64,768]{2,1,0:T(8,128)(2,1)S(1)}, bf16[2,64,768]{2,1,0:T(8,128)(2,1)S(1)}, u32[]{:S(2)}, u32[]{:S(2)}) collective-permute-start(bf16[2,64,768]{2,1,0:T(8,128)(2,1)S(1)} %copy-done.26), channel_id=1, source_target_pairs={{0,1},{1,0},{2,3},{3,2},{4,5},{5,4},{6,7},{7,6},{8,9},{9,8},{10,11... | collective-permute-start | bytes 589832 | tf_op jit(solution)/shard_map/ppermute | solution.py:413
  100.0 25.0 %collective-permute-start.8 = (bf16[2,2,64,768]{3,2,1,0:T(8,128)(2,1)S(1)}, bf16[2,2,64,768]{3,2,1,0:T(8,128)(2,1)S(1)}, u32[]{:S(2)}, u32[]{:S(2)}) collective-permute-start(bf16[2,2,64,768]{3,2,1,0:T(8,128)(2,1)S(1)} %maximum_select_fusion.3), channel_id=1, source_target_pairs={{0,2},{1,3},{2,0},{3,1},{4,6},{5,7},{6,4},{7,5},{8,10},{9,11},{10,... | collective-permute-start | bytes 1179656 | tf_op jit(solution)/shard_map/ppermute | solution.py:413
  205.4 231.0 %reduce-scatter.3.cloned.1.call-start = ((), (), s32[]{:S(2)}) async-start(), calls=%async_computation.5 | async-start | bytes 5308416 | tf_op jit(solution)/shard_map/reduce_scatter | solution.py:477
  229.9 42.3 %collective-permute-start.11 = (bf16[256,768]{1,0:T(8,128)(2,1)}, bf16[256,768]{1,0:T(8,128)(2,1)}, u32[]{:S(2)}, u32[]{:S(2)}) collective-permute-start(bf16[256,768]{1,0:T(8,128)(2,1)} %get-tuple-element.153), channel_id=1, source_target_pairs={{3,2},{7,6},{11,10},{15,14},{19,18},{23,22},{27,26},{31,30}} | collective-permute-start | bytes 1179656 | tf_op jit(solution)/shard_map/ppermute | solution.py:378
  231.5 55.6 %collective-permute-start.13 = (bf16[256,768]{1,0:T(8,128)(2,1)}, bf16[256,768]{1,0:T(8,128)(2,1)}, u32[]{:S(2)}, u32[]{:S(2)}) collective-permute-start(bf16[256,768]{1,0:T(8,128)(2,1)} %get-tuple-element.153), channel_id=1, source_target_pairs={{2,0},{6,4},{10,8},{14,12},{18,16},{22,20},{26,24},{30,28}} | collective-permute-start | bytes 1179656 | tf_op jit(solution)/shard_map/ppermute | solution.py:381
  244.3 41.6 %collective-permute-start.12 = (bf16[256,768]{1,0:T(8,128)(2,1)}, bf16[256,768]{1,0:T(8,128)(2,1)S(1)}, u32[]{:S(2)}, u32[]{:S(2)}) collective-permute-start(bf16[256,768]{1,0:T(8,128)(2,1)} %get-tuple-element.152), channel_id=1, source_target_pairs={{3,0},{7,4},{11,8},{15,12},{19,16},{23,20},{27,24},{31,28}} | collective-permute-start | bytes 1179656 | tf_op jit(solution)/shard_map/ppermute | solution.py:380
  247.7 45.7 %collective-permute-start.9 = (bf16[4,2,48,3840]{3,2,1,0:T(8,128)(2,1)}, bf16[4,2,48,3840]{3,2,1,0:T(8,128)(2,1)}, u32[]{:S(2)}, u32[]{:S(2)}) collective-permute-start(bf16[4,2,48,3840]{3,2,1,0:T(8,128)(2,1)} %dynamic-slice_bitcast_fusion), channel_id=1, source_target_pairs={{0,4},{4,0},{8,12},{12,8},{16,20},{20,16},{24,28},{28,24},{1,5},{5... | collective-permute-start | bytes 8847368 | tf_op jit(solution)/shard_map/ppermute | solution.py:413
  276.5 16.9 %collective-permute-start.10 = (bf16[2,2,64,768]{3,2,1,0:T(8,128)(2,1)}, bf16[2,2,64,768]{3,2,1,0:T(8,128)(2,1)}, u32[]{:S(2)}, u32[]{:S(2)}) collective-permute-start(bf16[2,2,64,768]{3,2,1,0:T(8,128)(2,1)} %dynamic-slice_bitcast_fusion.2), channel_id=1, source_target_pairs={{0,1},{1,0},{2,3},{3,2},{4,5},{5,4},{6,7},{7,6},{8,9},{9,8},{10,11... | collective-permute-start | bytes 1179656 | tf_op jit(solution)/shard_map/ppermute | solution.py:413
  285.8 123.8 %collective-permute-start.17 = (bf16[256,768]{1,0:T(8,128)(2,1)}, bf16[256,768]{1,0:T(8,128)(2,1)}, u32[]{:S(2)}, u32[]{:S(2)}) collective-permute-start(bf16[256,768]{1,0:T(8,128)(2,1)} %get-tuple-element.151), channel_id=1, source_target_pairs={{2,0},{6,4},{10,8},{14,12},{18,16},{22,20},{26,24},{30,28}} | collective-permute-start | bytes 1179656 | tf_op jit(solution)/shard_map/ppermute | solution.py:381
  296.1 20.1 %collective-permute-start.41 = (f32[17,768]{1,0:T(8,128)S(1)}, f32[17,768]{1,0:T(8,128)S(1)}, u32[]{:S(2)}, u32[]{:S(2)}) collective-permute-start(f32[17,768]{1,0:T(8,128)S(1)} %concatenate.199), channel_id=1, source_target_pairs={{0,4},{4,0},{8,12},{12,8},{16,20},{20,16},{24,28},{28,24},{1,5},{5... | collective-permute-start | bytes 156680 | tf_op jit(solution)/shard_map/ppermute | solution.py:413
  303.0 63.4 %collective-permute-start.29 = (bf16[2,2,48,3840]{3,2,1,0:T(8,128)(2,1)}, bf16[2,2,48,3840]{3,2,1,0:T(8,128)(2,1)}, u32[]{:S(2)}, u32[]{:S(2)}) collective-permute-start(bf16[2,2,48,3840]{3,2,1,0:T(8,128)(2,1)} %pad_maximum_fusion.5), channel_id=1, source_target_pairs={{0,8},{4,20},{8,0},{12,28},{16,24},{20,4},{24,16},{28,12},{1,9},{5... | collective-permute-start | bytes 4423688 | tf_op jit(solution)/shard_map/ppermute | solution.py:413
  314.6 53.5 %collective-permute-start.22 = (bf16[4,2,48,2304]{3,2,1,0:T(8,128)(2,1)S(1)}, bf16[4,2,48,2304]{3,2,1,0:T(8,128)(2,1)S(1)}, u32[]{:S(2)}, u32[]{:S(2)}) collective-permute-start(bf16[4,2,48,2304]{3,2,1,0:T(8,128)(2,1)S(1)} %dynamic-slice_bitcast_fusion.1), channel_id=1, source_target_pairs={{0,4},{4,0},{8,12},{12,8},{16,20},{20,16},{24,28},{28,24},{1,5},{5... | collective-permute-start | bytes 5308424 | tf_op jit(solution)/shard_map/ppermute | solution.py:413
  316.2 20.6 %collective-permute-start.42 = (f32[17,768]{1,0:T(8,128)S(1)}, f32[17,768]{1,0:T(8,128)S(1)}, u32[]{:S(2)}, u32[]{:S(2)}) collective-permute-start(f32[17,768]{1,0:T(8,128)S(1)} %add.360), channel_id=1, source_target_pairs={{0,8},{4,12},{8,0},{12,4},{16,24},{20,28},{24,16},{28,20},{1,9},{5... | collective-permute-start | bytes 156680 | tf_op jit(solution)/shard_map/ppermute | solution.py:413
  317.6 31.1 %collective-permute-start.21 = (bf16[2,64,768]{2,1,0:T(8,128)(2,1)S(1)}, bf16[2,64,768]{2,1,0:T(8,128)(2,1)S(1)}, u32[]{:S(2)}, u32[]{:S(2)}) collective-permute-start(bf16[2,64,768]{2,1,0:T(8,128)(2,1)S(1)} %dynamic-slice_bitcast_fusion.5), channel_id=1, source_target_pairs={{0,2},{1,3},{2,0},{3,1},{4,6},{5,7},{6,4},{7,5},{8,10},{9,11},{10,... | collective-permute-start | bytes 589832 | tf_op jit(solution)/shard_map/ppermute | solution.py:413
  347.4 51.4 %collective-permute-start.16 = (bf16[256,768]{1,0:T(8,128)(2,1)}, bf16[256,768]{1,0:T(8,128)(2,1)}, u32[]{:S(2)}, u32[]{:S(2)}) collective-permute-start(bf16[256,768]{1,0:T(8,128)(2,1)} %get-tuple-element.150), channel_id=1, source_target_pairs={{3,0},{7,4},{11,8},{15,12},{19,16},{23,20},{27,24},{31,28}} | collective-permute-start | bytes 1179656 | tf_op jit(solution)/shard_map/ppermute | solution.py:380
  363.2 47.2 %collective-permute-start.18 = (bf16[256,768]{1,0:T(8,128)(2,1)}, bf16[256,768]{1,0:T(8,128)(2,1)}, u32[]{:S(2)}, u32[]{:S(2)}) collective-permute-start(bf16[256,768]{1,0:T(8,128)(2,1)} %get-tuple-element.150), channel_id=1, source_target_pairs={{0,1},{1,2},{2,3},{4,5},{5,6},{6,7},{8,9},{9,10},{10,11},{12,13},{... | collective-permute-start | bytes 1179656 | tf_op jit(solution)/shard_map/ppermute | solution.py:382
  368.8 17.9 %collective-permute-start.23 = (bf16[2,2,48,2304]{3,2,1,0:T(8,128)(2,1)S(1)}, bf16[2,2,48,2304]{3,2,1,0:T(8,128)(2,1)S(1)}, u32[]{:S(2)}, u32[]{:S(2)}) collective-permute-start(bf16[2,2,48,2304]{3,2,1,0:T(8,128)(2,1)S(1)} %pad_maximum_fusion.6), channel_id=1, source_target_pairs={{0,8},{4,20},{8,0},{12,28},{16,24},{20,4},{24,16},{28,12},{1,9},{5... | collective-permute-start | bytes 2654216 | tf_op jit(solution)/shard_map/ppermute | solution.py:413
  371.0 17.6 %collective-permute-start.30 = (bf16[2,48,3840]{2,1,0:T(8,128)(2,1)S(1)}, bf16[2,48,3840]{2,1,0:T(8,128)(2,1)S(1)}, u32[]{:S(2)}, u32[]{:S(2)}) collective-permute-start(bf16[2,48,3840]{2,1,0:T(8,128)(2,1)S(1)} %slice_bitcast_fusion), channel_id=1, source_target_pairs={{0,16},{4,12},{8,24},{12,4},{16,0},{20,28},{24,8},{28,20},{1,17},{... | collective-permute-start | bytes 2211848 | tf_op jit(solution)/shard_map/ppermute | solution.py:413
  415.0 24.2 %collective-permute-start.33 = (bf16[2,48,3840]{2,1,0:T(8,128)(2,1)S(1)}, bf16[2,48,3840]{2,1,0:T(8,128)(2,1)S(1)}, u32[]{:S(2)}, u32[]{:S(2)}) collective-permute-start(bf16[2,48,3840]{2,1,0:T(8,128)(2,1)S(1)} %add_convert_fusion.5), channel_id=1, source_target_pairs={{1,0},{2,3},{5,4},{6,7},{9,8},{10,11},{13,12},{14,15},{17,16},{18,... | collective-permute-start | bytes 2211848 | tf_op jit(solution)/shard_map/ppermute | solution.py:472
  417.7 26.3 %collective-permute-start.27 = (bf16[2,48,2304]{2,1,0:T(8,128)(2,1)S(1)}, bf16[2,48,2304]{2,1,0:T(8,128)(2,1)S(1)}, u32[]{:S(2)}, u32[]{:S(2)}) collective-permute-start(bf16[2,48,2304]{2,1,0:T(8,128)(2,1)S(1)} %add_convert_fusion.11), channel_id=1, source_target_pairs={{1,0},{2,3},{5,4},{6,7},{9,8},{10,11},{13,12},{14,15},{17,16},{18,... | collective-permute-start | bytes 1327112 | tf_op jit(solution)/shard_map/ppermute | solution.py:472
  419.0 29.6 %collective-permute-start.38 = (bf16[384,768]{1,0:T(8,128)(2,1)}, bf16[384,768]{1,0:T(8,128)(2,1)S(1)}, u32[]{:S(2)}, u32[]{:S(2)}) collective-permute-start(bf16[384,768]{1,0:T(8,128)(2,1)} %reduce-scatter.5.cloned.1.call-done), channel_id=1, source_target_pairs={{0,1},{3,2},{4,5},{7,6},{8,9},{11,10},{12,13},{15,14},{16,17},{19,... | collective-permute-start | bytes 1769480 | tf_op jit(solution)/shard_map/ppermute | solution.py:470
  436.4 17.0 %collective-permute-start.35 = (bf16[96,3072]{1,0:T(8,128)(2,1)}, bf16[96,3072]{1,0:T(8,128)(2,1)}, u32[]{:S(2)}, u32[]{:S(2)}) collective-permute-start(bf16[96,3072]{1,0:T(8,128)(2,1)} %reduce-scatter.3.cloned.1.call-done), channel_id=1, source_target_pairs={{0,1},{3,2},{4,5},{7,6},{8,9},{11,10},{12,13},{15,14},{16,17},{19,... | collective-permute-start | bytes 1769480 | tf_op jit(solution)/shard_map/ppermute | solution.py:470
  465.7 26.6 %collective-permute-start.37 = (bf16[96,3072]{1,0:T(8,128)(2,1)S(1)}, bf16[96,3072]{1,0:T(8,128)(2,1)S(1)}, u32[]{:S(2)}, u32[]{:S(2)}) collective-permute-start(bf16[96,3072]{1,0:T(8,128)(2,1)S(1)} %add_convert_fusion.9), channel_id=1, source_target_pairs={{1,0},{2,3},{5,4},{6,7},{9,8},{10,11},{13,12},{14,15},{17,16},{18,... | collective-permute-start | bytes 1769480 | tf_op jit(solution)/shard_map/ppermute | solution.py:472
  (87 other events, 634.9 us)
Sparse Core Ops, SparseCore 0:
  12.5 61.9 all-gather.3
  76.3 38.7 all-gather.5
  117.0 38.7 all-gather.7
  205.5 53.7 reduce-scatter.4
  283.8 64.9 reduce-scatter.2

commit v3 on v2

--- a/solution.py
+++ b/solution.py
@@ -164,7 +164,7 @@
     )(queries, keys_values, ids[2], ids[1], context, upstream, totals)
 
 
-CHUNK = 512
+CHUNK = 768
 
 
 def normalised(summed):
@@ -196,7 +196,23 @@
     return jnp.sum(values, axis=0, keepdims=True)
 
 
+def slot_copies(source, keep_ref, send_ref, place_ref, semaphores, columns=None, chips=None):
+    rows = keep_ref.shape[1]
+    core = place_ref[0]
+    found = []
+    for chip in range(4) if chips is None else chips:
+        for number, (slots_ref, owner) in enumerate(((keep_ref, core), (send_ref, 1 - core))):
+            at = pl.ds(pl.multiple_of((2 * chip + owner) * rows, 16), rows)
+            slot = place_ref[1 + 4 * number + chip]
+            taken, given = source.at[at], slots_ref.at[slot]
+            if columns is not None:
+                taken, given = source.at[at, columns], slots_ref.at[slot, :, columns]
+            found.append(pltpu.make_async_copy(taken, given, semaphores.at[2 * chip + number]))
+    return found
+
+
 def ffn_kernel(
+    place_ref,
     first_ref,
     cross_ref,
     cot_ref,
@@ -208,27 +224,17 @@
     final_ref,
     d_sum_ref,
     d_ctx_ref,
-    g_cross_ref,
     sums_ref,
     hidden_sums_ref,
-    g_in_ref,
-    g_out_ref,
-    w_cross,
-    w_in,
-    w_out,
-    hidden,
-    slope,
-    total,
-    low,
-    d_low,
-    g_in,
-    g_out,
-    load_sem,
-    in_sem,
-    out_sem,
+    *others,
 ):
+    grad_refs, scratch = others[:-14], others[-14:]
+    w_cross, w_in, w_out, hidden, slope, total, low, d_low, g_in, g_out = scratch[:10]
+    load_sem, out_sem, in_sem, cross_sem = scratch[10:14]
     rows, width = first_ref.shape
-    count = w_in.shape[1] // CHUNK
+    hidden_width = w_in.shape[1]
+    count = hidden_width // CHUNK
+    slotted = len(grad_refs) == 4
     cross_at = early_ref.shape[1] - width
     loads = [
         pltpu.make_async_copy(early_ref.at[:, cross_at:], w_cross, load_sem.at[0]),
@@ -268,13 +274,6 @@
     sums_ref[2:3] = total_row(d_low[...].astype(WIDE))
     total[...] = d_third
 
-    def copies(step):
-        at = pl.ds(pl.multiple_of(step * CHUNK, CHUNK), CHUNK)
-        return (
-            pltpu.make_async_copy(g_in.at[:, at], g_in_ref.at[:, at], in_sem.at[step]),
-            pltpu.make_async_copy(g_out.at[at, :], g_out_ref.at[at, :], out_sem.at[step]),
-        )
-
     def backward(step, carry):
         at = pl.ds(pl.multiple_of(step * CHUNK, CHUNK), CHUNK)
         g_out[at, :] = left_transposed(hidden[:, at], d_low[...]).astype(LOW)
@@ -283,11 +282,31 @@
         hidden_sums_ref[:, at] = total_row(d_activation.astype(WIDE))
         g_in[:, at] = left_transposed(low[...], d_activation).astype(LOW)
         total[...] += right_transposed(d_activation, w_in[:, at])
-        for copy in copies(step):
+        if slotted:
+            for copy in slot_copies(g_out, *grad_refs[2:], place_ref, out_sem, None, [step]):
+                copy.start()
+        return carry
+
+    lax.fori_loop(0, count, backward, 0)
+    if slotted:
+        copies = [
+            slot_copies(g_out, *grad_refs[2:], place_ref, out_sem),
+            slot_copies(
+                g_in, *grad_refs[:2], place_ref, in_sem, pl.ds(0, hidden_width)
+            ),
+            slot_copies(
+                g_in, *grad_refs[:2], place_ref, cross_sem, pl.ds(hidden_width, width)
+            ),
+        ]
+    else:
+        copies = [
+            [pltpu.make_async_copy(g_out, grad_refs[1], out_sem.at[0])],
+            [pltpu.make_async_copy(g_in, grad_refs[0], in_sem.at[0])],
+        ]
+        copies[0][0].start()
+    if slotted:
+        for copy in copies[1]:
             copy.start()
-        return carry
-
-    lax.fori_loop(0, count, backward, 0)
     d_second = total[...]
     unit = d_sum_ref[...]
     sums_ref[3:4] = total_row(d_second * unit)
@@ -296,40 +315,41 @@
     d_sum_ref[...] = d_second_sum
     d_cross = d_second_sum.astype(LOW)
     sums_ref[5:6] = total_row(d_cross.astype(WIDE))
+    g_in[:, hidden_width:] = left_transposed(cross_ref[...], d_cross).astype(LOW)
+    for copy in copies[-1]:
+        copy.start()
     d_ctx = right_transposed(d_cross, w_cross[...]).astype(LOW)
     d_ctx_ref[...] = d_ctx
     sums_ref[6:7] = total_row(d_ctx.astype(WIDE))
     sums_ref[7:8] = jnp.zeros_like(sums_ref[7:8])
-    g_cross_ref[...] = left_transposed(cross_ref[...], d_cross).astype(LOW)
-
-    def drain(step, carry):
-        for copy in copies(step):
+    for group in copies:
+        for copy in group:
             copy.wait()
-        return carry
-
-    lax.fori_loop(0, count, drain, 0)
-
-
-def ffn_stage(first, cross, cotangent, vectors, hidden_bias, early, ffn_in, ffn_out):
+
+
+def ffn_stage(
+    places, first, cross, cotangent, vectors, hidden_bias, early, ffn_in, ffn_out, slotted
+):
     rows, width = first.shape
     hidden_width = ffn_in.shape[1]
     count = hidden_width // CHUNK
     inside = pl.BlockSpec(memory_space=pltpu.VMEM)
     outside = pl.BlockSpec(memory_space=pl.ANY)
+    grads = [(width, hidden_width + width), (hidden_width, width)]
+    if slotted:
+        grads = [(4, shape[0] // 8, shape[1]) for shape in grads for _ in range(2)]
     return pl.pallas_call(
         ffn_kernel,
-        in_specs=[inside] * 5 + [outside] * 3,
-        out_specs=[inside] * 6 + [outside] * 2,
+        in_specs=[pl.BlockSpec(memory_space=pltpu.SMEM)] + [inside] * 5 + [outside] * 3,
+        out_specs=[inside] * 5 + [outside] * len(grads),
         out_shape=[
             jax.ShapeDtypeStruct((rows, width), LOW),
             jax.ShapeDtypeStruct((rows, width), WIDE),
             jax.ShapeDtypeStruct((rows, width), LOW),
-            jax.ShapeDtypeStruct((width, width), LOW),
             jax.ShapeDtypeStruct((8, width), WIDE),
             jax.ShapeDtypeStruct((1, hidden_width), WIDE),
-            jax.ShapeDtypeStruct((width, hidden_width), LOW),
-            jax.ShapeDtypeStruct((hidden_width, width), LOW),
-        ],
+        ]
+        + [jax.ShapeDtypeStruct(shape, LOW) for shape in grads],
         scratch_shapes=[
             pltpu.VMEM((width, width), LOW),
             pltpu.VMEM((width, hidden_width), LOW),
@@ -339,11 +359,12 @@
             pltpu.VMEM((rows, width), WIDE),
             pltpu.VMEM((rows, width), LOW),
             pltpu.VMEM((rows, width), LOW),
-            pltpu.VMEM((width, hidden_width), LOW),
+            pltpu.VMEM((width, hidden_width + width), LOW),
             pltpu.VMEM((hidden_width, width), LOW),
             pltpu.SemaphoreType.DMA((3,)),
-            pltpu.SemaphoreType.DMA((count,)),
-            pltpu.SemaphoreType.DMA((count,)),
+            pltpu.SemaphoreType.DMA((8,)),
+            pltpu.SemaphoreType.DMA((8,)),
+            pltpu.SemaphoreType.DMA((8,)),
         ],
         compiler_params=pltpu.CompilerParams(vmem_limit_bytes=58 << 20),
         cost_estimate=pl.CostEstimate(
@@ -352,46 +373,140 @@
             bytes_accessed=12 * width * hidden_width,
         ),
         name="ffn_stage",
-    )(first, cross, cotangent, vectors, hidden_bias, early, ffn_in, ffn_out)
+    )(places, first, cross, cotangent, vectors, hidden_bias, early, ffn_in, ffn_out)
+
+
+def apart(start, width):
+    pair, half = divmod(start // PAIR, 2)
+    return half * width + pair * PAIR
+
+
+def slotted_products(places, groups, extra=()):
+    arrays = [value for group in groups for pair in group for value in pair]
+    width = arrays[0].shape[1]
+    widths = [group[0][1].shape[1] for group in groups]
+    columns = sum(widths) + (128 if extra else 0)
+    extras = [part[0] for part in extra]
+
+    def kernel(place_ref, *refs):
+        inputs, refs = refs[: len(arrays)], refs[len(arrays) :]
+        extra_refs, refs = refs[: len(extras)], refs[len(extras) :]
+        keep_ref, send_ref = refs[:2]
+        buffers, (rows_ref, total, load_sem, store_sem) = refs[2:-4], refs[-4:]
+        loads = [
+            pltpu.make_async_copy(inputs[number], buffers[number], load_sem.at[number])
+            for number in range(len(arrays))
+        ]
+        for load in loads:
+            load.start()
+        copies = []
+
+        def leave(number, at, size):
+            group = slot_copies(
+                total, keep_ref, send_ref, place_ref, store_sem.at[number], pl.ds(at, size)
+            )
+            for copy in group:
+                copy.start()
+            copies.extend(group)
+
+        at = number = 0
+        for index, group in enumerate(groups):
+            value = None
+            for _ in group:
+                loads[number].wait()
+                loads[number + 1].wait()
+                term = left_transposed(buffers[number][...], buffers[number + 1][...])
+                value = term if value is None else value + term
+                number += 2
+            value = value.astype(LOW)
+            for start in range(0, widths[index], PAIR):
+                given = at + (start if widths[index] == width else apart(start, width))
+                total[:, given : given + PAIR] = value[:, start : start + PAIR]
+            leave(index, at, widths[index])
+            at += widths[index]
+        if extras:
+            rows_ref[...] = jnp.zeros_like(rows_ref)
+            for extra_ref, (_, first, given, count) in zip(extra_refs, extra):
+                rows_ref[given : given + count] = extra_ref[first : first + count]
+            total[:, at:] = jnp.transpose(rows_ref[...]).astype(LOW)
+            leave(len(groups), at, columns - at)
+        for copy in copies:
+            copy.wait()
+
+    outside = pl.BlockSpec(memory_space=pl.ANY)
+    shape = jax.ShapeDtypeStruct((4, width // 8, columns), LOW)
+    return pl.pallas_call(
+        kernel,
+        in_specs=[pl.BlockSpec(memory_space=pltpu.SMEM)]
+        + [outside] * len(arrays)
+        + [pl.BlockSpec(memory_space=pltpu.VMEM)] * len(extras),
+        out_specs=[outside] * 2,
+        out_shape=[shape] * 2,
+        scratch_shapes=[pltpu.VMEM(value.shape, LOW) for value in arrays]
+        + [
+            pltpu.VMEM((128, width), WIDE),
+            pltpu.VMEM((width, columns), LOW),
+            pltpu.SemaphoreType.DMA((len(arrays),)),
+            pltpu.SemaphoreType.DMA((len(groups) + 1, 8)),
+        ],
+        compiler_params=pltpu.CompilerParams(vmem_limit_bytes=58 << 20),
+        cost_estimate=pl.CostEstimate(
+            flops=2 * width * sum(left.size // width * right.shape[1]
+                                  for group in groups for left, right in group),
+            transcendentals=0,
+            bytes_accessed=sum(2 * value.size for value in arrays) + 2 * width * columns,
+        ),
+        name="slotted_products",
+    )(places, *arrays, *extras)
+
+
+def plain_products(groups):
+    found = [sum([left_transposed(*pair) for pair in group]) for group in groups]
+    width = found[0].shape[1]
+    found = [part if part.shape[1] == width else deinterleaved(part) for part in found]
+    return jnp.concatenate([part.astype(LOW) for part in found], axis=1)
 
 
 def gathered_back(own, groups):
-    place = lax.axis_index("seq")
-    behind = lax.ppermute(own, "seq", [(source, source + 1) for source in range(groups - 1)])
-    ahead = lax.ppermute(own, "seq", [(source, source - 1) for source in range(1, groups)])
+    slots = [own]
+    around = lax.ppermute(own, "seq", [(source, (source - 1) % groups) for source in range(groups)])
+    for step in range(1, groups - 1):
+        pairs = [(source, source + 1) for source in range(step - 1, groups - 1)]
+        slots.append(lax.ppermute(slots[-1], "seq", pairs))
+    return slots + [around]
+
+
+def scatter_steps(slots, groups):
+    ring = [(source, (source + 1) % groups) for source in range(groups)]
     if groups == 4:
-        last = lax.ppermute(own, "seq", [(0, 3)])
-        going = jnp.where(place == 2, behind, own)
-        slots = [own, behind, lax.ppermute(going, "seq", [(0, 2), (2, 3)])]
+        parts = [moved(slots[2], "seq", [(3, 2), (2, 1)]), moved(slots[3], "seq", ring)]
+        ahead, around = yield parts
+        back = [(source, source - 1) for source in range(1, groups)]
+        last, around = yield [moved(plus(slots[1], ahead), "seq", back), around]
+        parts = [around, last]
     else:
-        slots = [own, behind]
-        for step in range(2, groups):
-            pairs = [(source, source + 1) for source in range(step - 1, groups - 1)]
-            slots.append(lax.ppermute(slots[-1], "seq", pairs))
-        last = slots.pop()
-    return slots + [jnp.where(place == groups - 1, last, ahead)]
-
-
-def scatter_steps(slots, groups):
-    forth = [(source, source + 1) for source in range(groups - 1)]
-    if groups == 4:
-        ahead = lax.ppermute(slots[2], "seq", [(3, 2)])
-        parts = [
-            lax.ppermute(slots[3], "seq", [(3, 0)]),
-            lax.ppermute(slots[2], "seq", [(2, 0)]),
-            lax.ppermute(slots[3], "seq", forth),
-        ]
-        ahead, parts = yield ahead, parts
-        back = [(source, source - 1) for source in range(1, groups)]
-        last, parts = yield lax.ppermute(plus(slots[1], ahead), "seq", back), parts
-        parts = parts + [last]
-    else:
-        parts = [lax.ppermute(slots[groups - 1], "seq", forth)]
-        for step in range(groups - 1, 0, -1):
+        parts = [moved(slots[groups - 1], "seq", ring)]
+        for step in range(groups - 2, 0, -1):
             pairs = [(source, source - step) for source in range(step, groups)]
-            parts.append(lax.ppermute(slots[step], "seq", pairs))
+            parts.append(moved(slots[step], "seq", pairs))
         parts = yield parts
     return sum([part.astype(WIDE) for part in parts], slots[0].astype(WIDE))
+
+
+class Order:
+    token = None
+
+    def hold(self, value):
+        if self.token is not None:
+            self.token, value = lax.optimization_barrier((self.token, value))
+        return value
+
+
+timeline = Order()
+
+
+def moved(value, axis_name, pairs):
+    return lax.ppermute(timeline.hold(value), axis_name, pairs)
 
 
 def tied(value, *others):
@@ -410,7 +525,7 @@
 def crossed(value, axis_name, masks):
     count = lax.axis_size(axis_name)
     pairs = [(source, source ^ masks[source % len(masks)]) for source in range(count)]
-    return lax.ppermute(value, axis_name, pairs)
+    return moved(value, axis_name, pairs)
 
 
 CORE = (1,)
@@ -433,6 +548,10 @@
 
 def plus(left, right):
     return (left.astype(WIDE) + right.astype(WIDE)).astype(LOW)
+
+
+def summed(*parts):
+    return sum([part.astype(WIDE) for part in parts]).astype(LOW)
 
 
 class Chain:
@@ -447,6 +566,11 @@
                 self.pending = self.steps.send(self.pending)
             except StopIteration as stop:
                 self.result = stop.value
+
+    def advance(self):
+        if self.result is None:
+            self.pending = timeline.hold(self.pending)
+            self.step()
 
 
 def pumped(values, *chains):
@@ -458,18 +582,20 @@
     return values
 
 
-def finished(*chains):
+def finished(*chains, ahead=()):
+    for chain in ahead:
+        chain.advance()
     while any(chain.result is None for chain in chains):
         for chain in chains:
-            chain.step()
+            chain.advance()
     return [chain.result for chain in chains]
 
 
 def places_steps(sums):
     place = lax.axis_index("seq")
-    sums = plus(sums, (yield lax.ppermute(sums, "seq", [(0, 1), (3, 2)])))
-    sums = plus(sums, (yield lax.ppermute(sums, "seq", [(1, 2), (2, 1)])))
-    back = yield lax.ppermute(sums, "seq", [(1, 0), (2, 3)])
+    sums = plus(sums, (yield moved(sums, "seq", [(0, 1), (3, 2)])))
+    sums = plus(sums, (yield moved(sums, "seq", [(1, 2), (2, 1)])))
+    back = yield moved(sums, "seq", [(1, 0), (2, 3)])
     return jnp.where((place == 0) | (place == 3), back, sums)
 
 
@@ -480,23 +606,25 @@
     return (yield from places_steps(share)).astype(WIDE)
 
 
-def exchange_steps(gradient):
-    if lax.axis_size("dp") != 8 or lax.axis_size("seq") != 4:
-        return (yield from offloaded_steps(gradient))
+def slot_steps(keep, send):
+    core = yield crossed(send, "dp", CORE)
+    one = yield crossed(summed(keep[2:], core[2:]), "dp", FIRST)
+    two = yield crossed(summed(keep[1], core[1], one[1]), "dp", SECOND)
+    share = summed(keep[0], core[0], one[0], two)
+    return (yield from places_steps(share)).astype(WIDE)
+
+
+def slot_places():
     index = lax.axis_index("dp")
     core, chip = index % 2, index // 2
-    first, second = chip_masks(core)
-    rows, columns = gradient.shape
-    half = rows // 16
-    view = gradient.reshape(4, 2, 2, half, columns)
-    sums = plus(picked(view, core, 2), (yield crossed(picked(view, 1 - core, 2), "dp", CORE)))
-    going = jnp.stack([picked(sums, chip ^ first), picked(sums, chip ^ 3)])
-    kept = jnp.stack([picked(sums, chip), picked(sums, chip ^ second)])
-    sums = plus(kept, (yield crossed(going, "dp", FIRST)))
-    sums = plus(sums[0], (yield crossed(sums[1], "dp", SECOND)))
-    sums = yield from places_steps(sums)
-    own = by_bit(core, picked(sums, core), (yield crossed(picked(sums, 1 - core), "dp", CORE)))
-    return own.reshape(2 * half, columns).astype(WIDE)
+
+    def slots(core):
+        first, second = chip_masks(core)
+        away = jnp.arange(4) ^ chip
+        return jnp.where(away == 0, 0, jnp.where(away == second, 1, jnp.where(away == first, 2, 3)))
+
+    places = jnp.concatenate([core[None], slots(core), slots(1 - core)])
+    return places.astype(jnp.int32)
 
 
 def gather_small(values):
@@ -576,6 +704,8 @@
     length = local_len * groups
     enc_length = enc_local * groups
     hidden_width = ffn_in.shape[1]
+    slotted = shards == 8 and groups == 4
+    places = slot_places() if slotted else jnp.zeros((9,), jnp.int32)
 
     attn_q, attn_kv = attn_in[:, :width], interleaved(attn_in[:, width:])
     cross_q, cross_kv = cross_in[:, :width], interleaved(cross_in[:, width:])
@@ -617,12 +747,15 @@
     ffn_out = gather_rows(ffn_out)
     enc_gather = Chain(gather_steps(tied(encoded, slots[-1])))
 
-    token_all = jnp.concatenate(slots, axis=1).reshape(batch * length, width)
+    token_each = [
+        jnp.concatenate([slot[number] for slot in slots], axis=0) for number in range(batch)
+    ]
     token_flat = tokens.reshape(rows, width)
     queries = (product(token_flat, attn_q) + bias_all[0]).astype(LOW)
     queries = queries.reshape(batch, local_len, width)
-    keys_values = (product(token_all, attn_kv) + value_bias).astype(LOW)
-    keys_values = keys_values.reshape(batch, length, 2 * width)
+    keys_values = jnp.stack(
+        [(product(each, attn_kv) + value_bias).astype(LOW) for each in token_each]
+    )
 
     queries, keys_values = pumped((queries, keys_values), enc_gather)
     context, totals = attend_forward(queries, keys_values, ids)
@@ -642,117 +775,132 @@
     stage_vectors = jnp.stack(
         [bias_all[5], gain_all[1], bias_all[8], bias_all[6], gain_all[2], bias_all[9]]
     )
-    final, d_second_sum, d_cross_ctx, grad_cross_out, sums, d_bias_hidden, grad_in, grad_out = (
-        ffn_stage(
-            first,
-            cross_flat,
-            cotangent.reshape(rows, width),
-            stage_vectors,
-            bias_hidden[None],
-            early,
-            ffn_in,
-            ffn_out,
-        )
-    )
-    out_chain = Chain(offloaded_steps(grad_out))
-    in_chain = Chain(offloaded_steps(grad_in))
+    final, d_second_sum, d_cross_ctx, sums, d_bias_hidden, *grads = ffn_stage(
+        places,
+        first,
+        cross_flat,
+        cotangent.reshape(rows, width),
+        stage_vectors,
+        bias_hidden[None],
+        early,
+        ffn_in,
+        ffn_out,
+        slotted,
+    )
+    if slotted:
+        out_chain = Chain(slot_steps(*grads[2:]))
+        in_chain = Chain(slot_steps(*grads[:2]))
+    else:
+        out_chain = Chain(offloaded_steps(grads[1]))
+        in_chain = Chain(offloaded_steps(grads[0]))
+
+    def gradient_chain(groups, after, extra=()):
+        if slotted:
+            products = slotted_products(places, groups, extra)
+            products, after = lax.optimization_barrier((products, after))
+            return Chain(slot_steps(*products)), after
+        gradient, after = lax.optimization_barrier((plain_products(groups), after))
+        return Chain(offloaded_steps(gradient)), after
+
     d_cross_ctx = d_cross_ctx.reshape(cross_context.shape)
     d_cross_q, d_enc = attend_backward(
         cross_queries, enc_kv, enc_ids, cross_context, d_cross_ctx, cross_totals, 0, batch
     )
+    d_cross_q, d_enc = pumped((d_cross_q, d_enc), out_chain, in_chain)
     d_cross_q = d_cross_q.reshape(rows, width)
     d_enc = d_enc.reshape(-1, 2 * width)
+    d_encoded = right_transposed(d_enc, cross_kv)
+    d_encoded = d_encoded.reshape(batch, groups, enc_local, width).astype(LOW)
+    d_encoded, d_cross_q = lax.optimization_barrier((d_encoded, d_cross_q))
+    enc_chain = Chain(chunk_steps(d_encoded.transpose(1, 0, 2, 3)))
     d_first = d_second_sum + right_transposed(d_cross_q, cross_q)
     d_first_sum, d_gain_one, d_offset_one = norm_backward(first_sum, gain_all[0], d_first)
     d_attn = d_first_sum.astype(LOW)
     d_context = right_transposed(d_attn, attn_out).astype(LOW).reshape(context.shape)
-
-    def attention_backward(number, d_context):
+    d_context = pumped(d_context, out_chain, enc_chain)
+    left = (context_flat, first_low, enc_all, d_attn, d_cross_q, d_enc)
+    left, d_context = lax.optimization_barrier((left, d_context))
+    mid_chain, d_context = gradient_chain([[pair] for pair in zip(left[:3], left[3:])], d_context)
+
+    def token_chain(d_kv, after):
+        d_part = right_transposed(d_kv, attn_kv).astype(LOW)
+        d_part, after = lax.optimization_barrier((d_part, after))
+        d_part = d_part.reshape(groups, local_len, width)
+        return Chain(scatter_steps(list(d_part), groups)), after
+
+    d_query, d_key_value, token_chains = [], [], []
+    for number in range(batch):
         d_q, d_kv = attend_backward(
             queries, keys_values, ids, context, d_context, totals, number, 1
         )
-        d_part = right_transposed(d_kv[0], attn_kv).astype(LOW)
-        d_part = d_part.reshape(groups, local_len, width)
-        return d_q, d_kv, Chain(scatter_steps(list(d_part), groups))
-
-    d_queries, d_keys_values, token_chains = [], [], []
-    for number in range(batch):
-        d_q, d_kv, chain = attention_backward(number, d_context)
-        d_queries.append(d_q)
-        d_keys_values.append(d_kv)
+        pumps = (out_chain, in_chain, mid_chain, enc_chain)[: 2 if number else 4]
+        d_q, d_kv, d_context = pumped((d_q[0], d_kv[0], d_context), *pumps)
+        d_query.append(d_q)
+        if number == 0:
+            chain, (d_kv, d_context) = token_chain(d_kv, (d_kv, d_context))
+            token_chains.append(chain)
+        d_key_value.append(d_kv)
+    part = width // shards
+    hidden_rows = d_bias_hidden.reshape(shards, -1, part).transpose(1, 0, 2).reshape(-1, width)
+    vectors = gain_rows + bias_rows + hidden_rows.shape[0]
+    query_rows = column_total(jnp.concatenate(d_query, axis=0))[None]
+    singles = [d_gain_one[None], query_rows]
+    singles += [column_total(d_context.reshape(rows, width))[None], column_total(d_attn)[None]]
+    singles += [column_total(d_cross_q)[None], d_offset_one[None]]
+    extra = [(one, 0, at, 1) for one, at in zip(singles, (0, 3, 4, 5, 6, 10))]
+    extra += [(sums, row, at, 1) for row, at in enumerate((2, 12, 9, 1, 11, 8, 7))]
+    extra.append((hidden_rows, 0, gain_rows + bias_rows, hidden_rows.shape[0]))
+    query_rows = jnp.concatenate(d_query, axis=0)
+    query_rows, d_query, d_key_value = lax.optimization_barrier((query_rows, d_query, d_key_value))
+    attn_chain, (query_rows, d_key_value) = gradient_chain(
+        [
+            list(zip([tokens[number] for number in range(batch)], d_query)),
+            list(zip(token_each, d_key_value)),
+        ],
+        (query_rows, d_key_value),
+        extra,
+    )
+    query_rows, d_key_value = pumped(
+        (query_rows, d_key_value), mid_chain, out_chain, token_chains[0]
+    )
+    for d_kv in d_key_value[1:]:
+        chain, query_rows = token_chain(d_kv, query_rows)
         token_chains.append(chain)
-        if number == 0:
-            left = (context_flat, first_low, enc_all, d_attn, d_cross_q, d_enc)
-            left, d_kv = lax.optimization_barrier((left, d_kv))
-            middle = [left_transposed(one, two) for one, two in zip(left[:3], left[3:])]
-            middle.append(grad_cross_out)
-            middle = jnp.concatenate([part.astype(LOW) for part in middle], axis=1)
-            mid_chain = Chain(exchange_steps(middle))
-            d_encoded = right_transposed(left[5], cross_kv)
-            d_encoded = d_encoded.reshape(batch, groups, enc_local, width).astype(LOW)
-            enc_chain = Chain(chunk_steps(d_encoded.transpose(1, 0, 2, 3)))
-            d_context, middle, d_encoded = lax.optimization_barrier((d_context, middle, d_encoded))
-    d_query = jnp.concatenate(d_queries, axis=0).reshape(rows, width)
-    d_kv = jnp.concatenate(d_keys_values, axis=0).reshape(batch * length, 2 * width)
-    d_query, d_kv = pumped((d_query, d_kv), mid_chain, enc_chain, token_chains[0])
-    grad_attn = jnp.concatenate(
-        [
-            left_transposed(token_flat, d_query).astype(LOW),
-            left_transposed(token_all, d_kv).astype(LOW),
-        ],
-        axis=1,
-    )
-    attn_chain = Chain(exchange_steps(grad_attn))
-    d_tokens = d_first_sum + right_transposed(d_query, attn_q)
-    d_tokens = d_tokens.reshape(tokens.shape)
-    vector_grads = jnp.stack(
-        [
-            d_gain_one,
-            sums[3],
-            sums[0],
-            column_total(d_query),
-            column_total(d_context.reshape(rows, width)),
-            column_total(d_attn),
-            column_total(d_cross_q),
-            sums[6],
-            sums[5],
-            sums[2],
-            d_offset_one,
-            sums[4],
-            sums[1],
-        ]
-    )
-    vector_grads = jnp.concatenate([vector_grads, d_bias_hidden.reshape(-1, width)], axis=0)
-    small_chain = Chain(small_steps(vector_grads))
-    chains = [attn_chain, small_chain, mid_chain, out_chain, enc_chain, in_chain]
-    grad_attn, vector_grads, middle, grad_ffn_out, d_encoded, grad_ffn_in, *d_parts = finished(
-        *chains, *token_chains
-    )
-    d_tokens = jnp.stack([d_tokens[number] + part for number, part in enumerate(d_parts)])
-    grad_attn_in = jnp.concatenate(
-        [grad_attn[:, :width], deinterleaved(grad_attn[:, width:])], axis=1
-    )
-    grad_cross_in = jnp.concatenate(
-        [middle[:, width : 2 * width], deinterleaved(middle[:, 2 * width : 4 * width])], axis=1
-    )
-    flat_hidden = vector_grads[gain_rows + bias_rows :].reshape(-1)
-    part = width // shards
-    mine = lax.dynamic_slice_in_dim(vector_grads, owner * part, part, axis=1)
-    hidden_part = hidden_width // shards
-    grad_bias_ff = lax.dynamic_slice_in_dim(flat_hidden, owner * hidden_part, hidden_part)
+    query_rows = pumped(query_rows, attn_chain, in_chain)
+    d_tokens = d_first_sum + right_transposed(query_rows, attn_q)
+    timeline.token = d_tokens.reshape(tokens.shape)
+    early, late = token_chains[0], token_chains[-1]
+    early, late = token_chains[0], token_chains[-1]
+    ahead = [mid_chain, out_chain, attn_chain, early, in_chain, mid_chain, attn_chain, late]
+    ahead += [in_chain, mid_chain, attn_chain, mid_chain, attn_chain, late]
+    chains = [attn_chain, mid_chain, in_chain, out_chain, enc_chain]
+    grad_attn, middle, grad_in, grad_ffn_out, d_encoded, *d_parts = finished(
+        *chains, *token_chains, ahead=ahead
+    )
+    d_tokens, timeline.token = timeline.token, None
+    d_tokens = d_tokens + jnp.stack(d_parts)
+    if slotted:
+        mine = grad_attn[:, 3 * width :].T
+    else:
+        vector_grads = jnp.zeros((vectors, width), WIDE)
+        for value, first, at, count in extra:
+            vector_grads = vector_grads.at[at : at + count].set(value[first : first + count])
+        (vector_grads,) = finished(Chain(small_steps(vector_grads)))
+        mine = lax.dynamic_slice_in_dim(vector_grads, owner * part, part, axis=1)
+    grad_cross_out = grad_in[:, hidden_width:]
     return (
         final.reshape(batch, local_len, width),
         d_tokens,
         d_encoded,
-        grad_attn_in,
+        grad_attn[:, : 3 * width],
         middle[:, :width],
-        grad_cross_in,
-        middle[:, 4 * width :],
-        grad_ffn_in,
+        middle[:, width : 4 * width],
+        grad_cross_out,
+        grad_in[:, :hidden_width],
         grad_ffn_out,
         mine[:gain_rows],
         mine[gain_rows : gain_rows + bias_rows],
-        grad_bias_ff,
+        mine[gain_rows + bias_rows : vectors].reshape(-1),
     )
 
 

time: 506 us -> 448 us (0.89)
  starting transfers between devices: 108 us -> 66.5 us
  Pallas kernels: 103 us -> 122 us
  waiting for transfers between devices: 124 us -> 111 us
  matrix products: 57.5 us -> 45.4 us
  local copies, waits for them, and re-layouts: 43.3 us -> 32.8 us
    ppermute x46 -> x40, starting transfers between devices: 108 us -> 66.4 us  [the longest x37 59.3 us: moved(): return lax.ppermute(timeline.hold(value), axis_name, pairs)]
    ppermute x46 -> x40, waiting for transfers between devices: 116 us -> 84.7 us  [the longest x37 64.4 us: moved(): return lax.ppermute(timeline.hold(value), axis_name, pairs)]
    convert_element_type x4 -> x16, other arithmetic: 2.42 us -> 22.5 us  [the longest x12 21.1 us: summed(): return sum([part.astype(WIDE) for part in parts]).astype(LOW)]
    pallas_call x1 -> x3, Pallas kernels: 33.8 us -> 52.9 us  [the longest x1 33.2 us: ffn_stage(): pl.pallas_call(ffn_kernel, in_specs=[pl.BlockSpec(memory_space=pltpu.SMEM...]
    all_gather x3, waiting for transfers between devices: 7.44 us -> 25.1 us  [gather_rows(): return lax.all_gather(shard, 'dp', axis=0, tiled=True)]
    convert_element_type x17 -> x11, other arithmetic: 17.6 us -> 3.5 us  [plus(): return (left.astype(WIDE) + right.astype(WIDE)).astype(LOW)]
    dot_general x5 -> x0, matrix products: 12.9 us -> none  [left_transposed(): lax.dot_general(left, right, (((0,), (0,)), ((), ())), preferred_element_...]
    concatenate x7 -> x3, other arithmetic: 9.46 us -> 3.14 us  [the longest x2 2.48 us: local(): jnp.concatenate([slot[number] for slot in slots], axis=0)]
  transfers between devices with their start and end apart: 51 -> 43, of which waited for: 20 -> 13; matrix products, arithmetic and copies ran while one was open for 27% -> 25% of each run, Pallas kernels for 11% -> 18%
where the time goes in v3:
time: 448 us; the launch traced here: 442 us
  Pallas kernels  122 us (27%)
  waiting for transfers between devices  111 us (25%)
  starting transfers between devices  66.5 us (15%)
  other arithmetic  49.2 us (11%)
  matrix products  45.4 us (10%)
  local copies, waits for them, and re-layouts  32.8 us (7%)
  between operations  15.2 us (3%)
    ppermute x37, waiting for transfers between devices, moved(): return lax.ppermute(timeline.hold(value), axis_name, pairs)  64.4 us
    ppermute x37, starting transfers between devices, moved(): return lax.ppermute(timeline.hold(value), axis_name, pairs)  59.3 us
    pallas_call x3, Pallas kernels, attend_backward(): pl.pallas_call(backward_kernel, grid=(count, pairs), in_specs=[one, pl.Bl...  37.7 us
    pallas_call x1, Pallas kernels, ffn_stage(): pl.pallas_call(ffn_kernel, in_specs=[pl.BlockSpec(memory_space=pltpu.SMEM...  33.2 us
    pallas_call x2, Pallas kernels, attend_forward(): pl.pallas_call(forward_kernel, grid=(batch, pairs), in_specs=[one, pl.Blo...  31.4 us
    all_gather x3, waiting for transfers between devices, gather_rows(): return lax.all_gather(shard, 'dp', axis=0, tiled=True)  25.1 us
    dot_general x6, matrix products, product(): return jnp.dot(left, right, preferred_element_type=WIDE)  25 us
    convert_element_type x12, other arithmetic, summed(): return sum([part.astype(WIDE) for part in parts]).astype(LOW)  21.1 us
  transfers between devices with their start and end apart: 43, of which 13 were waited for; matrix products, arithmetic and copies ran while one was open for 25% of the time, Pallas kernels for 18%

profile of v3, /device:TPU:0, one launch (start us, length us, event | category | flops | bytes accessed | tf_op | source)
XLA Modules:
  0.0 441.6 jit_solution(7659518116247059224)
XLA Ops:
  13.2 5.0 %collective-permute-start = (bf16[2,256,768]{2,1,0:T(8,128)(2,1)S(1)}, bf16[2,256,768]{2,1,0:T(8,128)(2,1)S(1)}, u32[]{:S(2)}, u32[]{:S(2)}) collective-permute-start(bf16[2,256,768]{2,1,0:T(8,128)(2,1)S(1)} %copy-done.3), channel_id=1, source_target_pairs={{0,1},{1,2},{2,3},{4,5},{5,6},{6,7},{8,9},{9,10},{10,11},{12,13},{... | collective-permute-start | bytes 2359304 | tf_op jit(solution)/shard_map/ppermute | solution.py:475
  25.7 10.4 %collective-permute-done = bf16[2,256,768]{2,1,0:T(8,128)(2,1)S(1)} collective-permute-done((bf16[2,256,768]{2,1,0:T(8,128)(2,1)S(1)}, bf16[2,256,768]{2,1,0:T(8,128)(2,1)S(1)}, u32[]{:S(2)}, u32[]{:S(2)}) %collective-permute-start) | collective-permute-done | bytes 786464 | tf_op jit(solution)/shard_map/ppermute | solution.py:475
  41.8 10.0 %collective-permute-done.2 = bf16[2,256,768]{2,1,0:T(8,128)(2,1)S(1)} collective-permute-done((bf16[2,256,768]{2,1,0:T(8,128)(2,1)S(1)}, bf16[2,256,768]{2,1,0:T(8,128)(2,1)S(1)}, u32[]{:S(2)}, u32[]{:S(2)}) %collective-permute-start.2) | collective-permute-done | bytes 786464 | tf_op jit(solution)/shard_map/ppermute | solution.py:472
  51.8 22.1 %all-gather.4.cloned.1.call-done.early_ref = bf16[768,6144]{1,0:T(8,128)(2,1)} async-done(((bf16[96,6144]{1,0:T(8,128)(2,1)}), bf16[768,6144]{1,0:T(8,128)(2,1)}) %all-gather.4.cloned.1.call-update) | async-done | bytes 9437200 | tf_op jit(solution)/shard_map/all_gather | solution.py:542
  84.7 6.5 %fusion = bf16[1,1024,1536]{2,1,0:T(8,128)(2,1)S(1)} fusion(f32[1536]{0:T(1024)S(1)} %copy-done.47, bf16[768,6144]{1,0:T(8,128)(2,1)} %all-gather.4.cloned.1.call-done.early_ref, bf16[256,768]{1,0:T(8,128)(2,1)S(1)} %get-tuple-element.368, bf16[256,768]{1,0:T(8,128)(2,1)S(1)} %get-tuple-element.389, bf16[256,768]{1,0:T(8,128)(2,1)S(1)} %get-tuple-element.364, ...), kind=kOutput, calls=%fused_computation.4 | convolution fusion | flops 2425356288 | bytes 7084032 | tf_op jit(solution)/shard_map/dot_general | solution.py:17
  91.2 6.0 %fusion.1 = bf16[1,1024,1536]{2,1,0:T(8,128)(2,1)S(1)} fusion(f32[1536]{0:T(1024)S(1)} %copy-done.47, bf16[768,6144]{1,0:T(8,128)(2,1)} %all-gather.4.cloned.1.call-done.early_ref, bf16[256,768]{1,0:T(8,128)(2,1)S(1)} %get-tuple-element.369, bf16[256,768]{1,0:T(8,128)(2,1)S(1)} %get-tuple-element.388, bf16[256,768]{1,0:T(8,128)(2,1)S(1)} %get-tuple-element.365, ...), kind=kOutput, calls=%fused_computation.5 | convolution fusion | flops 2425356288 | bytes 7084032 | tf_op jit(solution)/shard_map/dot_general | solution.py:17
  97.2 3.3 pad_maximum_fusion.kv_ref
  107.3 20.8 %attend_forward.2 = (bf16[2,256,768]{2,1,0:T(8,128)(2,1)}, f32[2,6,8,512]{3,2,1,0:T(8,128)}) custom-call(bf16[2,256,768]{2,1,0:T(8,128)(2,1)} %bitcast.207, bf16[2,1024,1536]{2,1,0:T(8,128)(2,1)} %pad_maximum_fusion.kv_ref, s32[2,256,1]{2,1,0:T(8,128)} %copy.43.qid_ref, s32[2,1,1024]{2,1,0:T(1,128)} %broadcast_select_fusion.1.kid_ref), custom_call_target="tpu_custom_call" | custom-call | flops 12582912000 | bytes 12582912 | tf_op jit(solution)/shard_map/attend_forward/pallas_call | solution.py:113
  137.8 4.3 fusion.2
  142.0 10.6 %attend_forward.3 = (bf16[2,256,768]{2,1,0:T(8,128)(2,1)}, f32[2,6,8,512]{3,2,1,0:T(8,128)}) custom-call(bf16[2,256,768]{2,1,0:T(8,128)(2,1)} %bitcast.212, bf16[2,256,1536]{2,1,0:T(8,128)(2,1)} %bitcast.202, s32[2,256,1]{2,1,0:T(8,128)} %broadcast_in_dim_broadcast_in_dim.11.qid_ref, s32[2,1,256]{2,1,0:T(1,128)} %broadcast_in_dim_broadcast_in_dim.8.kid_ref), custom_call_target="tpu_custom_call" | custom-call | flops 3145728000 | bytes 3145728 | tf_op jit(solution)/shard_map/attend_forward/pallas_call | solution.py:113
  155.7 33.2 %ffn_stage.1 = (bf16[512,768]{1,0:T(8,128)(2,1)}, f32[512,768]{1,0:T(8,128)}, bf16[512,768]{1,0:T(8,128)(2,1)}, f32[8,768]{1,0:T(8,128)}, f32[1,3072]{1,0:T(1,12...) custom-call(s32[9]{0:T(128)} %pad_add_fusion.place_ref, ...), custom_call_target="tpu_custom_call" | custom-call | flops 19327352832 | bytes 28311552 | tf_op jit(solution)/shard_map/ffn_stage/pallas_call | solution.py:341
  192.1 12.5 %attend_backward.3 = (bf16[2,256,768]{2,1,0:T(8,128)(2,1)}, bf16[2,256,1536]{2,1,0:T(8,128)(2,1)}) custom-call(bf16[2,256,768]{2,1,0:T(8,128)(2,1)} %bitcast.213, bf16[2,256,1536]{2,1,0:T(8,128)(2,1)} %bitcast.203, s32[2,1,256]{2,1,0:T(1,128)} %broadcast_in_dim_broadcast_in_dim.10.qid_ref, s32[2,256,1]{2,1,0:T(8,128)} %broadcast_in_dim_broadcast_in_dim.9.kid_ref, ...), custom_call_target="tpu_custom_call" | custom-call | flops 3145728000 | bytes 3145728 | tf_op jit(solution)/shard_map/attend_backward/pallas_call | solution.py:140
  218.5 3.3 convolution_convert_fusion.2
  221.8 3.5 collective-permute-done.11
  226.3 7.3 %slotted_products.2 = (bf16[4,96,3072]{2,1,0:T(8,128)(2,1)}, bf16[4,96,3072]{2,1,0:T(8,128)(2,1)}) custom-call(s32[9]{0:T(128)} %pad_add_fusion.place_ref, bf16[512,768]{1,0:T(8,128)(2,1)} %bitcast.210, bf16[512,768]{1,0:T(8,128)(2,1)} %copy-done.36, bf16[512,768]{1,0:T(8,128)(2,1)} %copy-done.34, bf16[512,768]{1,0:T(8,128)(2,1)} %bitcast.167, ...), custom_call_target="tpu_custom_call" | custom-call | flops 2415919104 | bytes 10223616 | tf_op jit(solution)/shard_map/slotted_products/pallas_call | solution.py:438
  233.7 3.4 add_convert_fusion.2
  252.2 12.6 %attend_backward.4 = (bf16[1,256,768]{2,1,0:T(8,128)(2,1)}, bf16[1,1024,1536]{2,1,0:T(8,128)(2,1)}) custom-call(bf16[2,256,768]{2,1,0:T(8,128)(2,1)} %bitcast.208, bf16[2,1024,1536]{2,1,0:T(8,128)(2,1)} %pad_maximum_fusion.kv_ref, s32[2,1,256]{2,1,0:T(1,128)} %broadcast_in_dim.118.qid_ref, s32[2,1024,1]{2,1,0:T(8,128)} %broadcast_select_fusion.kid_ref, ...), custom_call_target="tpu_custom_call" | custom-call | flops 6291456000 | bytes 6291456 | tf_op jit(solution)/shard_map/attend_backward/pallas_call | solution.py:140
  270.0 3.6 collective-permute-start.16
  273.5 4.3 convolution_convert_fusion.1
  285.7 12.6 %attend_backward.5 = (bf16[1,256,768]{2,1,0:T(8,128)(2,1)}, bf16[1,1024,1536]{2,1,0:T(8,128)(2,1)}) custom-call(bf16[2,256,768]{2,1,0:T(8,128)(2,1)} %bitcast.209, bf16[2,1024,1536]{2,1,0:T(8,128)(2,1)} %pad_maximum_fusion.kv_ref, s32[2,1,256]{2,1,0:T(1,128)} %broadcast_in_dim.118.qid_ref, s32[2,1024,1]{2,1,0:T(8,128)} %broadcast_select_fusion.kid_ref, ...), custom_call_target="tpu_custom_call" | custom-call | flops 6291456000 | bytes 6291456 | tf_op jit(solution)/shard_map/attend_backward/pallas_call | solution.py:140
  303.1 12.5 %slotted_products.3 = (bf16[4,96,2432]{2,1,0:T(8,128)(2,1)}, bf16[4,96,2432]{2,1,0:T(8,128)(2,1)}) custom-call(s32[9]{0:T(128)} %pad_add_fusion.place_ref, bf16[256,768]{1,0:T(8,128)(2,1)} %get-tuple-element.359.refs_0_, bf16[256,768]{1,0:T(8,128)(2,1)} %bitcast.172, bf16[256,768]{1,0:T(8,128)(2,1)} %get-tuple-element.358.refs_2_, ...), custom_call_target="tpu_custom_call" | custom-call | flops 5435817984 | bytes 14745600 | tf_op jit(solution)/shard_map/slotted_products/pallas_call | solution.py:438
  315.6 5.3 %collective-permute-start.23 = (bf16[96,3840]{1,0:T(8,128)(2,1)S(1)}, bf16[96,3840]{1,0:T(8,128)(2,1)S(1)}, u32[]{:S(2)}, u32[]{:S(2)}) collective-permute-start(bf16[96,3840]{1,0:T(8,128)(2,1)S(1)} %fusion.11), channel_id=1, source_target_pairs={{0,1},{3,2},{4,5},{7,6},{8,9},{11,10},{12,13},{15,14},{16,17},{19,... | collective-permute-start | bytes 2211848 | tf_op jit(solution)/shard_map/ppermute | solution.py:509
  325.3 4.3 convolution_convert_fusion
  332.1 3.5 collective-permute-done.23
  347.7 10.9 %collective-permute-done.26 = bf16[2,96,2432]{2,1,0:T(8,128)(2,1)S(1)} collective-permute-done((bf16[2,96,2432]{2,1,0:T(8,128)(2,1)S(1)}, bf16[2,96,2432]{2,1,0:T(8,128)(2,1)S(1)}, u32[]{:S(2)}, u32[]{:S(2)}) %collective-permute-start.26) | collective-permute-done | bytes 933920 | tf_op jit(solution)/shard_map/ppermute | solution.py:509
  358.6 5.0 %collective-permute-start.29 = (bf16[96,3072]{1,0:T(8,128)(2,1)S(1)}, bf16[96,3072]{1,0:T(8,128)(2,1)S(1)}, u32[]{:S(2)}, u32[]{:S(2)}) collective-permute-start(bf16[96,3072]{1,0:T(8,128)(2,1)S(1)} %fusion.15), channel_id=1, source_target_pairs={{0,1},{3,2},{4,5},{7,6},{8,9},{11,10},{12,13},{15,14},{16,17},{19,... | collective-permute-start | bytes 1769480 | tf_op jit(solution)/shard_map/ppermute | solution.py:509
  364.1 8.3 %collective-permute-done.29 = bf16[96,3072]{1,0:T(8,128)(2,1)S(1)} collective-permute-done((bf16[96,3072]{1,0:T(8,128)(2,1)S(1)}, bf16[96,3072]{1,0:T(8,128)(2,1)S(1)}, u32[]{:S(2)}, u32[]{:S(2)}) %collective-permute-start.29) | collective-permute-done | bytes 589856 | tf_op jit(solution)/shard_map/ppermute | solution.py:509
  376.5 4.5 %collective-permute-done.30 = bf16[96,2432]{1,0:T(8,128)(2,1)S(1)} collective-permute-done((bf16[96,2432]{1,0:T(8,128)(2,1)S(1)}, bf16[96,2432]{1,0:T(8,128)(2,1)S(1)}, u32[]{:S(2)}, u32[]{:S(2)}) %collective-permute-start.30) | collective-permute-done | bytes 466976 | tf_op jit(solution)/shard_map/ppermute | solution.py:509
  381.4 8.6 %collective-permute-start.35 = (bf16[96,2432]{1,0:T(8,128)(2,1)S(1)}, bf16[96,2432]{1,0:T(8,128)(2,1)S(1)}, u32[]{:S(2)}, u32[]{:S(2)}) collective-permute-start(bf16[96,2432]{1,0:T(8,128)(2,1)S(1)} %fusion.24), channel_id=1, source_target_pairs={{0,1},{3,2},{4,5},{7,6},{8,9},{11,10},{12,13},{15,14},{16,17},{19,... | collective-permute-start | bytes 1400840 | tf_op jit(solution)/shard_map/ppermute | solution.py:509
  391.3 8.0 %collective-permute-done.33 = bf16[96,3840]{1,0:T(8,128)(2,1)S(1)} collective-permute-done((bf16[96,3840]{1,0:T(8,128)(2,1)S(1)}, bf16[96,3840]{1,0:T(8,128)(2,1)S(1)}, u32[]{:S(2)}, u32[]{:S(2)}) %collective-permute-start.33) | collective-permute-done | bytes 737312 | tf_op jit(solution)/shard_map/ppermute | solution.py:509
  403.6 14.4 %collective-permute-done.36 = bf16[96,3072]{1,0:T(8,128)(2,1)S(1)} collective-permute-done((bf16[96,3072]{1,0:T(8,128)(2,1)S(1)}, bf16[96,3072]{1,0:T(8,128)(2,1)S(1)}, u32[]{:S(2)}, u32[]{:S(2)}) %collective-permute-start.36) | collective-permute-done | bytes 589856 | tf_op jit(solution)/shard_map/ppermute | solution.py:509
  421.4 9.0 %collective-permute-done.39 = bf16[96,2432]{1,0:T(8,128)(2,1)S(1)} collective-permute-done((bf16[96,2432]{1,0:T(8,128)(2,1)S(1)}, bf16[96,2432]{1,0:T(8,128)(2,1)S(1)}, u32[]{:S(2)}, u32[]{:S(2)}) %collective-permute-start.39) | collective-permute-done | bytes 466976 | tf_op jit(solution)/shard_map/ppermute | solution.py:509
  (344 shorter events, 137.1 us)
Async XLA Ops:
  7.2 66.7 %all-gather.4.cloned.1.call-start = ((), (), s32[]{:S(2)}) async-start(), calls=%async_computation | async-start | bytes 10616832 | tf_op jit(solution)/shard_map/all_gather | solution.py:542
  12.4 140.3 %all-gather.6.cloned.1.call-start = ((), (), s32[]{:S(2)}) async-start(), calls=%async_computation.1 | async-start | bytes 5308416 | tf_op jit(solution)/shard_map/all_gather | solution.py:542
  13.1 142.5 %all-gather.8.cloned.1.call-start = ((), (), s32[]{:S(2)}) async-start(), calls=%async_computation.2 | async-start | bytes 5308416 | tf_op jit(solution)/shard_map/all_gather | solution.py:542
  13.2 22.9 %collective-permute-start = (bf16[2,256,768]{2,1,0:T(8,128)(2,1)S(1)}, bf16[2,256,768]{2,1,0:T(8,128)(2,1)S(1)}, u32[]{:S(2)}, u32[]{:S(2)}) collective-permute-start(bf16[2,256,768]{2,1,0:T(8,128)(2,1)S(1)} %copy-done.3), channel_id=1, source_target_pairs={{0,1},{1,2},{2,3},{4,5},{5,6},{6,7},{8,9},{9,10},{10,11},{12,13},{... | collective-permute-start | bytes 2359304 | tf_op jit(solution)/shard_map/ppermute | solution.py:475
  18.2 33.6 %collective-permute-start.2 = (bf16[2,256,768]{2,1,0:T(8,128)(2,1)S(1)}, bf16[2,256,768]{2,1,0:T(8,128)(2,1)S(1)}, u32[]{:S(2)}, u32[]{:S(2)}) collective-permute-start(bf16[2,256,768]{2,1,0:T(8,128)(2,1)S(1)} %copy-done.3), channel_id=1, source_target_pairs={{0,3},{1,0},{2,1},{3,2},{4,7},{5,4},{6,5},{7,6},{8,11},{9,8},{10,9... | collective-permute-start | bytes 2359304 | tf_op jit(solution)/shard_map/ppermute | solution.py:472
  36.0 15.8 %collective-permute-start.1 = (bf16[2,256,768]{2,1,0:T(8,128)(2,1)S(1)}, bf16[2,256,768]{2,1,0:T(8,128)(2,1)S(1)}, u32[]{:S(2)}, u32[]{:S(2)}) collective-permute-start(bf16[2,256,768]{2,1,0:T(8,128)(2,1)S(1)} %collective-permute-done), channel_id=1, source_target_pairs={{1,2},{2,3},{5,6},{6,7},{9,10},{10,11},{13,14},{14,15},{17,18},{18... | collective-permute-start | bytes 2359304 | tf_op jit(solution)/shard_map/ppermute | solution.py:475
  76.7 26.8 %collective-permute-start.6 = (bf16[2,64,768]{2,1,0:T(8,128)(2,1)}, bf16[2,64,768]{2,1,0:T(8,128)(2,1)}, u32[]{:S(2)}, u32[]{:S(2)}) collective-permute-start(bf16[2,64,768]{2,1,0:T(8,128)(2,1)} %param.15), channel_id=1, source_target_pairs={{0,1},{1,0},{2,3},{3,2},{4,5},{5,4},{6,7},{7,6},{8,9},{9,8},{10,11... | collective-permute-start | bytes 589832 | tf_op jit(solution)/shard_map/ppermute | solution.py:509
  104.8 24.6 %collective-permute-start.7 = (bf16[2,2,64,768]{3,2,1,0:T(8,128)(2,1)S(1)}, bf16[2,2,64,768]{3,2,1,0:T(8,128)(2,1)S(1)}, u32[]{:S(2)}, u32[]{:S(2)}) collective-permute-start(bf16[2,2,64,768]{3,2,1,0:T(8,128)(2,1)S(1)} %maximum_select_fusion.1), channel_id=1, source_target_pairs={{0,2},{1,3},{2,0},{3,1},{4,6},{5,7},{6,4},{7,5},{8,10},{9,11},{10,... | collective-permute-start | bytes 1179656 | tf_op jit(solution)/shard_map/ppermute | solution.py:509
  188.9 15.8 %collective-permute-start.9 = (bf16[4,96,3840]{2,1,0:T(8,128)(2,1)}, bf16[4,96,3840]{2,1,0:T(8,128)(2,1)}, u32[]{:S(2)}, u32[]{:S(2)}) collective-permute-start(bf16[4,96,3840]{2,1,0:T(8,128)(2,1)} %get-tuple-element.195), channel_id=1, source_target_pairs={{0,4},{4,0},{8,12},{12,8},{16,20},{20,16},{24,28},{28,24},{1,5},{5... | collective-permute-start | bytes 8847368 | tf_op jit(solution)/shard_map/ppermute | solution.py:509
  206.7 18.6 %collective-permute-start.10 = (bf16[2,384,768]{2,1,0:T(8,128)(2,1)S(1)}, bf16[2,384,768]{2,1,0:T(8,128)(2,1)S(1)}, u32[]{:S(2)}, u32[]{:S(2)}) collective-permute-start(bf16[2,384,768]{2,1,0:T(8,128)(2,1)S(1)} %add_convert_fusion.4), channel_id=1, source_target_pairs={{0,8},{4,20},{8,0},{12,28},{16,24},{20,4},{24,16},{28,12},{1,9},{5... | collective-permute-start | bytes 3538952 | tf_op jit(solution)/shard_map/ppermute | solution.py:509
  233.6 31.2 %collective-permute-start.14 = (bf16[4,96,3072]{2,1,0:T(8,128)(2,1)}, bf16[4,96,3072]{2,1,0:T(8,128)(2,1)}, u32[]{:S(2)}, u32[]{:S(2)}) collective-permute-start(bf16[4,96,3072]{2,1,0:T(8,128)(2,1)} %get-tuple-element.221), channel_id=1, source_target_pairs={{0,4},{4,0},{8,12},{12,8},{16,20},{20,16},{24,28},{28,24},{1,5},{5... | collective-permute-start | bytes 7077896 | tf_op jit(solution)/shard_map/ppermute | solution.py:509
  237.1 27.7 %collective-permute-start.13 = (bf16[2,96,3840]{2,1,0:T(8,128)(2,1)}, bf16[2,96,3840]{2,1,0:T(8,128)(2,1)}, u32[]{:S(2)}, u32[]{:S(2)}) collective-permute-start(bf16[2,96,3840]{2,1,0:T(8,128)(2,1)} %add_convert_fusion.2), channel_id=1, source_target_pairs={{0,8},{4,20},{8,0},{12,28},{16,24},{20,4},{24,16},{28,12},{1,9},{5... | collective-permute-start | bytes 4423688 | tf_op jit(solution)/shard_map/ppermute | solution.py:509
  246.6 18.2 %collective-permute-start.15 = (bf16[2,64,768]{2,1,0:T(8,128)(2,1)S(1)}, bf16[2,64,768]{2,1,0:T(8,128)(2,1)S(1)}, u32[]{:S(2)}, u32[]{:S(2)}) collective-permute-start(bf16[2,64,768]{2,1,0:T(8,128)(2,1)S(1)} %dynamic-slice_bitcast_fusion), channel_id=1, source_target_pairs={{0,2},{1,3},{2,0},{3,1},{4,6},{5,7},{6,4},{7,5},{8,10},{9,11},{10,... | collective-permute-start | bytes 589832 | tf_op jit(solution)/shard_map/ppermute | solution.py:509
  267.8 30.6 %collective-permute-start.17 = (bf16[96,3840]{1,0:T(8,128)(2,1)}, bf16[96,3840]{1,0:T(8,128)(2,1)}, u32[]{:S(2)}, u32[]{:S(2)}) collective-permute-start(bf16[96,3840]{1,0:T(8,128)(2,1)} %fusion.26), channel_id=1, source_target_pairs={{0,16},{4,12},{8,24},{12,4},{16,0},{20,28},{24,8},{28,20},{1,17},{... | collective-permute-start | bytes 2211848 | tf_op jit(solution)/shard_map/ppermute | solution.py:509
  270.0 28.4 %collective-permute-start.16 = (bf16[384,768]{1,0:T(8,128)(2,1)S(1)}, bf16[384,768]{1,0:T(8,128)(2,1)S(1)}, u32[]{:S(2)}, u32[]{:S(2)}) collective-permute-start(bf16[384,768]{1,0:T(8,128)(2,1)S(1)} %fusion.16), channel_id=1, source_target_pairs={{0,1},{3,2},{4,5},{7,6},{8,9},{11,10},{12,13},{15,14},{16,17},{19,... | collective-permute-start | bytes 1769480 | tf_op jit(solution)/shard_map/ppermute | solution.py:509
  281.0 40.0 %collective-permute-start.18 = (bf16[2,96,3072]{2,1,0:T(8,128)(2,1)}, bf16[2,96,3072]{2,1,0:T(8,128)(2,1)}, u32[]{:S(2)}, u32[]{:S(2)}) collective-permute-start(bf16[2,96,3072]{2,1,0:T(8,128)(2,1)} %add_convert_fusion.3), channel_id=1, source_target_pairs={{0,8},{4,20},{8,0},{12,28},{16,24},{20,4},{24,16},{28,12},{1,9},{5... | collective-permute-start | bytes 3538952 | tf_op jit(solution)/shard_map/ppermute | solution.py:509
  283.2 37.7 %collective-permute-start.20 = (bf16[256,768]{1,0:T(8,128)(2,1)}, bf16[256,768]{1,0:T(8,128)(2,1)}, u32[]{:S(2)}, u32[]{:S(2)}) collective-permute-start(bf16[256,768]{1,0:T(8,128)(2,1)} %get-tuple-element.357), channel_id=1, source_target_pairs={{3,2},{2,1},{7,6},{6,5},{11,10},{10,9},{15,14},{14,13},{19,18},{18... | collective-permute-start | bytes 1179656 | tf_op jit(solution)/shard_map/ppermute | solution.py:509
  284.9 36.1 %collective-permute-start.21 = (bf16[256,768]{1,0:T(8,128)(2,1)}, bf16[256,768]{1,0:T(8,128)(2,1)}, u32[]{:S(2)}, u32[]{:S(2)}) collective-permute-start(bf16[256,768]{1,0:T(8,128)(2,1)} %get-tuple-element.356), channel_id=1, source_target_pairs={{0,1},{1,2},{2,3},{3,0},{4,5},{5,6},{6,7},{7,4},{8,9},{9,10},{10,1... | collective-permute-start | bytes 1179656 | tf_op jit(solution)/shard_map/ppermute | solution.py:509
  298.5 22.5 %collective-permute-start.19 = (bf16[384,768]{1,0:T(8,128)(2,1)S(1)}, bf16[384,768]{1,0:T(8,128)(2,1)S(1)}, u32[]{:S(2)}, u32[]{:S(2)}) collective-permute-start(bf16[384,768]{1,0:T(8,128)(2,1)S(1)} %add_convert_fusion.15), channel_id=1, source_target_pairs={{1,2},{2,1},{5,6},{6,5},{9,10},{10,9},{13,14},{14,13},{17,18},{18,... | collective-permute-start | bytes 1769480 | tf_op jit(solution)/shard_map/ppermute | solution.py:509
  315.6 20.0 %collective-permute-start.23 = (bf16[96,3840]{1,0:T(8,128)(2,1)S(1)}, bf16[96,3840]{1,0:T(8,128)(2,1)S(1)}, u32[]{:S(2)}, u32[]{:S(2)}) collective-permute-start(bf16[96,3840]{1,0:T(8,128)(2,1)S(1)} %fusion.11), channel_id=1, source_target_pairs={{0,1},{3,2},{4,5},{7,6},{8,9},{11,10},{12,13},{15,14},{16,17},{19,... | collective-permute-start | bytes 2211848 | tf_op jit(solution)/shard_map/ppermute | solution.py:509
  321.2 23.4 %collective-permute-start.25 = (bf16[384,768]{1,0:T(8,128)(2,1)S(1)}, bf16[384,768]{1,0:T(8,128)(2,1)S(1)}, u32[]{:S(2)}, u32[]{:S(2)}) collective-permute-start(bf16[384,768]{1,0:T(8,128)(2,1)S(1)} %add_convert_fusion.13), channel_id=1, source_target_pairs={{1,0},{2,3},{5,4},{6,7},{9,8},{10,11},{13,12},{14,15},{17,16},{18,... | collective-permute-start | bytes 1769480 | tf_op jit(solution)/shard_map/ppermute | solution.py:509
  324.4 18.3 %collective-permute-start.24 = (bf16[96,3072]{1,0:T(8,128)(2,1)S(1)}, bf16[96,3072]{1,0:T(8,128)(2,1)S(1)}, u32[]{:S(2)}, u32[]{:S(2)}) collective-permute-start(bf16[96,3072]{1,0:T(8,128)(2,1)S(1)} %fusion.28), channel_id=1, source_target_pairs={{0,16},{4,12},{8,24},{12,4},{16,0},{20,28},{24,8},{28,20},{1,17},{... | collective-permute-start | bytes 1769480 | tf_op jit(solution)/shard_map/ppermute | solution.py:509
  330.7 33.1 %collective-permute-start.27 = (bf16[256,768]{1,0:T(8,128)(2,1)S(1)}, bf16[256,768]{1,0:T(8,128)(2,1)S(1)}, u32[]{:S(2)}, u32[]{:S(2)}) collective-permute-start(bf16[256,768]{1,0:T(8,128)(2,1)S(1)} %add_convert_fusion.21), channel_id=1, source_target_pairs={{1,0},{2,1},{3,2},{5,4},{6,5},{7,6},{9,8},{10,9},{11,10},{13,12},{... | collective-permute-start | bytes 1179656 | tf_op jit(solution)/shard_map/ppermute | solution.py:509
  335.6 45.7 %collective-permute-start.31 = (bf16[256,768]{1,0:T(8,128)(2,1)S(1)}, bf16[256,768]{1,0:T(8,128)(2,1)S(1)}, u32[]{:S(2)}, u32[]{:S(2)}) collective-permute-start(bf16[256,768]{1,0:T(8,128)(2,1)S(1)} %get-tuple-element.355), channel_id=1, source_target_pairs={{3,2},{2,1},{7,6},{6,5},{11,10},{10,9},{15,14},{14,13},{19,18},{18... | collective-permute-start | bytes 1179656 | tf_op jit(solution)/shard_map/ppermute | solution.py:509
  336.3 45.0 %collective-permute-start.32 = (bf16[256,768]{1,0:T(8,128)(2,1)S(1)}, bf16[256,768]{1,0:T(8,128)(2,1)S(1)}, u32[]{:S(2)}, u32[]{:S(2)}) collective-permute-start(bf16[256,768]{1,0:T(8,128)(2,1)S(1)} %get-tuple-element.354), channel_id=1, source_target_pairs={{0,1},{1,2},{2,3},{3,0},{4,5},{5,6},{6,7},{7,4},{8,9},{9,10},{10,1... | collective-permute-start | bytes 1179656 | tf_op jit(solution)/shard_map/ppermute | solution.py:509
  345.9 18.0 %collective-permute-start.28 = (bf16[96,3840]{1,0:T(8,128)(2,1)S(1)}, bf16[96,3840]{1,0:T(8,128)(2,1)S(1)}, u32[]{:S(2)}, u32[]{:S(2)}) collective-permute-start(bf16[96,3840]{1,0:T(8,128)(2,1)S(1)} %add_convert_fusion.9), channel_id=1, source_target_pairs={{1,2},{2,1},{5,6},{6,5},{9,10},{10,9},{13,14},{14,13},{17,18},{18,... | collective-permute-start | bytes 2211848 | tf_op jit(solution)/shard_map/ppermute | solution.py:509
  373.3 26.0 %collective-permute-start.33 = (bf16[96,3840]{1,0:T(8,128)(2,1)S(1)}, bf16[96,3840]{1,0:T(8,128)(2,1)S(1)}, u32[]{:S(2)}, u32[]{:S(2)}) collective-permute-start(bf16[96,3840]{1,0:T(8,128)(2,1)S(1)} %add_convert_fusion.8), channel_id=1, source_target_pairs={{1,0},{2,3},{5,4},{6,7},{9,8},{10,11},{13,12},{14,15},{17,16},{18,... | collective-permute-start | bytes 2211848 | tf_op jit(solution)/shard_map/ppermute | solution.py:509
  374.6 24.7 %collective-permute-start.34 = (bf16[96,3072]{1,0:T(8,128)(2,1)S(1)}, bf16[96,3072]{1,0:T(8,128)(2,1)S(1)}, u32[]{:S(2)}, u32[]{:S(2)}) collective-permute-start(bf16[96,3072]{1,0:T(8,128)(2,1)S(1)} %add_convert_fusion.12), channel_id=1, source_target_pairs={{1,2},{2,1},{5,6},{6,5},{9,10},{10,9},{13,14},{14,13},{17,18},{18,... | collective-permute-start | bytes 1769480 | tf_op jit(solution)/shard_map/ppermute | solution.py:509
  381.4 19.5 %collective-permute-start.35 = (bf16[96,2432]{1,0:T(8,128)(2,1)S(1)}, bf16[96,2432]{1,0:T(8,128)(2,1)S(1)}, u32[]{:S(2)}, u32[]{:S(2)}) collective-permute-start(bf16[96,2432]{1,0:T(8,128)(2,1)S(1)} %fusion.24), channel_id=1, source_target_pairs={{0,1},{3,2},{4,5},{7,6},{8,9},{11,10},{12,13},{15,14},{16,17},{19,... | collective-permute-start | bytes 1400840 | tf_op jit(solution)/shard_map/ppermute | solution.py:509
  390.0 31.2 %collective-permute-start.38 = (bf16[256,768]{1,0:T(8,128)(2,1)S(1)}, bf16[256,768]{1,0:T(8,128)(2,1)S(1)}, u32[]{:S(2)}, u32[]{:S(2)}) collective-permute-start(bf16[256,768]{1,0:T(8,128)(2,1)S(1)} %add_convert_fusion.20), channel_id=1, source_target_pairs={{1,0},{2,1},{3,2},{5,4},{6,5},{7,6},{9,8},{10,9},{11,10},{13,12},{... | collective-permute-start | bytes 1179656 | tf_op jit(solution)/shard_map/ppermute | solution.py:509
  399.5 18.5 %collective-permute-start.36 = (bf16[96,3072]{1,0:T(8,128)(2,1)S(1)}, bf16[96,3072]{1,0:T(8,128)(2,1)S(1)}, u32[]{:S(2)}, u32[]{:S(2)}) collective-permute-start(bf16[96,3072]{1,0:T(8,128)(2,1)S(1)} %add_convert_fusion.11), channel_id=1, source_target_pairs={{1,0},{2,3},{5,4},{6,7},{9,8},{10,11},{13,12},{14,15},{17,16},{18,... | collective-permute-start | bytes 1769480 | tf_op jit(solution)/shard_map/ppermute | solution.py:509
  401.0 17.1 %collective-permute-start.37 = (bf16[96,2432]{1,0:T(8,128)(2,1)S(1)}, bf16[96,2432]{1,0:T(8,128)(2,1)S(1)}, u32[]{:S(2)}, u32[]{:S(2)}) collective-permute-start(bf16[96,2432]{1,0:T(8,128)(2,1)S(1)} %add_convert_fusion.18), channel_id=1, source_target_pairs={{1,2},{2,1},{5,6},{6,5},{9,10},{10,9},{13,14},{14,13},{17,18},{18,... | collective-permute-start | bytes 1400840 | tf_op jit(solution)/shard_map/ppermute | solution.py:509
  (70 other events, 466.2 us)
Sparse Core Ops, SparseCore 0:
  12.5 61.4 all-gather.3
  75.8 39.0 all-gather.5
  116.8 38.8 all-gather.7

commit v4 on v3

--- a/solution.py
+++ b/solution.py
@@ -592,11 +592,14 @@
 
 
 def places_steps(sums):
-    place = lax.axis_index("seq")
-    sums = plus(sums, (yield moved(sums, "seq", [(0, 1), (3, 2)])))
-    sums = plus(sums, (yield moved(sums, "seq", [(1, 2), (2, 1)])))
-    back = yield moved(sums, "seq", [(1, 0), (2, 3)])
-    return jnp.where((place == 0) | (place == 3), back, sums)
+    half = sums.shape[0] // 2
+    even = lax.axis_index("seq") % 2 == 0
+    low, high = sums[:half], sums[half:]
+    brought = yield crossed(jnp.where(even, high, low), "seq", (1,))
+    own = plus(jnp.where(even, low, high), brought)
+    own = plus(own, (yield crossed(own, "seq", (2,))))
+    other = yield crossed(own, "seq", (1,))
+    return jnp.concatenate([jnp.where(even, own, other), jnp.where(even, other, own)], axis=0)
 
 
 def offloaded_steps(gradient):
@@ -836,9 +839,8 @@
         pumps = (out_chain, in_chain, mid_chain, enc_chain)[: 2 if number else 4]
         d_q, d_kv, d_context = pumped((d_q[0], d_kv[0], d_context), *pumps)
         d_query.append(d_q)
-        if number == 0:
-            chain, (d_kv, d_context) = token_chain(d_kv, (d_kv, d_context))
-            token_chains.append(chain)
+        chain, (d_kv, d_context) = token_chain(d_kv, (d_kv, d_context))
+        token_chains.append(chain)
         d_key_value.append(d_kv)
     part = width // shards
     hidden_rows = d_bias_hidden.reshape(shards, -1, part).transpose(1, 0, 2).reshape(-1, width)
@@ -863,16 +865,12 @@
     query_rows, d_key_value = pumped(
         (query_rows, d_key_value), mid_chain, out_chain, token_chains[0]
     )
-    for d_kv in d_key_value[1:]:
-        chain, query_rows = token_chain(d_kv, query_rows)
-        token_chains.append(chain)
-    query_rows = pumped(query_rows, attn_chain, in_chain)
+    query_rows = pumped(query_rows, attn_chain, in_chain, token_chains[-1])
     d_tokens = d_first_sum + right_transposed(query_rows, attn_q)
     timeline.token = d_tokens.reshape(tokens.shape)
     early, late = token_chains[0], token_chains[-1]
-    early, late = token_chains[0], token_chains[-1]
-    ahead = [mid_chain, out_chain, attn_chain, early, in_chain, mid_chain, attn_chain, late]
-    ahead += [in_chain, mid_chain, attn_chain, mid_chain, attn_chain, late]
+    ahead = [mid_chain, attn_chain, out_chain, early, in_chain, attn_chain, mid_chain]
+    ahead += [attn_chain, in_chain, mid_chain, attn_chain, late, mid_chain, attn_chain]
     chains = [attn_chain, mid_chain, in_chain, out_chain, enc_chain]
     grad_attn, middle, grad_in, grad_ffn_out, d_encoded, *d_parts = finished(
         *chains, *token_chains, ahead=ahead

time: 448 us -> 445 us (level)
  other arithmetic: 49.2 us -> 55.7 us
  starting transfers between devices: 66.5 us -> 61.3 us
    ppermute x37, starting transfers between devices: 59.3 us -> 54 us  [moved(): return lax.ppermute(timeline.hold(value), axis_name, pairs)]
  transfers between devices with their start and end apart: 43 -> 43, of which waited for: 13 -> 14; matrix products, arithmetic and copies ran while one was open for 25% -> 26% of each run, Pallas kernels for 18% -> 19%
where the time goes in v4:
time: 445 us; the launch traced here: 439 us
  Pallas kernels  122 us (27%)
  waiting for transfers between devices  108 us (24%)
  starting transfers between devices  61.3 us (14%)
  other arithmetic  55.7 us (13%)
  matrix products  46.3 us (10%)
  local copies, waits for them, and re-layouts  30.6 us (7%)
  between operations  15.1 us (3%)
    ppermute x37, waiting for transfers between devices, moved(): return lax.ppermute(timeline.hold(value), axis_name, pairs)  61.1 us
    ppermute x37, starting transfers between devices, moved(): return lax.ppermute(timeline.hold(value), axis_name, pairs)  54 us
    pallas_call x3, Pallas kernels, attend_backward(): pl.pallas_call(backward_kernel, grid=(count, pairs), in_specs=[one, pl.Bl...  38.1 us
    pallas_call x1, Pallas kernels, ffn_stage(): pl.pallas_call(ffn_kernel, in_specs=[pl.BlockSpec(memory_space=pltpu.SMEM...  33.2 us
    pallas_call x2, Pallas kernels, attend_forward(): pl.pallas_call(forward_kernel, grid=(batch, pairs), in_specs=[one, pl.Blo...  31.3 us
    all_gather x3, waiting for transfers between devices, gather_rows(): return lax.all_gather(shard, 'dp', axis=0, tiled=True)  25.5 us
    dot_general x6, matrix products, product(): return jnp.dot(left, right, preferred_element_type=WIDE)  24.7 us
    dot_general x6, matrix products, right_transposed(): lax.dot_general(left, right, (((1,), (1,)), ((), ())), preferred_element_...  21.6 us
  transfers between devices with their start and end apart: 43, of which 14 were waited for; matrix products, arithmetic and copies ran while one was open for 26% of the time, Pallas kernels for 19%

profile of v4, /device:TPU:0, one launch (start us, length us, event | category | flops | bytes accessed | tf_op | source)
XLA Modules:
  0.0 439.2 jit_solution(4722570019398579395)
XLA Ops:
  13.2 5.0 %collective-permute-start = (bf16[2,256,768]{2,1,0:T(8,128)(2,1)S(1)}, bf16[2,256,768]{2,1,0:T(8,128)(2,1)S(1)}, u32[]{:S(2)}, u32[]{:S(2)}) collective-permute-start(bf16[2,256,768]{2,1,0:T(8,128)(2,1)S(1)} %copy-done.4), channel_id=1, source_target_pairs={{0,1},{1,2},{2,3},{4,5},{5,6},{6,7},{8,9},{9,10},{10,11},{12,13},{... | collective-permute-start | bytes 2359304 | tf_op jit(solution)/shard_map/ppermute | solution.py:475
  25.6 10.4 %collective-permute-done = bf16[2,256,768]{2,1,0:T(8,128)(2,1)S(1)} collective-permute-done((bf16[2,256,768]{2,1,0:T(8,128)(2,1)S(1)}, bf16[2,256,768]{2,1,0:T(8,128)(2,1)S(1)}, u32[]{:S(2)}, u32[]{:S(2)}) %collective-permute-start) | collective-permute-done | bytes 786464 | tf_op jit(solution)/shard_map/ppermute | solution.py:475
  41.8 10.0 %collective-permute-done.2 = bf16[2,256,768]{2,1,0:T(8,128)(2,1)S(1)} collective-permute-done((bf16[2,256,768]{2,1,0:T(8,128)(2,1)S(1)}, bf16[2,256,768]{2,1,0:T(8,128)(2,1)S(1)}, u32[]{:S(2)}, u32[]{:S(2)}) %collective-permute-start.2) | collective-permute-done | bytes 786464 | tf_op jit(solution)/shard_map/ppermute | solution.py:472
  51.8 22.1 %all-gather.4.cloned.1.call-done.early_ref = bf16[768,6144]{1,0:T(8,128)(2,1)} async-done(((bf16[96,6144]{1,0:T(8,128)(2,1)}), bf16[768,6144]{1,0:T(8,128)(2,1)}) %all-gather.4.cloned.1.call-update) | async-done | bytes 9437200 | tf_op jit(solution)/shard_map/all_gather | solution.py:542
  84.7 6.2 %fusion = bf16[1,1024,1536]{2,1,0:T(8,128)(2,1)S(1)} fusion(f32[1536]{0:T(1024)S(1)} %copy-done.46, bf16[768,6144]{1,0:T(8,128)(2,1)} %all-gather.4.cloned.1.call-done.early_ref, bf16[256,768]{1,0:T(8,128)(2,1)S(1)} %get-tuple-element.360, bf16[256,768]{1,0:T(8,128)(2,1)S(1)} %get-tuple-element.389, bf16[256,768]{1,0:T(8,128)(2,1)S(1)} %get-tuple-element.356, ...), kind=kOutput, calls=%fused_computation.4 | convolution fusion | flops 2425356288 | bytes 7084032 | tf_op jit(solution)/shard_map/dot_general | solution.py:17
  90.9 6.0 %fusion.1 = bf16[1,1024,1536]{2,1,0:T(8,128)(2,1)S(1)} fusion(f32[1536]{0:T(1024)S(1)} %copy-done.46, bf16[768,6144]{1,0:T(8,128)(2,1)} %all-gather.4.cloned.1.call-done.early_ref, bf16[256,768]{1,0:T(8,128)(2,1)S(1)} %get-tuple-element.361, bf16[256,768]{1,0:T(8,128)(2,1)S(1)} %get-tuple-element.388, bf16[256,768]{1,0:T(8,128)(2,1)S(1)} %get-tuple-element.357, ...), kind=kOutput, calls=%fused_computation.5 | convolution fusion | flops 2425356288 | bytes 7084032 | tf_op jit(solution)/shard_map/dot_general | solution.py:17
  96.9 3.4 pad_maximum_fusion.kv_ref
  107.0 20.8 %attend_forward.2 = (bf16[2,256,768]{2,1,0:T(8,128)(2,1)}, f32[2,6,8,512]{3,2,1,0:T(8,128)}) custom-call(bf16[2,256,768]{2,1,0:T(8,128)(2,1)} %bitcast.207, bf16[2,1024,1536]{2,1,0:T(8,128)(2,1)} %pad_maximum_fusion.kv_ref, s32[2,256,1]{2,1,0:T(8,128)} %copy.43.qid_ref, s32[2,1,1024]{2,1,0:T(1,128)} %broadcast_select_fusion.13.kid_ref), custom_call_target="tpu_custom_call" | custom-call | flops 12582912000 | bytes 12582912 | tf_op jit(solution)/shard_map/attend_forward/pallas_call | solution.py:113
  134.2 3.2 add_convert_fusion.6
  137.5 4.2 fusion.2
  141.7 10.5 %attend_forward.3 = (bf16[2,256,768]{2,1,0:T(8,128)(2,1)}, f32[2,6,8,512]{3,2,1,0:T(8,128)}) custom-call(bf16[2,256,768]{2,1,0:T(8,128)(2,1)} %bitcast.212, bf16[2,256,1536]{2,1,0:T(8,128)(2,1)} %bitcast.202, s32[2,256,1]{2,1,0:T(8,128)} %broadcast_in_dim_broadcast_in_dim.11.qid_ref, s32[2,1,256]{2,1,0:T(1,128)} %broadcast_in_dim_broadcast_in_dim.8.kid_ref), custom_call_target="tpu_custom_call" | custom-call | flops 3145728000 | bytes 3145728 | tf_op jit(solution)/shard_map/attend_forward/pallas_call | solution.py:113
  152.2 3.4 all-gather.8.cloned.1.call-done.out_ref
  155.6 33.2 %ffn_stage.1 = (bf16[512,768]{1,0:T(8,128)(2,1)}, f32[512,768]{1,0:T(8,128)}, bf16[512,768]{1,0:T(8,128)(2,1)}, f32[8,768]{1,0:T(8,128)}, f32[1,3072]{1,0:T(1,12...) custom-call(s32[9]{0:T(128)} %pad_add_fusion.place_ref, ...), custom_call_target="tpu_custom_call" | custom-call | flops 19327352832 | bytes 28311552 | tf_op jit(solution)/shard_map/ffn_stage/pallas_call | solution.py:341
  192.1 12.8 %attend_backward.3 = (bf16[2,256,768]{2,1,0:T(8,128)(2,1)}, bf16[2,256,1536]{2,1,0:T(8,128)(2,1)}) custom-call(bf16[2,256,768]{2,1,0:T(8,128)(2,1)} %bitcast.213, bf16[2,256,1536]{2,1,0:T(8,128)(2,1)} %bitcast.203, s32[2,1,256]{2,1,0:T(1,128)} %broadcast_in_dim_broadcast_in_dim.10.qid_ref, s32[2,256,1]{2,1,0:T(8,128)} %broadcast_in_dim_broadcast_in_dim.9.kid_ref, ...), custom_call_target="tpu_custom_call" | custom-call | flops 3145728000 | bytes 3145728 | tf_op jit(solution)/shard_map/attend_backward/pallas_call | solution.py:140
  218.7 3.3 convolution_convert_fusion.2
  222.0 3.5 collective-permute-done.11
  226.5 7.3 %slotted_products.2 = (bf16[4,96,3072]{2,1,0:T(8,128)(2,1)}, bf16[4,96,3072]{2,1,0:T(8,128)(2,1)}) custom-call(s32[9]{0:T(128)} %pad_add_fusion.place_ref, bf16[512,768]{1,0:T(8,128)(2,1)} %bitcast.210, bf16[512,768]{1,0:T(8,128)(2,1)} %copy-done.36, bf16[512,768]{1,0:T(8,128)(2,1)} %copy-done.34, bf16[512,768]{1,0:T(8,128)(2,1)} %bitcast.167, ...), custom_call_target="tpu_custom_call" | custom-call | flops 2415919104 | bytes 10223616 | tf_op jit(solution)/shard_map/slotted_products/pallas_call | solution.py:438
  233.9 3.4 add_convert_fusion.2
  252.5 12.6 %attend_backward.4 = (bf16[1,256,768]{2,1,0:T(8,128)(2,1)}, bf16[1,1024,1536]{2,1,0:T(8,128)(2,1)}) custom-call(bf16[2,256,768]{2,1,0:T(8,128)(2,1)} %bitcast.208, bf16[2,1024,1536]{2,1,0:T(8,128)(2,1)} %pad_maximum_fusion.kv_ref, s32[2,1,256]{2,1,0:T(1,128)} %broadcast_in_dim.118.qid_ref, s32[2,1024,1]{2,1,0:T(8,128)} %broadcast_select_fusion.kid_ref, ...), custom_call_target="tpu_custom_call" | custom-call | flops 6291456000 | bytes 6291456 | tf_op jit(solution)/shard_map/attend_backward/pallas_call | solution.py:140
  272.9 5.4 %convolution_convert_fusion.1 = bf16[1024,768]{1,0:T(8,128)(2,1)} fusion(bf16[1024,1536]{1,0:T(8,128)(2,1)S(1)} %bitcast.199, bf16[768,6144]{1,0:T(8,128)(2,1)} %all-gather.4.cloned.1.call-done.early_ref), kind=kOutput, calls=%fused_computation.17 | convolution fusion | flops 2416705536 | bytes 7077888 | tf_op jit(solution)/shard_map/dot_general | solution.py:25
  280.9 12.8 %attend_backward.5 = (bf16[1,256,768]{2,1,0:T(8,128)(2,1)}, bf16[1,1024,1536]{2,1,0:T(8,128)(2,1)}) custom-call(bf16[2,256,768]{2,1,0:T(8,128)(2,1)} %bitcast.209, bf16[2,1024,1536]{2,1,0:T(8,128)(2,1)} %pad_maximum_fusion.kv_ref, s32[2,1,256]{2,1,0:T(1,128)} %broadcast_in_dim.118.qid_ref, s32[2,1024,1]{2,1,0:T(8,128)} %broadcast_select_fusion.kid_ref, ...), custom_call_target="tpu_custom_call" | custom-call | flops 6291456000 | bytes 6291456 | tf_op jit(solution)/shard_map/attend_backward/pallas_call | solution.py:140
  306.2 4.3 convolution_convert_fusion
  312.0 12.5 %slotted_products.3 = (bf16[4,96,2432]{2,1,0:T(8,128)(2,1)}, bf16[4,96,2432]{2,1,0:T(8,128)(2,1)}) custom-call(s32[9]{0:T(128)} %pad_add_fusion.place_ref, bf16[256,768]{1,0:T(8,128)(2,1)} %get-tuple-element.351.refs_0_, bf16[256,768]{1,0:T(8,128)(2,1)} %bitcast.172, bf16[256,768]{1,0:T(8,128)(2,1)} %get-tuple-element.350.refs_2_, ...), custom_call_target="tpu_custom_call" | custom-call | flops 5435817984 | bytes 14745600 | tf_op jit(solution)/shard_map/slotted_products/pallas_call | solution.py:438
  338.9 14.4 %collective-permute-done.25 = bf16[256,768]{1,0:T(8,128)(2,1)S(1)} collective-permute-done((bf16[256,768]{1,0:T(8,128)(2,1)S(1)}, bf16[256,768]{1,0:T(8,128)(2,1)S(1)}, u32[]{:S(2)}, u32[]{:S(2)}) %collective-permute-start.25) | collective-permute-done | bytes 393248 | tf_op jit(solution)/shard_map/ppermute | solution.py:509
  355.1 3.4 convolution_add_fusion.1
  361.4 11.0 %collective-permute-done.27 = bf16[2,96,2432]{2,1,0:T(8,128)(2,1)S(1)} collective-permute-done((bf16[2,96,2432]{2,1,0:T(8,128)(2,1)S(1)}, bf16[2,96,2432]{2,1,0:T(8,128)(2,1)S(1)}, u32[]{:S(2)}, u32[]{:S(2)}) %collective-permute-start.27) | collective-permute-done | bytes 933920 | tf_op jit(solution)/shard_map/ppermute | solution.py:509
  376.4 9.6 %collective-permute-start.34 = (bf16[48,3840]{1,0:T(8,128)(2,1)S(1)}, bf16[48,3840]{1,0:T(8,128)(2,1)S(1)}, u32[]{:S(2)}, u32[]{:S(2)}) collective-permute-start(bf16[48,3840]{1,0:T(8,128)(2,1)S(1)} %add_convert_fusion.14), channel_id=1, source_target_pairs={{0,1},{1,0},{2,3},{3,2},{4,5},{5,4},{6,7},{7,6},{8,9},{9,8},{10,11... | collective-permute-start | bytes 1105928 | tf_op jit(solution)/shard_map/ppermute | solution.py:509
  388.8 5.3 %collective-permute-start.33 = (bf16[48,2432]{1,0:T(8,128)(2,1)S(1)}, bf16[48,2432]{1,0:T(8,128)(2,1)S(1)}, u32[]{:S(2)}, u32[]{:S(2)}) collective-permute-start(bf16[48,2432]{1,0:T(8,128)(2,1)S(1)} %broadcast_select_fusion.12), channel_id=1, source_target_pairs={{0,1},{1,0},{2,3},{3,2},{4,5},{5,4},{6,7},{7,6},{8,9},{9,8},{10,11... | collective-permute-start | bytes 700424 | tf_op jit(solution)/shard_map/ppermute | solution.py:509
  394.2 10.8 %collective-permute-done.33 = bf16[48,2432]{1,0:T(8,128)(2,1)S(1)} collective-permute-done((bf16[48,2432]{1,0:T(8,128)(2,1)S(1)}, bf16[48,2432]{1,0:T(8,128)(2,1)S(1)}, u32[]{:S(2)}, u32[]{:S(2)}) %collective-permute-start.33) | collective-permute-done | bytes 233504 | tf_op jit(solution)/shard_map/ppermute | solution.py:509
  407.3 3.4 collective-permute-start.38
  410.7 8.8 %collective-permute-done.36 = bf16[48,2432]{1,0:T(8,128)(2,1)S(1)} collective-permute-done((bf16[48,2432]{1,0:T(8,128)(2,1)S(1)}, bf16[48,2432]{1,0:T(8,128)(2,1)S(1)}, u32[]{:S(2)}, u32[]{:S(2)}) %collective-permute-start.36) | collective-permute-done | bytes 233504 | tf_op jit(solution)/shard_map/ppermute | solution.py:509
  423.6 3.6 collective-permute-done.39
  (348 shorter events, 137.6 us)
Async XLA Ops:
  7.2 66.7 %all-gather.4.cloned.1.call-start = ((), (), s32[]{:S(2)}) async-start(), calls=%async_computation | async-start | bytes 10616832 | tf_op jit(solution)/shard_map/all_gather | solution.py:542
  12.4 139.8 %all-gather.6.cloned.1.call-start = ((), (), s32[]{:S(2)}) async-start(), calls=%async_computation.1 | async-start | bytes 5308416 | tf_op jit(solution)/shard_map/all_gather | solution.py:542
  13.1 142.5 %all-gather.8.cloned.1.call-start = ((), (), s32[]{:S(2)}) async-start(), calls=%async_computation.2 | async-start | bytes 5308416 | tf_op jit(solution)/shard_map/all_gather | solution.py:542
  13.2 22.9 %collective-permute-start = (bf16[2,256,768]{2,1,0:T(8,128)(2,1)S(1)}, bf16[2,256,768]{2,1,0:T(8,128)(2,1)S(1)}, u32[]{:S(2)}, u32[]{:S(2)}) collective-permute-start(bf16[2,256,768]{2,1,0:T(8,128)(2,1)S(1)} %copy-done.4), channel_id=1, source_target_pairs={{0,1},{1,2},{2,3},{4,5},{5,6},{6,7},{8,9},{9,10},{10,11},{12,13},{... | collective-permute-start | bytes 2359304 | tf_op jit(solution)/shard_map/ppermute | solution.py:475
  18.2 33.6 %collective-permute-start.2 = (bf16[2,256,768]{2,1,0:T(8,128)(2,1)S(1)}, bf16[2,256,768]{2,1,0:T(8,128)(2,1)S(1)}, u32[]{:S(2)}, u32[]{:S(2)}) collective-permute-start(bf16[2,256,768]{2,1,0:T(8,128)(2,1)S(1)} %copy-done.4), channel_id=1, source_target_pairs={{0,3},{1,0},{2,1},{3,2},{4,7},{5,4},{6,5},{7,6},{8,11},{9,8},{10,9... | collective-permute-start | bytes 2359304 | tf_op jit(solution)/shard_map/ppermute | solution.py:472
  36.0 15.8 %collective-permute-start.1 = (bf16[2,256,768]{2,1,0:T(8,128)(2,1)S(1)}, bf16[2,256,768]{2,1,0:T(8,128)(2,1)S(1)}, u32[]{:S(2)}, u32[]{:S(2)}) collective-permute-start(bf16[2,256,768]{2,1,0:T(8,128)(2,1)S(1)} %collective-permute-done), channel_id=1, source_target_pairs={{1,2},{2,3},{5,6},{6,7},{9,10},{10,11},{13,14},{14,15},{17,18},{18... | collective-permute-start | bytes 2359304 | tf_op jit(solution)/shard_map/ppermute | solution.py:475
  76.7 26.6 %collective-permute-start.6 = (bf16[2,64,768]{2,1,0:T(8,128)(2,1)}, bf16[2,64,768]{2,1,0:T(8,128)(2,1)}, u32[]{:S(2)}, u32[]{:S(2)}) collective-permute-start(bf16[2,64,768]{2,1,0:T(8,128)(2,1)} %param.15), channel_id=1, source_target_pairs={{0,1},{1,0},{2,3},{3,2},{4,5},{5,4},{6,7},{7,6},{8,9},{9,8},{10,11... | collective-permute-start | bytes 589832 | tf_op jit(solution)/shard_map/ppermute | solution.py:509
  104.6 24.5 %collective-permute-start.7 = (bf16[2,2,64,768]{3,2,1,0:T(8,128)(2,1)S(1)}, bf16[2,2,64,768]{3,2,1,0:T(8,128)(2,1)S(1)}, u32[]{:S(2)}, u32[]{:S(2)}) collective-permute-start(bf16[2,2,64,768]{3,2,1,0:T(8,128)(2,1)S(1)} %maximum_select_fusion.1), channel_id=1, source_target_pairs={{0,2},{1,3},{2,0},{3,1},{4,6},{5,7},{6,4},{7,5},{8,10},{9,11},{10,... | collective-permute-start | bytes 1179656 | tf_op jit(solution)/shard_map/ppermute | solution.py:509
  188.8 16.1 %collective-permute-start.9 = (bf16[4,96,3840]{2,1,0:T(8,128)(2,1)}, bf16[4,96,3840]{2,1,0:T(8,128)(2,1)}, u32[]{:S(2)}, u32[]{:S(2)}) collective-permute-start(bf16[4,96,3840]{2,1,0:T(8,128)(2,1)} %get-tuple-element.191), channel_id=1, source_target_pairs={{0,4},{4,0},{8,12},{12,8},{16,20},{20,16},{24,28},{28,24},{1,5},{5... | collective-permute-start | bytes 8847368 | tf_op jit(solution)/shard_map/ppermute | solution.py:509
  189.1 15.8 %collective-permute-start.8 = (bf16[4,384,768]{2,1,0:T(8,128)(2,1)}, bf16[4,384,768]{2,1,0:T(8,128)(2,1)}, u32[]{:S(2)}, u32[]{:S(2)}) collective-permute-start(bf16[4,384,768]{2,1,0:T(8,128)(2,1)} %get-tuple-element.190), channel_id=1, source_target_pairs={{0,4},{4,0},{8,12},{12,8},{16,20},{20,16},{24,28},{28,24},{1,5},{5... | collective-permute-start | bytes 7077896 | tf_op jit(solution)/shard_map/ppermute | solution.py:509
  206.9 18.5 %collective-permute-start.10 = (bf16[2,384,768]{2,1,0:T(8,128)(2,1)S(1)}, bf16[2,384,768]{2,1,0:T(8,128)(2,1)S(1)}, u32[]{:S(2)}, u32[]{:S(2)}) collective-permute-start(bf16[2,384,768]{2,1,0:T(8,128)(2,1)S(1)} %add_convert_fusion.4), channel_id=1, source_target_pairs={{0,8},{4,20},{8,0},{12,28},{16,24},{20,4},{24,16},{28,12},{1,9},{5... | collective-permute-start | bytes 3538952 | tf_op jit(solution)/shard_map/ppermute | solution.py:509
  233.8 31.3 %collective-permute-start.14 = (bf16[4,96,3072]{2,1,0:T(8,128)(2,1)}, bf16[4,96,3072]{2,1,0:T(8,128)(2,1)}, u32[]{:S(2)}, u32[]{:S(2)}) collective-permute-start(bf16[4,96,3072]{2,1,0:T(8,128)(2,1)} %get-tuple-element.217), channel_id=1, source_target_pairs={{0,4},{4,0},{8,12},{12,8},{16,20},{20,16},{24,28},{28,24},{1,5},{5... | collective-permute-start | bytes 7077896 | tf_op jit(solution)/shard_map/ppermute | solution.py:509
  237.3 27.8 %collective-permute-start.13 = (bf16[2,96,3840]{2,1,0:T(8,128)(2,1)}, bf16[2,96,3840]{2,1,0:T(8,128)(2,1)}, u32[]{:S(2)}, u32[]{:S(2)}) collective-permute-start(bf16[2,96,3840]{2,1,0:T(8,128)(2,1)} %add_convert_fusion.2), channel_id=1, source_target_pairs={{0,8},{4,20},{8,0},{12,28},{16,24},{20,4},{24,16},{28,12},{1,9},{5... | collective-permute-start | bytes 4423688 | tf_op jit(solution)/shard_map/ppermute | solution.py:509
  246.8 18.3 %collective-permute-start.15 = (bf16[2,64,768]{2,1,0:T(8,128)(2,1)S(1)}, bf16[2,64,768]{2,1,0:T(8,128)(2,1)S(1)}, u32[]{:S(2)}, u32[]{:S(2)}) collective-permute-start(bf16[2,64,768]{2,1,0:T(8,128)(2,1)S(1)} %dynamic-slice_bitcast_fusion), channel_id=1, source_target_pairs={{0,2},{1,3},{2,0},{3,1},{4,6},{5,7},{6,4},{7,5},{8,10},{9,11},{10,... | collective-permute-start | bytes 589832 | tf_op jit(solution)/shard_map/ppermute | solution.py:509
  268.1 31.6 %collective-permute-start.17 = (bf16[96,3840]{1,0:T(8,128)(2,1)}, bf16[96,3840]{1,0:T(8,128)(2,1)S(1)}, u32[]{:S(2)}, u32[]{:S(2)}) collective-permute-start(bf16[96,3840]{1,0:T(8,128)(2,1)} %fusion.26), channel_id=1, source_target_pairs={{0,16},{4,12},{8,24},{12,4},{16,0},{20,28},{24,8},{28,20},{1,17},{... | collective-permute-start | bytes 2211848 | tf_op jit(solution)/shard_map/ppermute | solution.py:509
  271.4 28.3 %collective-permute-start.16 = (bf16[192,768]{1,0:T(8,128)(2,1)}, bf16[192,768]{1,0:T(8,128)(2,1)}, u32[]{:S(2)}, u32[]{:S(2)}) collective-permute-start(bf16[192,768]{1,0:T(8,128)(2,1)} %broadcast_select_fusion.9), channel_id=1, source_target_pairs={{0,1},{1,0},{2,3},{3,2},{4,5},{5,4},{6,7},{7,6},{8,9},{9,8},{10,11... | collective-permute-start | bytes 884744 | tf_op jit(solution)/shard_map/ppermute | solution.py:509
  293.7 36.5 %collective-permute-start.18 = (bf16[2,96,3072]{2,1,0:T(8,128)(2,1)}, bf16[2,96,3072]{2,1,0:T(8,128)(2,1)}, u32[]{:S(2)}, u32[]{:S(2)}) collective-permute-start(bf16[2,96,3072]{2,1,0:T(8,128)(2,1)} %add_convert_fusion.3), channel_id=1, source_target_pairs={{0,8},{4,20},{8,0},{12,28},{16,24},{20,4},{24,16},{28,12},{1,9},{5... | collective-permute-start | bytes 3538952 | tf_op jit(solution)/shard_map/ppermute | solution.py:509
  296.9 27.8 %collective-permute-start.20 = (bf16[256,768]{1,0:T(8,128)(2,1)}, bf16[256,768]{1,0:T(8,128)(2,1)}, u32[]{:S(2)}, u32[]{:S(2)}) collective-permute-start(bf16[256,768]{1,0:T(8,128)(2,1)} %get-tuple-element.349), channel_id=1, source_target_pairs={{3,2},{2,1},{7,6},{6,5},{11,10},{10,9},{15,14},{14,13},{19,18},{18... | collective-permute-start | bytes 1179656 | tf_op jit(solution)/shard_map/ppermute | solution.py:509
  298.3 28.3 %collective-permute-start.21 = (bf16[256,768]{1,0:T(8,128)(2,1)}, bf16[256,768]{1,0:T(8,128)(2,1)}, u32[]{:S(2)}, u32[]{:S(2)}) collective-permute-start(bf16[256,768]{1,0:T(8,128)(2,1)} %get-tuple-element.348), channel_id=1, source_target_pairs={{0,1},{1,2},{2,3},{3,0},{4,5},{5,6},{6,7},{7,4},{8,9},{9,10},{10,1... | collective-permute-start | bytes 1179656 | tf_op jit(solution)/shard_map/ppermute | solution.py:509
  303.0 27.2 %collective-permute-start.19 = (bf16[192,768]{1,0:T(8,128)(2,1)S(1)}, bf16[192,768]{1,0:T(8,128)(2,1)}, u32[]{:S(2)}, u32[]{:S(2)}) collective-permute-start(bf16[192,768]{1,0:T(8,128)(2,1)S(1)} %add_convert_fusion.19), channel_id=1, source_target_pairs={{0,2},{1,3},{2,0},{3,1},{4,6},{5,7},{6,4},{7,5},{8,10},{9,11},{10,... | collective-permute-start | bytes 884744 | tf_op jit(solution)/shard_map/ppermute | solution.py:509
  324.5 28.8 %collective-permute-start.22 = (bf16[4,96,2432]{2,1,0:T(8,128)(2,1)}, bf16[4,96,2432]{2,1,0:T(8,128)(2,1)S(1)}, u32[]{:S(2)}, u32[]{:S(2)}) collective-permute-start(bf16[4,96,2432]{2,1,0:T(8,128)(2,1)} %get-tuple-element.248), channel_id=1, source_target_pairs={{0,4},{4,0},{8,12},{12,8},{16,20},{20,16},{24,28},{28,24},{1,5},{5... | collective-permute-start | bytes 5603336 | tf_op jit(solution)/shard_map/ppermute | solution.py:509
  330.2 23.1 %collective-permute-start.25 = (bf16[256,768]{1,0:T(8,128)(2,1)S(1)}, bf16[256,768]{1,0:T(8,128)(2,1)S(1)}, u32[]{:S(2)}, u32[]{:S(2)}) collective-permute-start(bf16[256,768]{1,0:T(8,128)(2,1)S(1)} %get-tuple-element.346), channel_id=1, source_target_pairs={{0,1},{1,2},{2,3},{3,0},{4,5},{5,6},{6,7},{7,4},{8,9},{9,10},{10,1... | collective-permute-start | bytes 1179656 | tf_op jit(solution)/shard_map/ppermute | solution.py:509
  331.4 43.9 %collective-permute-start.29 = (bf16[256,768]{1,0:T(8,128)(2,1)S(1)}, bf16[256,768]{1,0:T(8,128)(2,1)S(1)}, u32[]{:S(2)}, u32[]{:S(2)}) collective-permute-start(bf16[256,768]{1,0:T(8,128)(2,1)S(1)} %add_convert_fusion.13), channel_id=1, source_target_pairs={{1,0},{2,1},{3,2},{5,4},{6,5},{7,6},{9,8},{10,9},{11,10},{13,12},{... | collective-permute-start | bytes 1179656 | tf_op jit(solution)/shard_map/ppermute | solution.py:509
  337.9 37.4 %collective-permute-start.28 = (bf16[192,768]{1,0:T(8,128)(2,1)S(1)}, bf16[192,768]{1,0:T(8,128)(2,1)S(1)}, u32[]{:S(2)}, u32[]{:S(2)}) collective-permute-start(bf16[192,768]{1,0:T(8,128)(2,1)S(1)} %add_convert_fusion.18), channel_id=1, source_target_pairs={{0,1},{1,0},{2,3},{3,2},{4,5},{5,4},{6,7},{7,6},{8,9},{9,8},{10,11... | collective-permute-start | bytes 884744 | tf_op jit(solution)/shard_map/ppermute | solution.py:509
  338.0 20.8 %collective-permute-start.26 = (bf16[96,3072]{1,0:T(8,128)(2,1)S(1)}, bf16[96,3072]{1,0:T(8,128)(2,1)S(1)}, u32[]{:S(2)}, u32[]{:S(2)}) collective-permute-start(bf16[96,3072]{1,0:T(8,128)(2,1)S(1)} %fusion.28), channel_id=1, source_target_pairs={{0,16},{4,12},{8,24},{12,4},{16,0},{20,28},{24,8},{28,20},{1,17},{... | collective-permute-start | bytes 1769480 | tf_op jit(solution)/shard_map/ppermute | solution.py:509
  353.4 66.2 %collective-permute-start.37 = (bf16[256,768]{1,0:T(8,128)(2,1)S(1)}, bf16[256,768]{1,0:T(8,128)(2,1)S(1)}, u32[]{:S(2)}, u32[]{:S(2)}) collective-permute-start(bf16[256,768]{1,0:T(8,128)(2,1)S(1)} %add_convert_fusion.12), channel_id=1, source_target_pairs={{1,0},{2,1},{3,2},{5,4},{6,5},{7,6},{9,8},{10,9},{11,10},{13,12},{... | collective-permute-start | bytes 1179656 | tf_op jit(solution)/shard_map/ppermute | solution.py:509
  355.1 20.2 %collective-permute-start.30 = (bf16[48,3840]{1,0:T(8,128)(2,1)S(1)}, bf16[48,3840]{1,0:T(8,128)(2,1)S(1)}, u32[]{:S(2)}, u32[]{:S(2)}) collective-permute-start(bf16[48,3840]{1,0:T(8,128)(2,1)S(1)} %add_convert_fusion.15), channel_id=1, source_target_pairs={{0,2},{1,3},{2,0},{3,1},{4,6},{5,7},{6,4},{7,5},{8,10},{9,11},{10,... | collective-permute-start | bytes 1105928 | tf_op jit(solution)/shard_map/ppermute | solution.py:509
  372.4 16.4 %collective-permute-start.32 = (bf16[48,3072]{1,0:T(8,128)(2,1)S(1)}, bf16[48,3072]{1,0:T(8,128)(2,1)S(1)}, u32[]{:S(2)}, u32[]{:S(2)}) collective-permute-start(bf16[48,3072]{1,0:T(8,128)(2,1)S(1)} %broadcast_select_fusion.6), channel_id=1, source_target_pairs={{0,1},{1,0},{2,3},{3,2},{4,5},{5,4},{6,7},{7,6},{8,9},{9,8},{10,11... | collective-permute-start | bytes 884744 | tf_op jit(solution)/shard_map/ppermute | solution.py:509
  376.4 28.8 %collective-permute-start.34 = (bf16[48,3840]{1,0:T(8,128)(2,1)S(1)}, bf16[48,3840]{1,0:T(8,128)(2,1)S(1)}, u32[]{:S(2)}, u32[]{:S(2)}) collective-permute-start(bf16[48,3840]{1,0:T(8,128)(2,1)S(1)} %add_convert_fusion.14), channel_id=1, source_target_pairs={{0,1},{1,0},{2,3},{3,2},{4,5},{5,4},{6,7},{7,6},{8,9},{9,8},{10,11... | collective-permute-start | bytes 1105928 | tf_op jit(solution)/shard_map/ppermute | solution.py:509
  388.8 16.3 %collective-permute-start.33 = (bf16[48,2432]{1,0:T(8,128)(2,1)S(1)}, bf16[48,2432]{1,0:T(8,128)(2,1)S(1)}, u32[]{:S(2)}, u32[]{:S(2)}) collective-permute-start(bf16[48,2432]{1,0:T(8,128)(2,1)S(1)} %broadcast_select_fusion.12), channel_id=1, source_target_pairs={{0,1},{1,0},{2,3},{3,2},{4,5},{5,4},{6,7},{7,6},{8,9},{9,8},{10,11... | collective-permute-start | bytes 700424 | tf_op jit(solution)/shard_map/ppermute | solution.py:509
  405.2 14.3 %collective-permute-start.36 = (bf16[48,2432]{1,0:T(8,128)(2,1)S(1)}, bf16[48,2432]{1,0:T(8,128)(2,1)S(1)}, u32[]{:S(2)}, u32[]{:S(2)}) collective-permute-start(bf16[48,2432]{1,0:T(8,128)(2,1)S(1)} %add_convert_fusion.21), channel_id=1, source_target_pairs={{0,2},{1,3},{2,0},{3,1},{4,6},{5,7},{6,4},{7,5},{8,10},{9,11},{10,... | collective-permute-start | bytes 700424 | tf_op jit(solution)/shard_map/ppermute | solution.py:509
  407.3 14.6 %collective-permute-start.38 = (bf16[48,3072]{1,0:T(8,128)(2,1)S(1)}, bf16[48,3072]{1,0:T(8,128)(2,1)S(1)}, u32[]{:S(2)}, u32[]{:S(2)}) collective-permute-start(bf16[48,3072]{1,0:T(8,128)(2,1)S(1)} %add_convert_fusion.16), channel_id=1, source_target_pairs={{0,1},{1,0},{2,3},{3,2},{4,5},{5,4},{6,7},{7,6},{8,9},{9,8},{10,11... | collective-permute-start | bytes 884744 | tf_op jit(solution)/shard_map/ppermute | solution.py:509
  (69 other events, 464.3 us)
Sparse Core Ops, SparseCore 0:
  12.5 61.4 all-gather.3
  75.8 39.0 all-gather.5
  116.8 38.7 all-gather.7

commit v5 on v4

--- a/solution.py
+++ b/solution.py
@@ -493,6 +493,28 @@
     return sum([part.astype(WIDE) for part in parts], slots[0].astype(WIDE))
 
 
+def pair_steps(slots, groups):
+    ring = [(source, (source + 1) % groups) for source in range(groups)]
+    back = [(source, source - 1) for source in range(1, groups)]
+    first = slots[0]
+    ahead, around = yield [
+        moved(first[2], "seq", [(3, 2), (2, 1)]),
+        moved(first[groups - 1], "seq", ring),
+    ]
+    second = slots[1]
+    going = jnp.concatenate([plus(first[1], ahead), second[2]], axis=0)
+    brought, last = yield [moved(going, "seq", back), moved(second[groups - 1], "seq", ring)]
+    ahead = brought[first[1].shape[0] :]
+    ended = yield moved(plus(second[1], ahead), "seq", back)
+    brought = brought[: first[1].shape[0]]
+    return jnp.stack(
+        [
+            first[0].astype(WIDE) + around.astype(WIDE) + brought.astype(WIDE),
+            second[0].astype(WIDE) + last.astype(WIDE) + ended.astype(WIDE),
+        ]
+    )
+
+
 class Order:
     token = None
 
@@ -828,10 +850,13 @@
     def token_chain(d_kv, after):
         d_part = right_transposed(d_kv, attn_kv).astype(LOW)
         d_part, after = lax.optimization_barrier((d_part, after))
-        d_part = d_part.reshape(groups, local_len, width)
-        return Chain(scatter_steps(list(d_part), groups)), after
-
-    d_query, d_key_value, token_chains = [], [], []
+        token_slots.append(list(d_part.reshape(groups, local_len, width)))
+        if not paired:
+            return Chain(scatter_steps(token_slots[-1], groups)), after
+        return Chain(pair_steps(token_slots, groups)) if len(token_slots) == 1 else None, after
+
+    paired = groups == 4 and batch == 2
+    d_query, d_key_value, token_chains, token_slots = [], [], [], []
     for number in range(batch):
         d_q, d_kv = attend_backward(
             queries, keys_values, ids, context, d_context, totals, number, 1
@@ -840,7 +865,8 @@
         d_q, d_kv, d_context = pumped((d_q[0], d_kv[0], d_context), *pumps)
         d_query.append(d_q)
         chain, (d_kv, d_context) = token_chain(d_kv, (d_kv, d_context))
-        token_chains.append(chain)
+        if chain is not None:
+            token_chains.append(chain)
         d_key_value.append(d_kv)
     part = width // shards
     hidden_rows = d_bias_hidden.reshape(shards, -1, part).transpose(1, 0, 2).reshape(-1, width)
@@ -865,18 +891,18 @@
     query_rows, d_key_value = pumped(
         (query_rows, d_key_value), mid_chain, out_chain, token_chains[0]
     )
-    query_rows = pumped(query_rows, attn_chain, in_chain, token_chains[-1])
+    query_rows = pumped(query_rows, attn_chain, in_chain)
     d_tokens = d_first_sum + right_transposed(query_rows, attn_q)
     timeline.token = d_tokens.reshape(tokens.shape)
     early, late = token_chains[0], token_chains[-1]
-    ahead = [mid_chain, attn_chain, out_chain, early, in_chain, attn_chain, mid_chain]
-    ahead += [attn_chain, in_chain, mid_chain, attn_chain, late, mid_chain, attn_chain]
+    ahead = [mid_chain, out_chain, attn_chain, late, in_chain, attn_chain, mid_chain]
+    ahead += [attn_chain, in_chain, mid_chain, attn_chain, early, mid_chain, attn_chain]
     chains = [attn_chain, mid_chain, in_chain, out_chain, enc_chain]
     grad_attn, middle, grad_in, grad_ffn_out, d_encoded, *d_parts = finished(
         *chains, *token_chains, ahead=ahead
     )
     d_tokens, timeline.token = timeline.token, None
-    d_tokens = d_tokens + jnp.stack(d_parts)
+    d_tokens = d_tokens + (d_parts[0] if paired else jnp.stack(d_parts))
     if slotted:
         mine = grad_attn[:, 3 * width :].T
     else:

time: 445 us -> 452 us (1.016)
  waiting for transfers between devices: 108 us -> 130 us
  starting transfers between devices: 61.3 us -> 46.7 us
    ppermute x37 -> x36, waiting for transfers between devices: 61.1 us -> 82.9 us  [moved(): return lax.ppermute(timeline.hold(value), axis_name, pairs)]
    ppermute x37 -> x36, starting transfers between devices: 54 us -> 39.5 us  [moved(): return lax.ppermute(timeline.hold(value), axis_name, pairs)]
  transfers between devices with their start and end apart: 43 -> 42, of which waited for: 14 -> 15; matrix products, arithmetic and copies ran while one was open for 26% -> 25% of each run, Pallas kernels for 19% -> 18%
where the time goes in v5:
time: 452 us; the launch traced here: 446 us
  waiting for transfers between devices  130 us (29%)
  Pallas kernels  122 us (27%)
  other arithmetic  55.4 us (12%)
  starting transfers between devices  46.7 us (10%)
  matrix products  46.3 us (10%)
  local copies, waits for them, and re-layouts  30.6 us (7%)
  between operations  15.1 us (3%)
    ppermute x36, waiting for transfers between devices, moved(): return lax.ppermute(timeline.hold(value), axis_name, pairs)  82.9 us
    ppermute x36, starting transfers between devices, moved(): return lax.ppermute(timeline.hold(value), axis_name, pairs)  39.5 us
    pallas_call x3, Pallas kernels, attend_backward(): pl.pallas_call(backward_kernel, grid=(count, pairs), in_specs=[one, pl.Bl...  38.2 us
    pallas_call x1, Pallas kernels, ffn_stage(): pl.pallas_call(ffn_kernel, in_specs=[pl.BlockSpec(memory_space=pltpu.SMEM...  33.2 us
    pallas_call x2, Pallas kernels, attend_forward(): pl.pallas_call(forward_kernel, grid=(batch, pairs), in_specs=[one, pl.Blo...  31.3 us
    all_gather x3, waiting for transfers between devices, gather_rows(): return lax.all_gather(shard, 'dp', axis=0, tiled=True)  25.5 us
    dot_general x6, matrix products, product(): return jnp.dot(left, right, preferred_element_type=WIDE)  24.7 us
    dot_general x6, matrix products, right_transposed(): lax.dot_general(left, right, (((1,), (1,)), ((), ())), preferred_element_...  21.6 us
  transfers between devices with their start and end apart: 42, of which 15 were waited for; matrix products, arithmetic and copies ran while one was open for 25% of the time, Pallas kernels for 18%

profile of v5, /device:TPU:0, one launch (start us, length us, event | category | flops | bytes accessed | tf_op | source)
XLA Modules:
  0.0 446.1 jit_solution(7290170265446047960)
XLA Ops:
  13.2 5.0 %collective-permute-start = (bf16[2,256,768]{2,1,0:T(8,128)(2,1)S(1)}, bf16[2,256,768]{2,1,0:T(8,128)(2,1)S(1)}, u32[]{:S(2)}, u32[]{:S(2)}) collective-permute-start(bf16[2,256,768]{2,1,0:T(8,128)(2,1)S(1)} %copy-done.4), channel_id=1, source_target_pairs={{0,1},{1,2},{2,3},{4,5},{5,6},{6,7},{8,9},{9,10},{10,11},{12,13},{... | collective-permute-start | bytes 2359304 | tf_op jit(solution)/shard_map/ppermute | solution.py:475
  25.6 10.4 %collective-permute-done = bf16[2,256,768]{2,1,0:T(8,128)(2,1)S(1)} collective-permute-done((bf16[2,256,768]{2,1,0:T(8,128)(2,1)S(1)}, bf16[2,256,768]{2,1,0:T(8,128)(2,1)S(1)}, u32[]{:S(2)}, u32[]{:S(2)}) %collective-permute-start) | collective-permute-done | bytes 786464 | tf_op jit(solution)/shard_map/ppermute | solution.py:475
  41.8 10.0 %collective-permute-done.2 = bf16[2,256,768]{2,1,0:T(8,128)(2,1)S(1)} collective-permute-done((bf16[2,256,768]{2,1,0:T(8,128)(2,1)S(1)}, bf16[2,256,768]{2,1,0:T(8,128)(2,1)S(1)}, u32[]{:S(2)}, u32[]{:S(2)}) %collective-permute-start.2) | collective-permute-done | bytes 786464 | tf_op jit(solution)/shard_map/ppermute | solution.py:472
  51.8 22.1 %all-gather.4.cloned.1.call-done.early_ref = bf16[768,6144]{1,0:T(8,128)(2,1)} async-done(((bf16[96,6144]{1,0:T(8,128)(2,1)}), bf16[768,6144]{1,0:T(8,128)(2,1)}) %all-gather.4.cloned.1.call-update) | async-done | bytes 9437200 | tf_op jit(solution)/shard_map/all_gather | solution.py:564
  84.7 6.2 %fusion = bf16[1,1024,1536]{2,1,0:T(8,128)(2,1)S(1)} fusion(f32[1536]{0:T(1024)S(1)} %copy-done.47, bf16[768,6144]{1,0:T(8,128)(2,1)} %all-gather.4.cloned.1.call-done.early_ref, bf16[256,768]{1,0:T(8,128)(2,1)S(1)} %get-tuple-element.360, bf16[256,768]{1,0:T(8,128)(2,1)S(1)} %get-tuple-element.389, bf16[256,768]{1,0:T(8,128)(2,1)S(1)} %get-tuple-element.356, ...), kind=kOutput, calls=%fused_computation.4 | convolution fusion | flops 2425356288 | bytes 7084032 | tf_op jit(solution)/shard_map/dot_general | solution.py:17
  90.9 6.0 %fusion.1 = bf16[1,1024,1536]{2,1,0:T(8,128)(2,1)S(1)} fusion(f32[1536]{0:T(1024)S(1)} %copy-done.47, bf16[768,6144]{1,0:T(8,128)(2,1)} %all-gather.4.cloned.1.call-done.early_ref, bf16[256,768]{1,0:T(8,128)(2,1)S(1)} %get-tuple-element.361, bf16[256,768]{1,0:T(8,128)(2,1)S(1)} %get-tuple-element.388, bf16[256,768]{1,0:T(8,128)(2,1)S(1)} %get-tuple-element.357, ...), kind=kOutput, calls=%fused_computation.5 | convolution fusion | flops 2425356288 | bytes 7084032 | tf_op jit(solution)/shard_map/dot_general | solution.py:17
  96.9 3.4 pad_maximum_fusion.kv_ref
  107.0 20.8 %attend_forward.2 = (bf16[2,256,768]{2,1,0:T(8,128)(2,1)}, f32[2,6,8,512]{3,2,1,0:T(8,128)}) custom-call(bf16[2,256,768]{2,1,0:T(8,128)(2,1)} %bitcast.207, bf16[2,1024,1536]{2,1,0:T(8,128)(2,1)} %pad_maximum_fusion.kv_ref, s32[2,256,1]{2,1,0:T(8,128)} %copy.43.qid_ref, s32[2,1,1024]{2,1,0:T(1,128)} %broadcast_select_fusion.13.kid_ref), custom_call_target="tpu_custom_call" | custom-call | flops 12582912000 | bytes 12582912 | tf_op jit(solution)/shard_map/attend_forward/pallas_call | solution.py:113
  134.2 3.2 add_convert_fusion.6
  137.5 4.2 fusion.2
  141.7 10.5 %attend_forward.3 = (bf16[2,256,768]{2,1,0:T(8,128)(2,1)}, f32[2,6,8,512]{3,2,1,0:T(8,128)}) custom-call(bf16[2,256,768]{2,1,0:T(8,128)(2,1)} %bitcast.212, bf16[2,256,1536]{2,1,0:T(8,128)(2,1)} %bitcast.202, s32[2,256,1]{2,1,0:T(8,128)} %broadcast_in_dim_broadcast_in_dim.11.qid_ref, s32[2,1,256]{2,1,0:T(1,128)} %broadcast_in_dim_broadcast_in_dim.8.kid_ref), custom_call_target="tpu_custom_call" | custom-call | flops 3145728000 | bytes 3145728 | tf_op jit(solution)/shard_map/attend_forward/pallas_call | solution.py:113
  152.2 3.4 all-gather.8.cloned.1.call-done.out_ref
  155.6 33.2 %ffn_stage.1 = (bf16[512,768]{1,0:T(8,128)(2,1)}, f32[512,768]{1,0:T(8,128)}, bf16[512,768]{1,0:T(8,128)(2,1)}, f32[8,768]{1,0:T(8,128)}, f32[1,3072]{1,0:T(1,12...) custom-call(s32[9]{0:T(128)} %pad_add_fusion.place_ref, ...), custom_call_target="tpu_custom_call" | custom-call | flops 19327352832 | bytes 28311552 | tf_op jit(solution)/shard_map/ffn_stage/pallas_call | solution.py:341
  192.1 12.8 %attend_backward.3 = (bf16[2,256,768]{2,1,0:T(8,128)(2,1)}, bf16[2,256,1536]{2,1,0:T(8,128)(2,1)}) custom-call(bf16[2,256,768]{2,1,0:T(8,128)(2,1)} %bitcast.213, bf16[2,256,1536]{2,1,0:T(8,128)(2,1)} %bitcast.203, s32[2,1,256]{2,1,0:T(1,128)} %broadcast_in_dim_broadcast_in_dim.10.qid_ref, s32[2,256,1]{2,1,0:T(8,128)} %broadcast_in_dim_broadcast_in_dim.9.kid_ref, ...), custom_call_target="tpu_custom_call" | custom-call | flops 3145728000 | bytes 3145728 | tf_op jit(solution)/shard_map/attend_backward/pallas_call | solution.py:140
  218.7 3.3 convolution_convert_fusion.2
  222.1 3.4 collective-permute-done.11
  226.5 7.2 %slotted_products.2 = (bf16[4,96,3072]{2,1,0:T(8,128)(2,1)}, bf16[4,96,3072]{2,1,0:T(8,128)(2,1)}) custom-call(s32[9]{0:T(128)} %pad_add_fusion.place_ref, bf16[512,768]{1,0:T(8,128)(2,1)} %bitcast.210, bf16[512,768]{1,0:T(8,128)(2,1)} %copy-done.37, bf16[512,768]{1,0:T(8,128)(2,1)} %copy-done.35, bf16[512,768]{1,0:T(8,128)(2,1)} %bitcast.167, ...), custom_call_target="tpu_custom_call" | custom-call | flops 2415919104 | bytes 10223616 | tf_op jit(solution)/shard_map/slotted_products/pallas_call | solution.py:438
  233.9 3.4 add_convert_fusion.2
  252.4 12.6 %attend_backward.4 = (bf16[1,256,768]{2,1,0:T(8,128)(2,1)}, bf16[1,1024,1536]{2,1,0:T(8,128)(2,1)}) custom-call(bf16[2,256,768]{2,1,0:T(8,128)(2,1)} %bitcast.208, bf16[2,1024,1536]{2,1,0:T(8,128)(2,1)} %pad_maximum_fusion.kv_ref, s32[2,1,256]{2,1,0:T(1,128)} %broadcast_in_dim.118.qid_ref, s32[2,1024,1]{2,1,0:T(8,128)} %broadcast_select_fusion.kid_ref, ...), custom_call_target="tpu_custom_call" | custom-call | flops 6291456000 | bytes 6291456 | tf_op jit(solution)/shard_map/attend_backward/pallas_call | solution.py:140
  272.9 5.4 %convolution_convert_fusion.1 = bf16[1024,768]{1,0:T(8,128)(2,1)} fusion(bf16[1024,1536]{1,0:T(8,128)(2,1)S(1)} %bitcast.199, bf16[768,6144]{1,0:T(8,128)(2,1)} %all-gather.4.cloned.1.call-done.early_ref), kind=kOutput, calls=%fused_computation.17 | convolution fusion | flops 2416705536 | bytes 7077888 | tf_op jit(solution)/shard_map/dot_general | solution.py:25
  280.9 12.8 %attend_backward.5 = (bf16[1,256,768]{2,1,0:T(8,128)(2,1)}, bf16[1,1024,1536]{2,1,0:T(8,128)(2,1)}) custom-call(bf16[2,256,768]{2,1,0:T(8,128)(2,1)} %bitcast.209, bf16[2,1024,1536]{2,1,0:T(8,128)(2,1)} %pad_maximum_fusion.kv_ref, s32[2,1,256]{2,1,0:T(1,128)} %broadcast_in_dim.118.qid_ref, s32[2,1024,1]{2,1,0:T(8,128)} %broadcast_select_fusion.kid_ref, ...), custom_call_target="tpu_custom_call" | custom-call | flops 6291456000 | bytes 6291456 | tf_op jit(solution)/shard_map/attend_backward/pallas_call | solution.py:140
  302.9 3.2 collective-permute-start.19
  306.1 4.3 convolution_convert_fusion
  311.9 12.5 %slotted_products.3 = (bf16[4,96,2432]{2,1,0:T(8,128)(2,1)}, bf16[4,96,2432]{2,1,0:T(8,128)(2,1)}) custom-call(s32[9]{0:T(128)} %pad_add_fusion.place_ref, bf16[256,768]{1,0:T(8,128)(2,1)} %get-tuple-element.351.refs_0_, bf16[256,768]{1,0:T(8,128)(2,1)} %bitcast.172, bf16[256,768]{1,0:T(8,128)(2,1)} %get-tuple-element.350.refs_2_, ...), custom_call_target="tpu_custom_call" | custom-call | flops 5435817984 | bytes 14745600 | tf_op jit(solution)/shard_map/slotted_products/pallas_call | solution.py:438
  326.8 3.3 collective-permute-done.19
  338.0 8.3 %collective-permute-done.23 = bf16[48,3840]{1,0:T(8,128)(2,1)S(1)} collective-permute-done((bf16[48,3840]{1,0:T(8,128)(2,1)S(1)}, bf16[48,3840]{1,0:T(8,128)(2,1)S(1)}, u32[]{:S(2)}, u32[]{:S(2)}) %collective-permute-start.23) | collective-permute-done | bytes 368672 | tf_op jit(solution)/shard_map/ppermute | solution.py:531
  347.4 3.4 convolution_add_fusion.1
  351.0 5.1 %collective-permute-done.24 = bf16[96,3072]{1,0:T(8,128)(2,1)S(1)} collective-permute-done((bf16[96,3072]{1,0:T(8,128)(2,1)S(1)}, bf16[96,3072]{1,0:T(8,128)(2,1)S(1)}, u32[]{:S(2)}, u32[]{:S(2)}) %collective-permute-start.24) | collective-permute-done | bytes 589856 | tf_op jit(solution)/shard_map/ppermute | solution.py:531
  358.7 18.6 %collective-permute-done.25 = bf16[192,768]{1,0:T(8,128)(2,1)S(1)} collective-permute-done((bf16[192,768]{1,0:T(8,128)(2,1)S(1)}, bf16[192,768]{1,0:T(8,128)(2,1)S(1)}, u32[]{:S(2)}, u32[]{:S(2)}) %collective-permute-start.25) | collective-permute-done | bytes 294944 | tf_op jit(solution)/shard_map/ppermute | solution.py:531
  384.4 4.2 collective-permute-done.30
  391.2 22.7 %collective-permute-done.32 = bf16[48,2432]{1,0:T(8,128)(2,1)S(1)} collective-permute-done((bf16[48,2432]{1,0:T(8,128)(2,1)S(1)}, bf16[48,2432]{1,0:T(8,128)(2,1)S(1)}, u32[]{:S(2)}, u32[]{:S(2)}) %collective-permute-start.32) | collective-permute-done | bytes 233504 | tf_op jit(solution)/shard_map/ppermute | solution.py:531
  416.2 9.7 %collective-permute-done.35 = bf16[48,2432]{1,0:T(8,128)(2,1)S(1)} collective-permute-done((bf16[48,2432]{1,0:T(8,128)(2,1)S(1)}, bf16[48,2432]{1,0:T(8,128)(2,1)S(1)}, u32[]{:S(2)}, u32[]{:S(2)}) %collective-permute-start.35) | collective-permute-done | bytes 233504 | tf_op jit(solution)/shard_map/ppermute | solution.py:531
  (348 shorter events, 136.4 us)
Async XLA Ops:
  7.2 66.7 %all-gather.4.cloned.1.call-start = ((), (), s32[]{:S(2)}) async-start(), calls=%async_computation | async-start | bytes 10616832 | tf_op jit(solution)/shard_map/all_gather | solution.py:564
  12.4 139.8 %all-gather.6.cloned.1.call-start = ((), (), s32[]{:S(2)}) async-start(), calls=%async_computation.1 | async-start | bytes 5308416 | tf_op jit(solution)/shard_map/all_gather | solution.py:564
  13.1 142.5 %all-gather.8.cloned.1.call-start = ((), (), s32[]{:S(2)}) async-start(), calls=%async_computation.2 | async-start | bytes 5308416 | tf_op jit(solution)/shard_map/all_gather | solution.py:564
  13.2 22.9 %collective-permute-start = (bf16[2,256,768]{2,1,0:T(8,128)(2,1)S(1)}, bf16[2,256,768]{2,1,0:T(8,128)(2,1)S(1)}, u32[]{:S(2)}, u32[]{:S(2)}) collective-permute-start(bf16[2,256,768]{2,1,0:T(8,128)(2,1)S(1)} %copy-done.4), channel_id=1, source_target_pairs={{0,1},{1,2},{2,3},{4,5},{5,6},{6,7},{8,9},{9,10},{10,11},{12,13},{... | collective-permute-start | bytes 2359304 | tf_op jit(solution)/shard_map/ppermute | solution.py:475
  18.2 33.6 %collective-permute-start.2 = (bf16[2,256,768]{2,1,0:T(8,128)(2,1)S(1)}, bf16[2,256,768]{2,1,0:T(8,128)(2,1)S(1)}, u32[]{:S(2)}, u32[]{:S(2)}) collective-permute-start(bf16[2,256,768]{2,1,0:T(8,128)(2,1)S(1)} %copy-done.4), channel_id=1, source_target_pairs={{0,3},{1,0},{2,1},{3,2},{4,7},{5,4},{6,5},{7,6},{8,11},{9,8},{10,9... | collective-permute-start | bytes 2359304 | tf_op jit(solution)/shard_map/ppermute | solution.py:472
  36.0 15.8 %collective-permute-start.1 = (bf16[2,256,768]{2,1,0:T(8,128)(2,1)S(1)}, bf16[2,256,768]{2,1,0:T(8,128)(2,1)S(1)}, u32[]{:S(2)}, u32[]{:S(2)}) collective-permute-start(bf16[2,256,768]{2,1,0:T(8,128)(2,1)S(1)} %collective-permute-done), channel_id=1, source_target_pairs={{1,2},{2,3},{5,6},{6,7},{9,10},{10,11},{13,14},{14,15},{17,18},{18... | collective-permute-start | bytes 2359304 | tf_op jit(solution)/shard_map/ppermute | solution.py:475
  76.7 26.6 %collective-permute-start.6 = (bf16[2,64,768]{2,1,0:T(8,128)(2,1)}, bf16[2,64,768]{2,1,0:T(8,128)(2,1)}, u32[]{:S(2)}, u32[]{:S(2)}) collective-permute-start(bf16[2,64,768]{2,1,0:T(8,128)(2,1)} %param.15), channel_id=1, source_target_pairs={{0,1},{1,0},{2,3},{3,2},{4,5},{5,4},{6,7},{7,6},{8,9},{9,8},{10,11... | collective-permute-start | bytes 589832 | tf_op jit(solution)/shard_map/ppermute | solution.py:531
  104.6 24.5 %collective-permute-start.7 = (bf16[2,2,64,768]{3,2,1,0:T(8,128)(2,1)S(1)}, bf16[2,2,64,768]{3,2,1,0:T(8,128)(2,1)S(1)}, u32[]{:S(2)}, u32[]{:S(2)}) collective-permute-start(bf16[2,2,64,768]{3,2,1,0:T(8,128)(2,1)S(1)} %maximum_select_fusion.1), channel_id=1, source_target_pairs={{0,2},{1,3},{2,0},{3,1},{4,6},{5,7},{6,4},{7,5},{8,10},{9,11},{10,... | collective-permute-start | bytes 1179656 | tf_op jit(solution)/shard_map/ppermute | solution.py:531
  188.8 16.1 %collective-permute-start.9 = (bf16[4,96,3840]{2,1,0:T(8,128)(2,1)}, bf16[4,96,3840]{2,1,0:T(8,128)(2,1)}, u32[]{:S(2)}, u32[]{:S(2)}) collective-permute-start(bf16[4,96,3840]{2,1,0:T(8,128)(2,1)} %get-tuple-element.190), channel_id=1, source_target_pairs={{0,4},{4,0},{8,12},{12,8},{16,20},{20,16},{24,28},{28,24},{1,5},{5... | collective-permute-start | bytes 8847368 | tf_op jit(solution)/shard_map/ppermute | solution.py:531
  189.1 15.7 %collective-permute-start.8 = (bf16[4,384,768]{2,1,0:T(8,128)(2,1)}, bf16[4,384,768]{2,1,0:T(8,128)(2,1)}, u32[]{:S(2)}, u32[]{:S(2)}) collective-permute-start(bf16[4,384,768]{2,1,0:T(8,128)(2,1)} %get-tuple-element.189), channel_id=1, source_target_pairs={{0,4},{4,0},{8,12},{12,8},{16,20},{20,16},{24,28},{28,24},{1,5},{5... | collective-permute-start | bytes 7077896 | tf_op jit(solution)/shard_map/ppermute | solution.py:531
  206.9 18.5 %collective-permute-start.10 = (bf16[2,384,768]{2,1,0:T(8,128)(2,1)S(1)}, bf16[2,384,768]{2,1,0:T(8,128)(2,1)S(1)}, u32[]{:S(2)}, u32[]{:S(2)}) collective-permute-start(bf16[2,384,768]{2,1,0:T(8,128)(2,1)S(1)} %add_convert_fusion.4), channel_id=1, source_target_pairs={{0,8},{4,20},{8,0},{12,28},{16,24},{20,4},{24,16},{28,12},{1,9},{5... | collective-permute-start | bytes 3538952 | tf_op jit(solution)/shard_map/ppermute | solution.py:531
  233.8 31.4 %collective-permute-start.14 = (bf16[4,96,3072]{2,1,0:T(8,128)(2,1)}, bf16[4,96,3072]{2,1,0:T(8,128)(2,1)}, u32[]{:S(2)}, u32[]{:S(2)}) collective-permute-start(bf16[4,96,3072]{2,1,0:T(8,128)(2,1)} %get-tuple-element.216), channel_id=1, source_target_pairs={{0,4},{4,0},{8,12},{12,8},{16,20},{20,16},{24,28},{28,24},{1,5},{5... | collective-permute-start | bytes 7077896 | tf_op jit(solution)/shard_map/ppermute | solution.py:531
  237.2 27.8 %collective-permute-start.13 = (bf16[2,96,3840]{2,1,0:T(8,128)(2,1)}, bf16[2,96,3840]{2,1,0:T(8,128)(2,1)}, u32[]{:S(2)}, u32[]{:S(2)}) collective-permute-start(bf16[2,96,3840]{2,1,0:T(8,128)(2,1)} %add_convert_fusion.2), channel_id=1, source_target_pairs={{0,8},{4,20},{8,0},{12,28},{16,24},{20,4},{24,16},{28,12},{1,9},{5... | collective-permute-start | bytes 4423688 | tf_op jit(solution)/shard_map/ppermute | solution.py:531
  246.8 18.3 %collective-permute-start.15 = (bf16[2,64,768]{2,1,0:T(8,128)(2,1)S(1)}, bf16[2,64,768]{2,1,0:T(8,128)(2,1)S(1)}, u32[]{:S(2)}, u32[]{:S(2)}) collective-permute-start(bf16[2,64,768]{2,1,0:T(8,128)(2,1)S(1)} %dynamic-slice_bitcast_fusion), channel_id=1, source_target_pairs={{0,2},{1,3},{2,0},{3,1},{4,6},{5,7},{6,4},{7,5},{8,10},{9,11},{10,... | collective-permute-start | bytes 589832 | tf_op jit(solution)/shard_map/ppermute | solution.py:531
  250.9 14.2 %collective-permute-start.12 = (bf16[384,768]{1,0:T(8,128)(2,1)S(1)}, bf16[384,768]{1,0:T(8,128)(2,1)S(1)}, u32[]{:S(2)}, u32[]{:S(2)}) collective-permute-start(bf16[384,768]{1,0:T(8,128)(2,1)S(1)} %fusion.27), channel_id=1, source_target_pairs={{0,16},{4,12},{8,24},{12,4},{16,0},{20,28},{24,8},{28,20},{1,17},{... | collective-permute-start | bytes 1769480 | tf_op jit(solution)/shard_map/ppermute | solution.py:531
  268.1 31.6 %collective-permute-start.17 = (bf16[96,3840]{1,0:T(8,128)(2,1)}, bf16[96,3840]{1,0:T(8,128)(2,1)S(1)}, u32[]{:S(2)}, u32[]{:S(2)}) collective-permute-start(bf16[96,3840]{1,0:T(8,128)(2,1)} %fusion.26), channel_id=1, source_target_pairs={{0,16},{4,12},{8,24},{12,4},{16,0},{20,28},{24,8},{28,20},{1,17},{... | collective-permute-start | bytes 2211848 | tf_op jit(solution)/shard_map/ppermute | solution.py:531
  271.4 28.2 %collective-permute-start.16 = (bf16[192,768]{1,0:T(8,128)(2,1)}, bf16[192,768]{1,0:T(8,128)(2,1)}, u32[]{:S(2)}, u32[]{:S(2)}) collective-permute-start(bf16[192,768]{1,0:T(8,128)(2,1)} %broadcast_select_fusion.9), channel_id=1, source_target_pairs={{0,1},{1,0},{2,3},{3,2},{4,5},{5,4},{6,7},{7,6},{8,9},{9,8},{10,11... | collective-permute-start | bytes 884744 | tf_op jit(solution)/shard_map/ppermute | solution.py:531
  293.7 36.4 %collective-permute-start.18 = (bf16[2,96,3072]{2,1,0:T(8,128)(2,1)}, bf16[2,96,3072]{2,1,0:T(8,128)(2,1)}, u32[]{:S(2)}, u32[]{:S(2)}) collective-permute-start(bf16[2,96,3072]{2,1,0:T(8,128)(2,1)} %add_convert_fusion.3), channel_id=1, source_target_pairs={{0,8},{4,20},{8,0},{12,28},{16,24},{20,4},{24,16},{28,12},{1,9},{5... | collective-permute-start | bytes 3538952 | tf_op jit(solution)/shard_map/ppermute | solution.py:531
  296.8 27.9 %collective-permute-start.20 = (bf16[256,768]{1,0:T(8,128)(2,1)}, bf16[256,768]{1,0:T(8,128)(2,1)}, u32[]{:S(2)}, u32[]{:S(2)}) collective-permute-start(bf16[256,768]{1,0:T(8,128)(2,1)} %get-tuple-element.347), channel_id=1, source_target_pairs={{3,2},{2,1},{7,6},{6,5},{11,10},{10,9},{15,14},{14,13},{19,18},{18... | collective-permute-start | bytes 1179656 | tf_op jit(solution)/shard_map/ppermute | solution.py:531
  298.2 28.2 %collective-permute-start.21 = (bf16[256,768]{1,0:T(8,128)(2,1)}, bf16[256,768]{1,0:T(8,128)(2,1)}, u32[]{:S(2)}, u32[]{:S(2)}) collective-permute-start(bf16[256,768]{1,0:T(8,128)(2,1)} %get-tuple-element.346), channel_id=1, source_target_pairs={{0,1},{1,2},{2,3},{3,0},{4,5},{5,6},{6,7},{7,4},{8,9},{9,10},{10,1... | collective-permute-start | bytes 1179656 | tf_op jit(solution)/shard_map/ppermute | solution.py:531
  302.9 27.2 %collective-permute-start.19 = (bf16[192,768]{1,0:T(8,128)(2,1)S(1)}, bf16[192,768]{1,0:T(8,128)(2,1)}, u32[]{:S(2)}, u32[]{:S(2)}) collective-permute-start(bf16[192,768]{1,0:T(8,128)(2,1)S(1)} %add_convert_fusion.19), channel_id=1, source_target_pairs={{0,2},{1,3},{2,0},{3,1},{4,6},{5,7},{6,4},{7,5},{8,10},{9,11},{10,... | collective-permute-start | bytes 884744 | tf_op jit(solution)/shard_map/ppermute | solution.py:531
  324.5 22.7 %collective-permute-start.22 = (bf16[4,96,2432]{2,1,0:T(8,128)(2,1)}, bf16[4,96,2432]{2,1,0:T(8,128)(2,1)S(1)}, u32[]{:S(2)}, u32[]{:S(2)}) collective-permute-start(bf16[4,96,2432]{2,1,0:T(8,128)(2,1)} %get-tuple-element.247), channel_id=1, source_target_pairs={{0,4},{4,0},{8,12},{12,8},{16,20},{20,16},{24,28},{28,24},{1,5},{5... | collective-permute-start | bytes 5603336 | tf_op jit(solution)/shard_map/ppermute | solution.py:531
  324.7 21.6 %collective-permute-start.23 = (bf16[48,3840]{1,0:T(8,128)(2,1)S(1)}, bf16[48,3840]{1,0:T(8,128)(2,1)S(1)}, u32[]{:S(2)}, u32[]{:S(2)}) collective-permute-start(bf16[48,3840]{1,0:T(8,128)(2,1)S(1)} %broadcast_select_fusion.3), channel_id=1, source_target_pairs={{0,1},{1,0},{2,3},{3,2},{4,5},{5,4},{6,7},{7,6},{8,9},{9,8},{10,11... | collective-permute-start | bytes 1105928 | tf_op jit(solution)/shard_map/ppermute | solution.py:531
  326.4 52.2 %collective-permute-start.28 = (bf16[256,768]{1,0:T(8,128)(2,1)S(1)}, bf16[256,768]{1,0:T(8,128)(2,1)S(1)}, u32[]{:S(2)}, u32[]{:S(2)}) collective-permute-start(bf16[256,768]{1,0:T(8,128)(2,1)S(1)} %get-tuple-element.344), channel_id=1, source_target_pairs={{0,1},{1,2},{2,3},{3,0},{4,5},{5,6},{6,7},{7,4},{8,9},{9,10},{10,1... | collective-permute-start | bytes 1179656 | tf_op jit(solution)/shard_map/ppermute | solution.py:531
  331.2 47.4 %collective-permute-start.27 = (bf16[512,768]{1,0:T(8,128)(2,1)S(1)}, bf16[512,768]{1,0:T(8,128)(2,1)S(1)}, u32[]{:S(2)}, u32[]{:S(2)}) collective-permute-start(bf16[512,768]{1,0:T(8,128)(2,1)S(1)} %pad_maximum_fusion.3), channel_id=1, source_target_pairs={{1,0},{2,1},{3,2},{5,4},{6,5},{7,6},{9,8},{10,9},{11,10},{13,12},{... | collective-permute-start | bytes 2359304 | tf_op jit(solution)/shard_map/ppermute | solution.py:531
  333.8 43.5 %collective-permute-start.25 = (bf16[192,768]{1,0:T(8,128)(2,1)S(1)}, bf16[192,768]{1,0:T(8,128)(2,1)S(1)}, u32[]{:S(2)}, u32[]{:S(2)}) collective-permute-start(bf16[192,768]{1,0:T(8,128)(2,1)S(1)} %add_convert_fusion.18), channel_id=1, source_target_pairs={{0,1},{1,0},{2,3},{3,2},{4,5},{5,4},{6,7},{7,6},{8,9},{9,8},{10,11... | collective-permute-start | bytes 884744 | tf_op jit(solution)/shard_map/ppermute | solution.py:531
  347.3 32.6 %collective-permute-start.29 = (bf16[48,3840]{1,0:T(8,128)(2,1)S(1)}, bf16[48,3840]{1,0:T(8,128)(2,1)S(1)}, u32[]{:S(2)}, u32[]{:S(2)}) collective-permute-start(bf16[48,3840]{1,0:T(8,128)(2,1)S(1)} %add_convert_fusion.15), channel_id=1, source_target_pairs={{0,2},{1,3},{2,0},{3,1},{4,6},{5,7},{6,4},{7,5},{8,10},{9,11},{10,... | collective-permute-start | bytes 1105928 | tf_op jit(solution)/shard_map/ppermute | solution.py:531
  356.1 22.3 %collective-permute-start.26 = (bf16[2,96,2432]{2,1,0:T(8,128)(2,1)S(1)}, bf16[2,96,2432]{2,1,0:T(8,128)(2,1)S(1)}, u32[]{:S(2)}, u32[]{:S(2)}) collective-permute-start(bf16[2,96,2432]{2,1,0:T(8,128)(2,1)S(1)} %add_convert_fusion.5), channel_id=1, source_target_pairs={{0,8},{4,20},{8,0},{12,28},{16,24},{20,4},{24,16},{28,12},{1,9},{5... | collective-permute-start | bytes 2801672 | tf_op jit(solution)/shard_map/ppermute | solution.py:531
  381.0 33.0 %collective-permute-start.33 = (bf16[48,3840]{1,0:T(8,128)(2,1)S(1)}, bf16[48,3840]{1,0:T(8,128)(2,1)S(1)}, u32[]{:S(2)}, u32[]{:S(2)}) collective-permute-start(bf16[48,3840]{1,0:T(8,128)(2,1)S(1)} %add_convert_fusion.14), channel_id=1, source_target_pairs={{0,1},{1,0},{2,3},{3,2},{4,5},{5,4},{6,7},{7,6},{8,9},{9,8},{10,11... | collective-permute-start | bytes 1105928 | tf_op jit(solution)/shard_map/ppermute | solution.py:531
  383.1 42.8 %collective-permute-start.36 = (bf16[256,768]{1,0:T(8,128)(2,1)S(1)}, bf16[256,768]{1,0:T(8,128)(2,1)S(1)}, u32[]{:S(2)}, u32[]{:S(2)}) collective-permute-start(bf16[256,768]{1,0:T(8,128)(2,1)S(1)} %get-tuple-element.292), channel_id=1, source_target_pairs={{1,0},{2,1},{3,2},{5,4},{6,5},{7,6},{9,8},{10,9},{11,10},{13,12},{... | collective-permute-start | bytes 1179656 | tf_op jit(solution)/shard_map/ppermute | solution.py:531
  388.9 25.0 %collective-permute-start.32 = (bf16[48,2432]{1,0:T(8,128)(2,1)S(1)}, bf16[48,2432]{1,0:T(8,128)(2,1)S(1)}, u32[]{:S(2)}, u32[]{:S(2)}) collective-permute-start(bf16[48,2432]{1,0:T(8,128)(2,1)S(1)} %broadcast_select_fusion.12), channel_id=1, source_target_pairs={{0,1},{1,0},{2,3},{3,2},{4,5},{5,4},{6,7},{7,6},{8,9},{9,8},{10,11... | collective-permute-start | bytes 700424 | tf_op jit(solution)/shard_map/ppermute | solution.py:531
  391.1 24.9 %collective-permute-start.34 = (bf16[48,3072]{1,0:T(8,128)(2,1)S(1)}, bf16[48,3072]{1,0:T(8,128)(2,1)S(1)}, u32[]{:S(2)}, u32[]{:S(2)}) collective-permute-start(bf16[48,3072]{1,0:T(8,128)(2,1)S(1)} %add_convert_fusion.17), channel_id=1, source_target_pairs={{0,2},{1,3},{2,0},{3,1},{4,6},{5,7},{6,4},{7,5},{8,10},{9,11},{10,... | collective-permute-start | bytes 884744 | tf_op jit(solution)/shard_map/ppermute | solution.py:531
  (69 other events, 448.9 us)
Sparse Core Ops, SparseCore 0:
  12.5 61.4 all-gather.3
  75.8 39.0 all-gather.5
  116.8 38.7 all-gather.7
